TPU v7x, 512 devices: a whole 4x8x8 slice. The times are simulated.
512 devices in a mesh: grp: 16 (over y, core), path: 32 (over z, x).
Axes of the slice: x: 4, y: 8, z: 8, core: 2. Of those that a mesh axis runs over, the one named last changes fastest.
Arguments:
- link_state: bfloat16 [16, 16384, 256], P('grp', 'path'), may hold values from -6 to 6
- path_state: bfloat16 [16, 4096, 256], P('grp', 'path'), may hold values from -6 to 6
- path_links: int32 [4096, 8], P('path'), may hold values from -1 to 16383, as said below
- w_path_in: bfloat16 [256, 768], replicated, may hold values from -0.375 to 0.375
- w_path_hid: bfloat16 [256, 768], replicated, may hold values from -0.375 to 0.375
- w_link_in: bfloat16 [256, 768], replicated, may hold values from -0.375 to 0.375
- w_link_hid: bfloat16 [256, 768], replicated, may hold values from -0.375 to 0.375
- cotangent: bfloat16 [16, 4096, 128], P('grp', 'path'), may hold values from -0.0234375 to 0.0234375
Outputs:
- link_next: bfloat16 [16, 16384, 256], P('grp', 'path')
- path_final: bfloat16 [16, 4096, 256], P('grp', 'path')
- read_grad: float32 [128, 256], P('path')
Inputs may be any that keep to these rules, and one draw needn't show every extreme that they name: `path_links`: entry -1 marks no hop; each path's live entries come first and number two or more. In the rows of one device, at most 32 live entries name links of the block of 512 link ids held by any one index of path, and some block takes exactly 32.
All inputs are finite; a program needn't handle non-finite values.
Results may differ from a plain program's by a relative error of at most 0.0035.
Values may be sent and summed in bfloat16 or wider, within the bound.
A program may use at most 64 MiB of HBM per device.

v0:
```python
import jax
import jax.numpy as jnp
from jax import lax
from jax.sharding import PartitionSpec as P


def gated_update(projected, carried, w_hidden):
    width = carried.shape[1]
    recur = jnp.dot(carried.astype(jnp.bfloat16), w_hidden, preferred_element_type=jnp.float32)
    reset = jax.nn.sigmoid(projected[:, :width] + recur[:, :width])
    update = jax.nn.sigmoid(projected[:, width : 2 * width] + recur[:, width : 2 * width])
    candidate = jnp.tanh(projected[:, 2 * width :] + reset * recur[:, 2 * width :])
    return (1.0 - update) * candidate + update * carried


def shards(
    link_state, path_state, path_links, w_path_in, w_path_hid, w_link_in, w_link_hid, cotangent
):
    own_links = link_state[0]
    link_dev, width = own_links.shape
    peer_count = lax.axis_size("path")
    path_count, hop_count = path_links.shape
    flat_ids = path_links.reshape(-1)
    is_live = flat_ids >= 0
    owner_id = jnp.where(is_live, flat_ids // link_dev, peer_count)
    local_id = jnp.where(is_live, flat_ids % link_dev, -1)
    capacity = flat_ids.shape[0] // peer_count
    marks = (owner_id[:, None] == jnp.arange(peer_count)[None, :]).astype(jnp.int32)
    slot_id = jnp.sum((jnp.cumsum(marks, axis=0) - marks) * marks, axis=1)
    requests = (
        jnp.full((peer_count, capacity), -1, jnp.int32)
        .at[owner_id, slot_id]
        .set(local_id, mode="drop")
    )
    nothing = jnp.zeros((), jnp.bfloat16)
    every_link = lax.all_gather(own_links, "path", axis=0, tiled=True)
    fetched = jnp.where(is_live[:, None], every_link[jnp.where(is_live, flat_ids, 0)], nothing)
    received = lax.all_to_all(requests, "path", split_axis=0, concat_axis=0, tiled=True)
    projected = jnp.dot(fetched, w_path_in, preferred_element_type=jnp.float32)
    projected = projected.reshape(path_count, hop_count, 3 * width)
    live_grid = is_live.reshape(path_count, hop_count)
    carried = path_state[0].astype(jnp.float32)
    messages = []
    for hop_index in range(hop_count):
        renewed = gated_update(projected[:, hop_index], carried, w_path_hid)
        carried = jnp.where(live_grid[:, hop_index, None], renewed, carried)
        messages.append(carried.astype(jnp.bfloat16))
    path_final = carried.astype(jnp.bfloat16)
    flat_messages = jnp.stack(messages, axis=1).reshape(-1, width)
    outgoing = (
        jnp.zeros((peer_count, capacity, width), jnp.bfloat16)
        .at[owner_id, slot_id]
        .set(flat_messages, mode="drop")
    )
    incoming = lax.all_to_all(outgoing, "path", split_axis=0, concat_axis=0, tiled=True)
    selector = (received.reshape(-1)[None, :] == jnp.arange(link_dev)[:, None]).astype(jnp.bfloat16)
    link_sum = jnp.dot(selector, incoming.reshape(-1, width), preferred_element_type=jnp.float32)
    link_proj = jnp.dot(
        link_sum.astype(jnp.bfloat16), w_link_in, preferred_element_type=jnp.float32
    )
    link_next = gated_update(link_proj, own_links.astype(jnp.float32), w_link_hid).astype(
        jnp.bfloat16
    )
    grad_term = lax.dot_general(
        cotangent[0], path_final, (((0,), (0,)), ((), ())), preferred_element_type=jnp.float32
    )
    grad_whole = lax.psum(grad_term, ("grp", "path"))
    share = grad_whole.shape[0] // peer_count
    read_grad = lax.dynamic_slice_in_dim(grad_whole, lax.axis_index("path") * share, share, 0)
    return (link_next[None], path_final[None], read_grad)


def solution(mesh):
    return jax.shard_map(
        shards,
        mesh=mesh,
        in_specs=(
            P("grp", "path", None),
            P("grp", "path", None),
            P("path", None),
            P(),
            P(),
            P(),
            P(),
            P("grp", "path", None),
        ),
        out_specs=(P("grp", "path", None), P("grp", "path", None), P("path", None)),
        check_vma=False,
    )
```

profile of v0, /device:TPU:6, one launch (start us, length us, event | category | flops | bytes accessed | tf_op | source)
XLA Modules:
  0.0 424.8 jit_solution(9627529892946809395)
XLA Ops:
  7.2 0.7 all-gather.3.cloned.1.call-update
  7.9 0.8 copy.20
  9.0 9.0 %reduce-window.6 = s32[32,8,128]{2,1,0:T(8,128)S(1)} reduce-window(s32[32,8,128]{2,1,0:T(8,128)S(1)} %fusion.135, s32[]{:T(128)} %constant.44.clone.1), window={size=1x1x128 pad=0_0x0_0x127_0}, to_apply=%region_0.1 | reduce-window | flops 4161536 | bytes 262148 | tf_op jit(solution)/shard_map/reduce-window
  18.6 0.7 multiply_reduce_fusion
  19.4 4.3 %scatter_custom_fusion = s32[1024]{0:T(1024)S(1)} fusion(s32[1024]{0:T(1024)S(1)} %broadcast_select_fusion, s32[1024]{0:T(1024)S(1)} %get-tuple-element.33, s32[]{:T(128)} %constant.26.clone.1), kind=kCustom, calls=%fused_computation.239 | custom fusion | bytes 4100
  23.7 0.7 all_to_all.9
  24.4 13.4 %all-to-all-start = ((s32[32,1,32]{2,1,0:T(1,128)}), s32[32,1,32]{2,1,0:T(1,128)S(1)}, u32[]{:S(2)}, u32[]{:S(2)}) async-start(s32[32,1,32]{2,1,0:T(1,128)} %all_to_all.9), calls=%async_computation | async-start | bytes 32768 | tf_op jit(solution)/shard_map/all_to_all | solution.py:38
  37.8 0.7 broadcast_compare_fusion
  38.6 1.1 fusion.136
  39.6 78.9 %all-gather.3.cloned.1.call-done = bf16[1,16384,256]{2,1,0:T(8,128)(2,1)} async-done(((bf16[1,512,256]{2,1,0:T(8,128)(2,1)}), bf16[1,16384,256]{2,1,0:T(8,128)(2,1)}) %all-gather.3.cloned.1.call-update) | async-done | bytes 8388624 | tf_op jit(solution)/shard_map/all_gather | solution.py:36
  118.5 7.9 %gather_fusion = bf16[1024,256]{1,0:T(8,128)(2,1)S(1)} fusion(bf16[16384,256]{1,0:T(8,128)(2,1)} %bitcast.116, s32[1024]{0:T(1024)S(1)} %broadcast_clamp_fusion), kind=kCustom, calls=%fused_computation | custom fusion | bytes 1052672 | tf_op jit(solution)/shard_map/gather | solution.py:37
  126.5 0.6 convolution_bitcast_fusion
  127.1 2.1 fusion.170
  132.1 6.4 %scatter_custom_fusion.1 = bf16[1024,256]{1,0:T(8,128)(2,1)} fusion(s32[1024]{0:T(1024)S(1)} %broadcast_select_fusion, bf16[128,8,256]{2,0,1:T(8,128)(2,1)S(1)} %get-tuple-element.9, bf16[]{:T(256)} %constant.50.clone.1), kind=kCustom, calls=%fused_computation.26 | custom fusion | bytes 1048578
  138.5 7.7 %all-to-all-start.1 = ((bf16[32,32,256]{2,1,0:T(8,128)(2,1)}), bf16[32,32,256]{2,1,0:T(8,128)(2,1)}, u32[]{:S(2)}, u32[]{:S(2)}) async-start(bf16[32,32,256]{2,1,0:T(8,128)(2,1)} %bitcast.32), calls=%async_computation.1 | async-start | bytes 1048576 | tf_op jit(solution)/shard_map/all_to_all | solution.py:55
  146.2 0.9 convolution_bitcast_fusion.1
  147.1 0.4 fusion.23
  147.5 0.5 broadcast.260
  148.0 0.7 reduce.9
  148.8 263.3 %all-reduce.2.cloned.1.call-done = f32[128,256]{0,1:T(8,128)} async-done(((f32[128,256]{0,1:T(8,128)}), f32[128,256]{0,1:T(8,128)}) %all-reduce.2.cloned.1.call-update) | async-done | bytes 131088 | tf_op jit(solution)/shard_map/psum | solution.py:67
  412.1 1.0 constant_dynamic-slice_fusion
  413.1 0.7 copy.34
  413.8 2.2 fusion.2
  415.9 2.0 fusion.27
  (62 shorter events, 3.7 us)
Async XLA Ops:
  7.2 119.3 %copy-start = (bf16[256,768]{1,0:T(8,128)(2,1)S(1)}, bf16[256,768]{1,0:T(8,128)(2,1)}, u32[]{:S(2)}) copy-start(bf16[256,768]{1,0:T(8,128)(2,1)} %param.11) | copy-start | bytes 1179652
  7.2 31.4 %copy-start.1 = (bf16[256,768]{1,0:T(8,128)(2,1)S(1)}, bf16[256,768]{1,0:T(8,128)(2,1)}, u32[]{:S(2)}) copy-start(bf16[256,768]{1,0:T(8,128)(2,1)} %param.12) | copy-start | bytes 1179652
  7.2 111.4 %all-gather.3.cloned.1.call-start = ((), (), s32[]{:S(2)}) async-start(), calls=%async_computation.3 | async-start | bytes 8650752 | tf_op jit(solution)/shard_map/all_gather | solution.py:36
  24.4 114.1 %all-to-all-start = ((s32[32,1,32]{2,1,0:T(1,128)}), s32[32,1,32]{2,1,0:T(1,128)S(1)}, u32[]{:S(2)}, u32[]{:S(2)}) async-start(s32[32,1,32]{2,1,0:T(1,128)} %all_to_all.9), calls=%async_computation | async-start | bytes 32768 | tf_op jit(solution)/shard_map/all_to_all | solution.py:38
  127.1 2.2 copy-start.5
  131.9 14.3 %copy-start.6 = (bf16[1,128,128]{2,1,0:T(8,128)(2,1)S(1)}, bf16[1,128,128]{2,1,0:T(8,128)(2,1)}, u32[]{:S(2)}) copy-start(bf16[1,128,128]{2,1,0:T(8,128)(2,1)} %param.15) | copy-start | bytes 98308
  131.9 15.2 %copy-start.2 = (bf16[1,512,256]{2,1,0:T(8,128)(2,1)S(1)}, bf16[1,512,256]{2,1,0:T(8,128)(2,1)}, u32[]{:S(2)}) copy-start(bf16[1,512,256]{2,1,0:T(8,128)(2,1)} %param.8) | copy-start | bytes 786436
  131.9 15.2 %copy-start.3 = (bf16[256,768]{1,0:T(8,128)(2,1)S(1)}, bf16[256,768]{1,0:T(8,128)(2,1)}, u32[]{:S(2)}) copy-start(bf16[256,768]{1,0:T(8,128)(2,1)} %param.14) | copy-start | bytes 1179652
  132.1 15.0 %copy-start.4 = (bf16[128,256]{1,0:T(8,128)(2,1)}, bf16[128,256]{1,0:T(8,128)(2,1)S(1)}, u32[]{:S(2)}) copy-start(bf16[128,256]{1,0:T(8,128)(2,1)S(1)} %get-tuple-element.10) | copy-start | bytes 196612
  138.5 275.2 %all-to-all-start.1 = ((bf16[32,32,256]{2,1,0:T(8,128)(2,1)}), bf16[32,32,256]{2,1,0:T(8,128)(2,1)}, u32[]{:S(2)}, u32[]{:S(2)}) async-start(bf16[32,32,256]{2,1,0:T(8,128)(2,1)} %bitcast.32), calls=%async_computation.1 | async-start | bytes 1048576 | tf_op jit(solution)/shard_map/all_to_all | solution.py:55
  146.2 265.9 %all-reduce.2.cloned.1.call-start = ((), (), s32[]{:S(2)}) async-start(), calls=%async_computation.2 | async-start | bytes 262144 | tf_op jit(solution)/shard_map/psum | solution.py:67
Sparse Core Ops, SparseCore 0:
  11.2 107.3 all-gather.2
  152.6 259.4 all-reduce.1
where the time goes:
time: 429 us; the launch traced here: 425 us
  waiting for transfers between devices  343 us (80%)
  local copies, waits for them, and re-layouts  25.4 us (6%)
  starting transfers between devices  21.1 us (5%)
  between operations  14.5 us (3%)
  other arithmetic  14.4 us (3%)
  matrix products  6.54 us (2%)
    psum x1, waiting for transfers between devices, shards(): grad_whole = lax.psum(grad_term, ('grp', 'path'))  263 us
    all_gather x1, waiting for transfers between devices, shards(): every_link = lax.all_gather(own_links, 'path', axis=0, tiled=True)  78.9 us
    all_to_all x1, starting transfers between devices, shards(): lax.all_to_all(requests, 'path', split_axis=0, concat_axis=0, tiled=True)  13.4 us
    unnamed x26, local copies, waits for them, and re-layouts  12.4 us
    another operation x3, other arithmetic  9.14 us
  transfers between devices with their start and end apart: 4, of which 2 were waited for; matrix products, arithmetic and copies ran while one was open for 10% of the time, Pallas kernels for 0%

commit v1 on v0

v1 whole, which is shorter than its diff:
```python
import jax
import jax.numpy as jnp
from jax import lax
from jax.sharding import PartitionSpec as P


def gated_update(projected, carried, w_hidden):
    width = carried.shape[1]
    recur = jnp.dot(carried.astype(jnp.bfloat16), w_hidden, preferred_element_type=jnp.float32)
    reset = jax.nn.sigmoid(projected[:, :width] + recur[:, :width])
    update = jax.nn.sigmoid(projected[:, width : 2 * width] + recur[:, width : 2 * width])
    candidate = jnp.tanh(projected[:, 2 * width :] + reset * recur[:, 2 * width :])
    return (1.0 - update) * candidate + update * carried


def shards(
    link_state, path_state, path_links, w_path_in, w_path_hid, w_link_in, w_link_hid, cotangent
):
    bf16, f32 = jnp.bfloat16, jnp.float32
    own_links = link_state[0]
    link_dev, width = own_links.shape
    peer_count = lax.axis_size("path")
    path_count, hop_count = path_links.shape
    entries = path_count * hop_count
    capacity = entries // peer_count
    slots = peer_count * capacity
    flat_ids = path_links.reshape(-1)
    is_live = flat_ids >= 0
    owner_id = jnp.where(is_live, flat_ids // link_dev, peer_count)
    local_id = jnp.where(is_live, flat_ids % link_dev, 0)
    marks = (owner_id[:, None] == jnp.arange(peer_count)[None, :]).astype(bf16)
    order = jnp.arange(entries)
    earlier = (order[None, :] < order[:, None]).astype(bf16)
    before = jnp.dot(earlier, marks, preferred_element_type=f32)
    slot_id = jnp.sum(before * marks.astype(f32), axis=1).astype(jnp.int32)
    dest = jnp.where(is_live, owner_id * capacity + slot_id, -1)
    slot_ids = jnp.arange(slots)
    route = dest[None, :] == slot_ids[:, None]
    requests = jnp.sum(jnp.where(route, local_id[None, :] + 1, 0), axis=1) - 1
    received = lax.all_to_all(
        requests.reshape(peer_count, capacity), "path", split_axis=0, concat_axis=0, tiled=True
    ).reshape(-1)
    want = (received[:, None] == jnp.arange(link_dev)[None, :]).astype(bf16)
    served = jnp.dot(want, own_links, preferred_element_type=f32).astype(bf16)
    got = lax.all_to_all(
        served.reshape(peer_count, capacity, width), "path", split_axis=0, concat_axis=0, tiled=True
    ).reshape(slots, width)
    route_t = (dest[:, None] == slot_ids[None, :]).astype(bf16)
    fetched = jnp.dot(route_t, got, preferred_element_type=f32).astype(bf16)
    projected = jnp.dot(fetched, w_path_in, preferred_element_type=f32)
    projected = projected.reshape(path_count, hop_count, 3 * width)
    live_grid = is_live.reshape(path_count, hop_count)
    carried = path_state[0].astype(f32)
    messages = []
    for hop_index in range(hop_count):
        renewed = gated_update(projected[:, hop_index], carried, w_path_hid)
        carried = jnp.where(live_grid[:, hop_index, None], renewed, carried)
        messages.append(carried.astype(bf16))
    path_final = carried.astype(bf16)
    flat_messages = jnp.stack(messages, axis=1).reshape(-1, width)
    outgoing = jnp.dot(route.astype(bf16), flat_messages, preferred_element_type=f32).astype(bf16)
    incoming = lax.all_to_all(
        outgoing.reshape(peer_count, capacity, width), "path", split_axis=0, concat_axis=0, tiled=True
    ).reshape(slots, width)
    link_sum = lax.dot_general(
        want, incoming, (((0,), (0,)), ((), ())), preferred_element_type=f32
    )
    link_proj = jnp.dot(link_sum.astype(bf16), w_link_in, preferred_element_type=f32)
    link_next = gated_update(link_proj, own_links.astype(f32), w_link_hid).astype(bf16)
    grad_term = lax.dot_general(
        cotangent[0], path_final, (((0,), (0,)), ((), ())), preferred_element_type=f32
    )
    part = lax.psum_scatter(grad_term, "path", scatter_dimension=0, tiled=True)
    read_grad = lax.psum(part, "grp")
    return (link_next[None], path_final[None], read_grad)


def solution(mesh):
    return jax.shard_map(
        shards,
        mesh=mesh,
        in_specs=(
            P("grp", "path", None),
            P("grp", "path", None),
            P("path", None),
            P(),
            P(),
            P(),
            P(),
            P("grp", "path", None),
        ),
        out_specs=(P("grp", "path", None), P("grp", "path", None), P("path", None)),
        check_vma=False,
    )
```

time: 429 us -> 301 us (0.70)
  waiting for transfers between devices: 343 us -> 170 us
  blocking collectives: 0 us -> 67.6 us
  other arithmetic: 14.4 us -> 4.16 us
  starting transfers between devices: 21.1 us -> 11.2 us
  matrix products: 6.54 us -> 13.4 us
  local copies, waits for them, and re-layouts: 25.4 us -> 18.9 us
    psum x1 -> x0, waiting for transfers between devices: 263 us -> none  [shards(): grad_whole = lax.psum(grad_term, ('grp', 'path'))]
    unnamed x2, waiting for transfers between devices: 0.7 us -> 154 us
    all_gather x1 -> x0, waiting for transfers between devices: 78.9 us -> none  [shards(): every_link = lax.all_gather(own_links, 'path', axis=0, tiled=True)]
    psum x0 -> x1, blocking collectives: none -> 46.5 us  [shards(): read_grad = lax.psum(part, 'grp')]
    all_to_all x0 -> x1, blocking collectives: none -> 21.2 us  [shards(): lax.all_to_all(requests.reshape(peer_count, capacity), 'path', split_axis...]
    all_to_all x2, waiting for transfers between devices: 0.01 us -> 15.5 us  [the longest x1 15.5 us: shards(): lax.all_to_all(served.reshape(peer_count, capacity, width), 'path', split...]
    slice x1, local copies, waits for them, and re-layouts: 2.14 us -> 13.3 us  [shards(): renewed = gated_update(projected[:, hop_index], carried, w_path_hid)]
    all_to_all x2, starting transfers between devices: 21.1 us -> 11.1 us  [the longest x1 5.56 us: shards(): lax.all_to_all(served.reshape(peer_count, capacity, width), 'path', split...]
  transfers between devices with their start and end apart: 4 -> 3, of which waited for: 2 -> 2; matrix products, arithmetic and copies ran while one was open for 10% -> 1% of each run, Pallas kernels for 0% -> 0%
where the time goes in v1:
time: 301 us; the launch traced here: 300 us
  waiting for transfers between devices  170 us (56%)
  blocking collectives  67.6 us (22%)
  local copies, waits for them, and re-layouts  18.9 us (6%)
  between operations  15 us (5%)
  matrix products  13.4 us (4%)
  starting transfers between devices  11.2 us (4%)
  other arithmetic  4.16 us (1%)
    unnamed x2, waiting for transfers between devices  154 us
    psum x1, blocking collectives, shards(): read_grad = lax.psum(part, 'grp')  46.5 us
    all_to_all x1, blocking collectives, shards(): lax.all_to_all(requests.reshape(peer_count, capacity), 'path', split_axis...  21.2 us
    all_to_all x1, waiting for transfers between devices, shards(): lax.all_to_all(served.reshape(peer_count, capacity, width), 'path', split...  15.5 us
    slice x1, local copies, waits for them, and re-layouts, shards(): renewed = gated_update(projected[:, hop_index], carried, w_path_hid)  13.3 us
  transfers between devices with their start and end apart: 3, of which 2 were waited for; matrix products, arithmetic and copies ran while one was open for 1% of the time, Pallas kernels for 0%

profile of v1, /device:TPU:6, one launch (start us, length us, event | category | flops | bytes accessed | tf_op | source)
XLA Modules:
  0.0 300.2 jit_solution(5889730820409296890)
XLA Ops:
  7.2 0.9 copy.42
  8.2 0.5 fusion.13
  8.7 0.5 select_reduce_fusion
  9.3 21.2 %all_to_all.16 = s32[32,1,32]{2,1,0:T(1,128)S(1)} all-to-all(s32[32,1,32]{2,1,0:T(1,128)S(1)} %sub.41), channel_id=1, replica_groups=mesh['grp'=16,'path'=32] {'path'}, dimensions={0} | all-to-all | bytes 8192 | tf_op jit(solution)/shard_map/all_to_all | solution.py:40
  30.5 0.5 broadcast.189
  31.0 0.7 reduce.3
  31.8 2.3 fusion.7
  34.0 5.6 %all-to-all-start.1 = ((bf16[32,32,256]{2,1,0:T(8,128)(2,1)}), bf16[32,32,256]{2,1,0:T(8,128)(2,1)S(1)}, u32[]{:S(2)}, u32[]{:S(2)}) async-start(bf16[32,32,256]{2,1,0:T(8,128)(2,1)} %bitcast.2), calls=%async_computation.1 | async-start | bytes 1048576 | tf_op jit(solution)/shard_map/all_to_all | solution.py:45
  39.9 15.5 %all-to-all-done.1 = bf16[32,32,256]{2,1,0:T(8,128)(2,1)S(1)} async-done(((bf16[32,32,256]{2,1,0:T(8,128)(2,1)}), bf16[32,32,256]{2,1,0:T(8,128)(2,1)S(1)}, u32[]{:S(2)}, u32[]{:S(2)}) %all-to-all-start.1) | async-done | bytes 524320 | tf_op jit(solution)/shard_map/all_to_all | solution.py:45
  55.4 3.5 %convolution_bitcast_fusion = f32[128,8,768]{2,1,0:T(8,128)} fusion(bf16[256,768]{1,0:T(8,128)(2,1)S(1)} %copy-done, bf16[1024,256]{1,0:T(8,128)(2,1)S(1)} %bitcast.96, s32[1024]{0:T(1024)S(1)} %add_select_fusion.2), kind=kOutput, calls=%fused_computation.12 | convolution fusion | flops 940834816 | bytes 4067328 | tf_op jit(solution)/shard_map/dot_general | solution.py:50
  58.9 13.3 %fusion.171 = (f32[128,1,768]{2,1,0:T(1,128)S(1)}, f32[128,1,768]{2,1,0:T(1,128)S(1)}, f32[128,1,768]{2,1,0:T(1,128)S(1)}, f32[128,1,768]{2,1,0:T(1,128)S(1)}, f...) fusion(f32[128,8,768]{2,1,0:T(8,128)} %convolution_bitcast_fusion), kind=kLoop, calls=%fused_computation.235 | loop fusion | bytes 6291456 | tf_op jit(solution)/shard_map/slice | solution.py:56
  72.7 0.2 fusion.155
  75.0 1.8 fusion.9
  76.8 5.6 %all-to-all-start.2 = ((bf16[32,32,256]{2,1,0:T(8,128)(2,1)}), bf16[32,32,256]{2,1,0:T(8,128)(2,1)S(1)}, u32[]{:S(2)}, u32[]{:S(2)}) async-start(bf16[32,32,256]{2,1,0:T(8,128)(2,1)} %bitcast.30), calls=%async_computation.2 | async-start | bytes 1048576 | tf_op jit(solution)/shard_map/all_to_all | solution.py:62
  82.4 0.9 convolution_bitcast_fusion.1
  83.3 0.4 fusion.32
  83.7 1.3 dynamic-slice
  85.6 154.4 %all-reduce.3.cloned.1.call-done = f32[128,256]{0,1:T(8,128)} async-done(((f32[128,256]{0,1:T(8,128)}), f32[128,256]{0,1:T(8,128)}) %all-reduce.3.cloned.1.call-update) | async-done | bytes 131088
  240.0 1.0 constant_dynamic-slice_fusion
  241.0 46.5 %psum.7 = f32[4,256]{0,1:T(8,128)S(1)} all-reduce(f32[4,256]{0,1:T(8,128)S(1)} %constant_dynamic-slice_fusion), channel_id=1, replica_groups=mesh['grp'=16,'path'=32] {'grp'}, use_global_device_ids=true, to_apply=%region_3.4 | all-reduce | flops 1024 | bytes 8192 | tf_op jit(solution)/shard_map/psum | solution.py:74
  287.4 0.7 copy.52
  288.1 0.8 copy-done.2
  288.9 2.4 fusion.11
  291.3 2.0 fusion.35
  (47 shorter events, 3.0 us)
Async XLA Ops:
  7.2 48.2 %copy-start = (bf16[256,768]{1,0:T(8,128)(2,1)S(1)}, bf16[256,768]{1,0:T(8,128)(2,1)}, u32[]{:S(2)}) copy-start(bf16[256,768]{1,0:T(8,128)(2,1)} %param.11) | copy-start | bytes 1179652
  7.2 32.4 %copy-start.8 = (s32[128,8]{0,1:T(8,128)S(1)}, s32[128,8]{0,1:T(8,128)}, u32[]{:S(2)}) copy-start(s32[128,8]{0,1:T(8,128)} %param.10) | copy-start | bytes 12292
  7.2 32.5 %copy-start.1 = (bf16[256,768]{1,0:T(8,128)(2,1)S(1)}, bf16[256,768]{1,0:T(8,128)(2,1)}, u32[]{:S(2)}) copy-start(bf16[256,768]{1,0:T(8,128)(2,1)} %param.12) | copy-start | bytes 1179652
  7.2 32.5 %copy-start.6 = (bf16[1,128,256]{2,1,0:T(8,128)(2,1)S(1)}, bf16[1,128,256]{2,1,0:T(8,128)(2,1)}, u32[]{:S(2)}) copy-start(bf16[1,128,256]{2,1,0:T(8,128)(2,1)} %param.9) | copy-start | bytes 196612
  34.0 21.3 %all-to-all-start.1 = ((bf16[32,32,256]{2,1,0:T(8,128)(2,1)}), bf16[32,32,256]{2,1,0:T(8,128)(2,1)S(1)}, u32[]{:S(2)}, u32[]{:S(2)}) async-start(bf16[32,32,256]{2,1,0:T(8,128)(2,1)} %bitcast.2), calls=%async_computation.1 | async-start | bytes 1048576 | tf_op jit(solution)/shard_map/all_to_all | solution.py:45
  74.6 7.8 %copy-start.7 = (bf16[1,128,128]{2,1,0:T(8,128)(2,1)S(1)}, bf16[1,128,128]{2,1,0:T(8,128)(2,1)}, u32[]{:S(2)}) copy-start(bf16[1,128,128]{2,1,0:T(8,128)(2,1)} %param.15) | copy-start | bytes 98308
  74.8 8.5 %copy-start.3 = (bf16[1,512,256]{2,1,0:T(8,128)(2,1)S(1)}, bf16[1,512,256]{2,1,0:T(8,128)(2,1)}, u32[]{:S(2)}) copy-start(bf16[1,512,256]{2,1,0:T(8,128)(2,1)} %param.8) | copy-start | bytes 786436
  74.8 8.5 %copy-start.4 = (bf16[256,768]{1,0:T(8,128)(2,1)S(1)}, bf16[256,768]{1,0:T(8,128)(2,1)}, u32[]{:S(2)}) copy-start(bf16[256,768]{1,0:T(8,128)(2,1)} %param.14) | copy-start | bytes 1179652
  75.0 8.3 %copy-start.5 = (bf16[128,256]{1,0:T(8,128)(2,1)}, bf16[128,256]{1,0:T(8,128)(2,1)S(1)}, u32[]{:S(2)}) copy-start(bf16[128,256]{1,0:T(8,128)(2,1)S(1)} %get-tuple-element.16) | copy-start | bytes 196612
  76.8 211.4 %all-to-all-start.2 = ((bf16[32,32,256]{2,1,0:T(8,128)(2,1)}), bf16[32,32,256]{2,1,0:T(8,128)(2,1)S(1)}, u32[]{:S(2)}, u32[]{:S(2)}) async-start(bf16[32,32,256]{2,1,0:T(8,128)(2,1)} %bitcast.30), calls=%async_computation.2 | async-start | bytes 1048576 | tf_op jit(solution)/shard_map/all_to_all | solution.py:62
  82.3 157.6 %all-reduce.3.cloned.1.call-start = ((), (), s32[]{:S(2)}) async-start(), calls=%async_computation.3 | async-start | bytes 262144
  288.1 0.8 copy-start.2
Sparse Core Ops, SparseCore 0:
  87.2 152.7 all-reduce.2

commit v2 on v1

--- a/solution.py
+++ b/solution.py
@@ -1,7 +1,87 @@
 import jax
 import jax.numpy as jnp
 from jax import lax
+from jax.experimental import pallas as pl
+from jax.experimental.pallas import tpu as pltpu
 from jax.sharding import PartitionSpec as P
+
+MESH = pl.DeviceIdType.MESH
+
+
+def _readout_kernel(n_grp, n_path, term_ref, out_ref, recv1, recv2, mid, send1, got1, send2, got2):
+    g = lax.axis_index("grp")
+    p = lax.axis_index("path")
+    barrier = pltpu.get_barrier_semaphore()
+
+    def greet_path(k, c):
+        pl.semaphore_signal(barrier, inc=1, device_id=(g, lax.rem(p + k, n_path)), device_id_type=MESH)
+        return c
+
+    def greet_grp(k, c):
+        pl.semaphore_signal(barrier, inc=1, device_id=(lax.rem(g + k, n_grp), p), device_id_type=MESH)
+        return c
+
+    lax.fori_loop(1, n_path, greet_path, 0)
+    lax.fori_loop(1, n_grp, greet_grp, 0)
+    pl.semaphore_wait(barrier, (n_path - 1) + (n_grp - 1))
+
+    def path_copy(k, q):
+        return pltpu.make_async_remote_copy(
+            src_ref=term_ref.at[q], dst_ref=recv1.at[k - 1], send_sem=send1.at[k - 1],
+            recv_sem=got1.at[k - 1], device_id=(g, q), device_id_type=MESH)
+
+    def start1(k, c):
+        path_copy(k, lax.rem(p + k, n_path)).start()
+        return c
+
+    def finish1(k, c):
+        copy = path_copy(k, lax.rem(p + k, n_path))
+        copy.wait_send()
+        copy.wait_recv()
+        return c
+
+    lax.fori_loop(1, n_path, start1, 0)
+    lax.fori_loop(1, n_path, finish1, 0)
+    mid[...] = term_ref[p] + jnp.sum(recv1[...], axis=0)
+
+    def grp_copy(k, h):
+        return pltpu.make_async_remote_copy(
+            src_ref=mid, dst_ref=recv2.at[k - 1], send_sem=send2.at[k - 1],
+            recv_sem=got2.at[k - 1], device_id=(h, p), device_id_type=MESH)
+
+    def start2(k, c):
+        grp_copy(k, lax.rem(g + k, n_grp)).start()
+        return c
+
+    def finish2(k, c):
+        copy = grp_copy(k, lax.rem(g + k, n_grp))
+        copy.wait_send()
+        copy.wait_recv()
+        return c
+
+    lax.fori_loop(1, n_grp, start2, 0)
+    lax.fori_loop(1, n_grp, finish2, 0)
+    out_ref[...] = mid[...] + jnp.sum(recv2[...], axis=0)
+
+
+def readout_reduce(term, n_grp, n_path):
+    _, rows, width = term.shape
+    return pl.pallas_call(
+        lambda *refs: _readout_kernel(n_grp, n_path, *refs),
+        out_shape=jax.ShapeDtypeStruct((rows, width), jnp.float32),
+        in_specs=[pl.BlockSpec(memory_space=pltpu.VMEM)],
+        out_specs=pl.BlockSpec(memory_space=pltpu.VMEM),
+        scratch_shapes=[
+            pltpu.VMEM((n_path - 1, rows, width), jnp.float32),
+            pltpu.VMEM((n_grp - 1, rows, width), jnp.float32),
+            pltpu.VMEM((rows, width), jnp.float32),
+            pltpu.SemaphoreType.DMA((n_path - 1,)),
+            pltpu.SemaphoreType.DMA((n_path - 1,)),
+            pltpu.SemaphoreType.DMA((n_grp - 1,)),
+            pltpu.SemaphoreType.DMA((n_grp - 1,)),
+        ],
+        compiler_params=pltpu.CompilerParams(collective_id=0, has_side_effects=True),
+    )(term)
 
 
 def gated_update(projected, carried, w_hidden):
@@ -67,11 +147,9 @@
     )
     link_proj = jnp.dot(link_sum.astype(bf16), w_link_in, preferred_element_type=f32)
     link_next = gated_update(link_proj, own_links.astype(f32), w_link_hid).astype(bf16)
-    grad_term = lax.dot_general(
-        cotangent[0], path_final, (((0,), (0,)), ((), ())), preferred_element_type=f32
-    )
-    part = lax.psum_scatter(grad_term, "path", scatter_dimension=0, tiled=True)
-    read_grad = lax.psum(part, "grp")
+    cot = cotangent[0].reshape(path_count, peer_count, -1)
+    term = lax.dot_general(cot, path_final, (((0,), (0,)), ((), ())), preferred_element_type=f32)
+    read_grad = readout_reduce(term, lax.axis_size("grp"), peer_count)
     return (link_next[None], path_final[None], read_grad)
 
 

time: 301 us -> 113 us (0.38)
  the two profiles are of different devices: /device:TPU:6 before, /device:TPU:1 now
where the time goes in v2:
time: 113 us
  Pallas kernels  30.6 us (27%)
  blocking collectives  22.1 us (20%)
  local copies, waits for them, and re-layouts  17.4 us (15%)
  waiting for transfers between devices  14.4 us (13%)
  matrix products  12.7 us (11%)
  starting transfers between devices  10.2 us (9%)
  other arithmetic  4.15 us (4%)
    pallas_call x1, Pallas kernels, readout_reduce(): pl.pallas_call(lambda *refs: _readout_kernel(n_grp, n_path, *refs), out_s...  30.6 us
    all_to_all x1, blocking collectives, shards(): lax.all_to_all(requests.reshape(peer_count, capacity), 'path', split_axis...  22.1 us
    all_to_all x1, waiting for transfers between devices, shards(): lax.all_to_all(served.reshape(peer_count, capacity, width), 'path', split...  14.4 us
    slice x1, local copies, waits for them, and re-layouts, shards(): renewed = gated_update(projected[:, hop_index], carried, w_path_hid)  13.2 us
    all_to_all x1, starting transfers between devices, shards(): lax.all_to_all(outgoing.reshape(peer_count, capacity, width), 'path', spl...  6.29 us
    all_to_all x1, starting transfers between devices, shards(): lax.all_to_all(served.reshape(peer_count, capacity, width), 'path', split...  3.89 us
    dot_general x1, matrix products, shards(): projected = jnp.dot(fetched, w_path_in, preferred_element_type=f32)  3.47 us
    dot_general x1, matrix products, shards(): jnp.dot(link_sum.astype(bf16), w_link_in, preferred_element_type=f32)  2.42 us
  transfers between devices with their start and end apart: 2, of which 1 were waited for; matrix products, arithmetic and copies ran while one was open for 1% of the time, Pallas kernels for 27%

profile of v2, /device:TPU:1, one launch (start us, length us, event | category | flops | bytes accessed | tf_op | source)
XLA Modules:
  0.0 112.5 jit_solution(6599888800585794729)
XLA Ops:
  0.7 0.9 copy.34
  1.6 0.5 fusion.13
  2.2 0.5 select_reduce_fusion
  2.8 22.1 %all_to_all.16 = s32[32,1,32]{2,1,0:T(1,128)S(1)} all-to-all(s32[32,1,32]{2,1,0:T(1,128)S(1)} %sub.41), channel_id=1, replica_groups=mesh['grp'=16,'path'=32] {'path'}, dimensions={0} | all-to-all | bytes 8192 | tf_op jit(solution)/shard_map/all_to_all | solution.py:120
  24.9 0.5 broadcast.189
  25.4 0.7 reduce.3
  26.2 2.3 %fusion.7 = bf16[1024,256]{1,0:T(8,128)(2,1)} fusion(s32[1024]{0:T(1024)S(1)} %eq.29, bf16[1,512,256]{2,1,0:T(8,128)(2,1)} %param.8), kind=kOutput, calls=%fused_computation.13 | convolution fusion | flops 269221888 | bytes 790528 | tf_op jit(solution)/shard_map/dot_general | solution.py:124
  28.4 3.9 %all-to-all-start.1 = ((bf16[32,32,256]{2,1,0:T(8,128)(2,1)}), bf16[32,32,256]{2,1,0:T(8,128)(2,1)S(1)}, u32[]{:S(2)}, u32[]{:S(2)}) async-start(bf16[32,32,256]{2,1,0:T(8,128)(2,1)} %bitcast.2), calls=%async_computation.1 | async-start | bytes 1048576 | tf_op jit(solution)/shard_map/all_to_all | solution.py:125
  32.4 0.2 fusion.143
  32.6 14.4 %all-to-all-done.1 = bf16[32,32,256]{2,1,0:T(8,128)(2,1)S(1)} async-done(((bf16[32,32,256]{2,1,0:T(8,128)(2,1)}), bf16[32,32,256]{2,1,0:T(8,128)(2,1)S(1)}, u32[]{:S(2)}, u32[]{:S(2)}) %all-to-all-start.1) | async-done | bytes 524320 | tf_op jit(solution)/shard_map/all_to_all | solution.py:125
  47.0 3.5 %convolution_bitcast_fusion = f32[128,8,768]{2,1,0:T(8,128)} fusion(bf16[256,768]{1,0:T(8,128)(2,1)S(1)} %copy-done, bf16[1024,256]{1,0:T(8,128)(2,1)S(1)} %bitcast.94, s32[1024]{0:T(1024)S(1)} %add_select_fusion.2), kind=kOutput, calls=%fused_computation.12 | convolution fusion | flops 940834816 | bytes 4067328 | tf_op jit(solution)/shard_map/dot_general | solution.py:130
  50.5 13.2 %fusion.173 = (f32[128,1,768]{2,1,0:T(1,128)S(1)}, f32[128,1,768]{2,1,0:T(1,128)S(1)}, f32[128,1,768]{2,1,0:T(1,128)S(1)}, f32[128,1,768]{2,1,0:T(1,128)S(1)}, f...) fusion(f32[128,8,768]{2,1,0:T(8,128)} %convolution_bitcast_fusion), kind=kLoop, calls=%fused_computation.236 | loop fusion | bytes 6291456 | tf_op jit(solution)/shard_map/slice | solution.py:136
  63.9 0.2 fusion.159
  64.2 0.2 fusion.157
  65.0 0.2 fusion.153
  66.5 1.8 %fusion.9 = bf16[1024,256]{1,0:T(8,128)(2,1)} fusion(s32[1024]{0:T(1024)S(1)} %add_select_fusion.2, bf16[128,8,256]{2,0,1:T(8,128)(2,1)S(1)} %get-tuple-element.3), kind=kOutput, calls=%fused_computation.15 | convolution fusion | flops 538181632 | bytes 1052672 | tf_op jit(solution)/shard_map/dot_general | solution.py:141
  68.3 6.3 %all-to-all-start.2 = ((bf16[32,32,256]{2,1,0:T(8,128)(2,1)}), bf16[32,32,256]{2,1,0:T(8,128)(2,1)S(1)}, u32[]{:S(2)}, u32[]{:S(2)}) async-start(bf16[32,32,256]{2,1,0:T(8,128)(2,1)} %bitcast.30), calls=%async_computation.2 | async-start | bytes 1048576 | tf_op jit(solution)/shard_map/all_to_all | solution.py:142
  74.7 0.4 fusion.32
  75.3 0.7 copy.70
  76.0 30.6 %shard_map.103 = f32[4,256]{1,0:T(4,128)} custom-call(f32[32,4,256]{2,1,0:T(4,128)} %bitcast.95), custom_call_target="tpu_custom_call" | custom-call | tf_op jit(solution)/shard_map/pallas_call | solution.py:69
  106.7 0.8 copy-done.2
  107.5 2.4 %fusion.11 = f32[512,768]{1,0:T(8,128)S(1)} fusion(bf16[256,768]{1,0:T(8,128)(2,1)} %param.13, bf16[1024,256]{1,0:T(8,128)(2,1)} %bitcast.93, s32[1024]{0:T(1024)S(1)} %eq.29), kind=kOutput, calls=%fused_computation.17 | convolution fusion | flops 470417408 | bytes 2494464 | tf_op jit(solution)/shard_map/dot_general | solution.py:148
  109.9 2.0 %fusion.35 = bf16[1,512,256]{2,1,0:T(8,128)(2,1)} fusion(bf16[1,512,256]{2,1,0:T(8,128)(2,1)} %param.8, f32[512,768]{1,0:T(8,128)S(1)} %fusion.32, f32[512,768]{1,0:T(8,128)S(1)} %fusion.11), kind=kLoop, calls=%fused_computation.51 | loop fusion | flops 2097152 | bytes 3670016 | tf_op jit(solution)/shard_map/broadcast_in_dim | solution.py:153
  111.9 0.6 copy.79
  (46 shorter events, 2.6 us)
Async XLA Ops:
  0.6 46.4 %copy-start = (bf16[256,768]{1,0:T(8,128)(2,1)S(1)}, bf16[256,768]{1,0:T(8,128)(2,1)}, u32[]{:S(2)}) copy-start(bf16[256,768]{1,0:T(8,128)(2,1)} %param.11) | copy-start | bytes 1179652
  0.6 31.7 %copy-start.8 = (s32[128,8]{0,1:T(8,128)S(1)}, s32[128,8]{0,1:T(8,128)}, u32[]{:S(2)}) copy-start(s32[128,8]{0,1:T(8,128)} %param.10) | copy-start | bytes 12292
  0.7 31.7 %copy-start.1 = (bf16[256,768]{1,0:T(8,128)(2,1)S(1)}, bf16[256,768]{1,0:T(8,128)(2,1)}, u32[]{:S(2)}) copy-start(bf16[256,768]{1,0:T(8,128)(2,1)} %param.12) | copy-start | bytes 1179652
  0.7 31.7 %copy-start.6 = (bf16[1,128,256]{2,1,0:T(8,128)(2,1)S(1)}, bf16[1,128,256]{2,1,0:T(8,128)(2,1)}, u32[]{:S(2)}) copy-start(bf16[1,128,256]{2,1,0:T(8,128)(2,1)} %param.9) | copy-start | bytes 196612
  28.4 18.5 %all-to-all-start.1 = ((bf16[32,32,256]{2,1,0:T(8,128)(2,1)}), bf16[32,32,256]{2,1,0:T(8,128)(2,1)S(1)}, u32[]{:S(2)}, u32[]{:S(2)}) async-start(bf16[32,32,256]{2,1,0:T(8,128)(2,1)} %bitcast.2), calls=%async_computation.1 | async-start | bytes 1048576 | tf_op jit(solution)/shard_map/all_to_all | solution.py:125
  66.1 8.5 %copy-start.7 = (bf16[1,128,128]{2,1,0:T(8,128)(2,1)S(1)}, bf16[1,128,128]{2,1,0:T(8,128)(2,1)}, u32[]{:S(2)}) copy-start(bf16[1,128,128]{2,1,0:T(8,128)(2,1)} %param.15) | copy-start | bytes 98308
  66.1 8.6 %copy-start.3 = (bf16[1,512,256]{2,1,0:T(8,128)(2,1)S(1)}, bf16[1,512,256]{2,1,0:T(8,128)(2,1)}, u32[]{:S(2)}) copy-start(bf16[1,512,256]{2,1,0:T(8,128)(2,1)} %param.8) | copy-start | bytes 786436
  66.1 8.6 %copy-start.4 = (bf16[256,768]{1,0:T(8,128)(2,1)S(1)}, bf16[256,768]{1,0:T(8,128)(2,1)}, u32[]{:S(2)}) copy-start(bf16[256,768]{1,0:T(8,128)(2,1)} %param.14) | copy-start | bytes 1179652
  66.5 8.6 %copy-start.5 = (bf16[128,256]{1,0:T(8,128)(2,1)}, bf16[128,256]{1,0:T(8,128)(2,1)S(1)}, u32[]{:S(2)}) copy-start(bf16[128,256]{1,0:T(8,128)(2,1)S(1)} %get-tuple-element.4) | copy-start | bytes 196612
  68.3 38.4 %all-to-all-start.2 = ((bf16[32,32,256]{2,1,0:T(8,128)(2,1)}), bf16[32,32,256]{2,1,0:T(8,128)(2,1)S(1)}, u32[]{:S(2)}, u32[]{:S(2)}) async-start(bf16[32,32,256]{2,1,0:T(8,128)(2,1)} %bitcast.30), calls=%async_computation.2 | async-start | bytes 1048576 | tf_op jit(solution)/shard_map/all_to_all | solution.py:142
  106.7 5.3 %copy-start.9 = (f32[4,256]{1,0:T(4,128)S(1)}, f32[4,256]{1,0:T(4,128)}, u32[]{:S(2)}) copy-start(f32[4,256]{1,0:T(4,128)} %shard_map.103) | copy-start | bytes 12292
  106.7 0.8 copy-start.2

commit v3 on v2

v3 whole, which is shorter than its diff:
```python
import jax
import jax.numpy as jnp
from jax import lax
from jax.experimental import pallas as pl
from jax.experimental.pallas import tpu as pltpu
from jax.sharding import PartitionSpec as P

MESH = pl.DeviceIdType.MESH


def gated_update(projected, carried, w_hidden):
    width = carried.shape[1]
    recur = jnp.dot(carried.astype(jnp.bfloat16), w_hidden, preferred_element_type=jnp.float32)
    reset = jax.nn.sigmoid(projected[:, :width] + recur[:, :width])
    update = jax.nn.sigmoid(projected[:, width : 2 * width] + recur[:, width : 2 * width])
    candidate = jnp.tanh(projected[:, 2 * width :] + reset * recur[:, 2 * width :])
    return (1.0 - update) * candidate + update * carried


def _greet(barrier, g, p, n_grp, n_path, with_grp):
    def greet_path(k, c):
        pl.semaphore_signal(barrier, inc=1, device_id=(g, lax.rem(p + k, n_path)), device_id_type=MESH)
        return c

    def greet_grp(k, c):
        pl.semaphore_signal(barrier, inc=1, device_id=(lax.rem(g + k, n_grp), p), device_id_type=MESH)
        return c

    lax.fori_loop(1, n_path, greet_path, 0)
    count = n_path - 1
    if with_grp:
        lax.fori_loop(1, n_grp, greet_grp, 0)
        count += n_grp - 1
    pl.semaphore_wait(barrier, count)


def _ring_copies(src, dst, send, recv, g, p, n_path, sign):
    def make(k):
        return pltpu.make_async_remote_copy(
            src_ref=src.at[k], dst_ref=dst.at[k], send_sem=send.at[k - 1], recv_sem=recv.at[k - 1],
            device_id=(g, lax.rem(p + sign * k + n_path, n_path)), device_id_type=MESH)

    def start(k, c):
        make(k).start()
        return c

    def finish(k, c):
        copy = make(k)
        copy.wait_send()
        copy.wait_recv()
        return c

    return start, finish


def _fetch_kernel(n_grp, n_path, req_ref, links_ref, got_ref, ids_ref,
                  reqin, served, gotbuf, rsend, rrecv, asend, arecv):
    g = lax.axis_index("grp")
    p = lax.axis_index("path")
    _greet(pltpu.get_barrier_semaphore(), g, p, n_grp, n_path, False)
    start_req, finish_req = _ring_copies(req_ref, reqin, rsend, rrecv, g, p, n_path, 1)
    lax.fori_loop(1, n_path, start_req, 0)
    reqin[0] = req_ref[0]
    lax.fori_loop(1, n_path, finish_req, 0)
    n_k, cap, lanes = reqin.shape
    link_dev = links_ref.shape[0]
    ids = reqin[...].reshape(n_k * cap, lanes)[:, 0:1]
    want = (ids == lax.broadcasted_iota(jnp.int32, (1, link_dev), 1)).astype(jnp.bfloat16)
    rows = jnp.dot(want, links_ref[...], preferred_element_type=jnp.float32).astype(jnp.bfloat16)
    served[...] = rows.reshape(n_k, cap, rows.shape[-1])
    start_ans, finish_ans = _ring_copies(served, gotbuf, asend, arecv, g, p, n_path, -1)
    lax.fori_loop(1, n_path, start_ans, 0)
    gotbuf[0] = served[0]
    ids_ref[...] = reqin[...]
    lax.fori_loop(1, n_path, finish_ans, 0)
    got_ref[...] = gotbuf[...]


def fetch_rows(req, own_links, n_grp, n_path):
    n_k, cap, lanes = req.shape
    width = own_links.shape[1]
    return pl.pallas_call(
        lambda *refs: _fetch_kernel(n_grp, n_path, *refs),
        out_shape=(jax.ShapeDtypeStruct((n_k, cap, width), jnp.bfloat16),
                   jax.ShapeDtypeStruct((n_k, cap, lanes), jnp.int32)),
        in_specs=[pl.BlockSpec(memory_space=pltpu.VMEM)] * 2,
        out_specs=(pl.BlockSpec(memory_space=pltpu.VMEM),) * 2,
        scratch_shapes=[
            pltpu.VMEM((n_k, cap, lanes), jnp.int32),
            pltpu.VMEM((n_k, cap, width), jnp.bfloat16),
            pltpu.VMEM((n_k, cap, width), jnp.bfloat16),
            pltpu.SemaphoreType.DMA((n_path - 1,)),
            pltpu.SemaphoreType.DMA((n_path - 1,)),
            pltpu.SemaphoreType.DMA((n_path - 1,)),
            pltpu.SemaphoreType.DMA((n_path - 1,)),
        ],
        compiler_params=pltpu.CompilerParams(collective_id=0, has_side_effects=True),
    )(req, own_links)


def _message_kernel(n_grp, n_path, out_ref, term_ref, inc_ref, grad_ref,
                    inbuf, recv1, recv2, mid, msend, mrecv, send1, got1, send2, got2):
    g = lax.axis_index("grp")
    p = lax.axis_index("path")
    _greet(pltpu.get_barrier_semaphore(), g, p, n_grp, n_path, True)
    start_msg, finish_msg = _ring_copies(out_ref, inbuf, msend, mrecv, g, p, n_path, 1)
    lax.fori_loop(1, n_path, start_msg, 0)

    def path_copy(k, q):
        return pltpu.make_async_remote_copy(
            src_ref=term_ref.at[q], dst_ref=recv1.at[k - 1], send_sem=send1.at[k - 1],
            recv_sem=got1.at[k - 1], device_id=(g, q), device_id_type=MESH)

    def start1(k, c):
        path_copy(k, lax.rem(p + k, n_path)).start()
        return c

    def finish1(k, c):
        copy = path_copy(k, lax.rem(p + k, n_path))
        copy.wait_send()
        copy.wait_recv()
        return c

    lax.fori_loop(1, n_path, start1, 0)
    inbuf[0] = out_ref[0]
    lax.fori_loop(1, n_path, finish1, 0)
    mid[...] = term_ref[p] + jnp.sum(recv1[...], axis=0)

    def grp_copy(k, h):
        return pltpu.make_async_remote_copy(
            src_ref=mid, dst_ref=recv2.at[k - 1], send_sem=send2.at[k - 1],
            recv_sem=got2.at[k - 1], device_id=(h, p), device_id_type=MESH)

    def start2(k, c):
        grp_copy(k, lax.rem(g + k, n_grp)).start()
        return c

    def finish2(k, c):
        copy = grp_copy(k, lax.rem(g + k, n_grp))
        copy.wait_send()
        copy.wait_recv()
        return c

    lax.fori_loop(1, n_grp, start2, 0)
    lax.fori_loop(1, n_path, finish_msg, 0)
    inc_ref[...] = inbuf[...]
    lax.fori_loop(1, n_grp, finish2, 0)
    grad_ref[...] = mid[...] + jnp.sum(recv2[...], axis=0)


def exchange_messages(outgoing, term, n_grp, n_path):
    n_k, cap, width = outgoing.shape
    _, rows, gwidth = term.shape
    return pl.pallas_call(
        lambda *refs: _message_kernel(n_grp, n_path, *refs),
        out_shape=(jax.ShapeDtypeStruct((n_k, cap, width), jnp.bfloat16),
                   jax.ShapeDtypeStruct((rows, gwidth), jnp.float32)),
        in_specs=[pl.BlockSpec(memory_space=pltpu.VMEM)] * 2,
        out_specs=(pl.BlockSpec(memory_space=pltpu.VMEM),) * 2,
        scratch_shapes=[
            pltpu.VMEM((n_k, cap, width), jnp.bfloat16),
            pltpu.VMEM((n_path - 1, rows, gwidth), jnp.float32),
            pltpu.VMEM((n_grp - 1, rows, gwidth), jnp.float32),
            pltpu.VMEM((rows, gwidth), jnp.float32),
            pltpu.SemaphoreType.DMA((n_path - 1,)),
            pltpu.SemaphoreType.DMA((n_path - 1,)),
            pltpu.SemaphoreType.DMA((n_path - 1,)),
            pltpu.SemaphoreType.DMA((n_path - 1,)),
            pltpu.SemaphoreType.DMA((n_grp - 1,)),
            pltpu.SemaphoreType.DMA((n_grp - 1,)),
        ],
        compiler_params=pltpu.CompilerParams(collective_id=1, has_side_effects=True),
    )(outgoing, term)


def shards(
    link_state, path_state, path_links, w_path_in, w_path_hid, w_link_in, w_link_hid, cotangent
):
    bf16, f32 = jnp.bfloat16, jnp.float32
    own_links = link_state[0]
    link_dev, width = own_links.shape
    n_grp = lax.axis_size("grp")
    peer_count = lax.axis_size("path")
    me = lax.axis_index("path")
    path_count, hop_count = path_links.shape
    entries = path_count * hop_count
    capacity = entries // peer_count
    slots = peer_count * capacity
    flat_ids = path_links.reshape(-1)
    is_live = flat_ids >= 0
    owner_id = jnp.where(is_live, flat_ids // link_dev, peer_count)
    local_id = jnp.where(is_live, flat_ids % link_dev, 0)
    marks = (owner_id[:, None] == jnp.arange(peer_count)[None, :]).astype(bf16)
    order = jnp.arange(entries)
    earlier = (order[None, :] < order[:, None]).astype(bf16)
    before = jnp.dot(earlier, marks, preferred_element_type=f32)
    slot_id = jnp.sum(before * marks.astype(f32), axis=1).astype(jnp.int32)
    offset = lax.rem(owner_id - me + peer_count, peer_count)
    dest = jnp.where(is_live, offset * capacity + slot_id, -1)
    slot_ids = jnp.arange(slots)
    route = dest[None, :] == slot_ids[:, None]
    requests = jnp.sum(jnp.where(route, local_id[None, :] + 1, 0), axis=1) - 1
    req = jnp.broadcast_to(requests.reshape(peer_count, capacity, 1), (peer_count, capacity, 128))
    got, req_ids = fetch_rows(req, own_links, n_grp, peer_count)
    route_t = (dest[:, None] == slot_ids[None, :]).astype(bf16)
    fetched = jnp.dot(route_t, got.reshape(slots, width), preferred_element_type=f32).astype(bf16)
    projected = jnp.dot(fetched, w_path_in, preferred_element_type=f32)
    projected = projected.reshape(path_count, hop_count, 3 * width)
    live_grid = is_live.reshape(path_count, hop_count)
    carried = path_state[0].astype(f32)
    messages = []
    for hop_index in range(hop_count):
        renewed = gated_update(projected[:, hop_index], carried, w_path_hid)
        carried = jnp.where(live_grid[:, hop_index, None], renewed, carried)
        messages.append(carried.astype(bf16))
    path_final = carried.astype(bf16)
    flat_messages = jnp.stack(messages, axis=1).reshape(-1, width)
    outgoing = jnp.dot(route.astype(bf16), flat_messages, preferred_element_type=f32).astype(bf16)
    cot = cotangent[0].reshape(path_count, peer_count, -1)
    term = lax.dot_general(cot, path_final, (((0,), (0,)), ((), ())), preferred_element_type=f32)
    incoming, read_grad = exchange_messages(
        outgoing.reshape(peer_count, capacity, width), term, n_grp, peer_count)
    received = req_ids[:, :, 0].reshape(-1)
    want = (received[:, None] == jnp.arange(link_dev)[None, :]).astype(bf16)
    link_sum = lax.dot_general(
        want, incoming.reshape(slots, width), (((0,), (0,)), ((), ())), preferred_element_type=f32
    )
    link_proj = jnp.dot(link_sum.astype(bf16), w_link_in, preferred_element_type=f32)
    link_next = gated_update(link_proj, own_links.astype(f32), w_link_hid).astype(bf16)
    return (link_next[None], path_final[None], read_grad)


def solution(mesh):
    return jax.shard_map(
        shards,
        mesh=mesh,
        in_specs=(
            P("grp", "path", None),
            P("grp", "path", None),
            P("path", None),
            P(),
            P(),
            P(),
            P(),
            P("grp", "path", None),
        ),
        out_specs=(P("grp", "path", None), P("grp", "path", None), P("path", None)),
        check_vma=False,
    )
```

time: 113 us -> 99.6 us (0.88)
  Pallas kernels: 30.6 us -> 79.5 us
  blocking collectives: 22.1 us -> 0 us
  waiting for transfers between devices: 14.4 us -> 0 us
  local copies, waits for them, and re-layouts: 17.4 us -> 6.57 us
  starting transfers between devices: 10.2 us -> 0 us
  matrix products: 12.7 us -> 9.73 us
  other arithmetic: 4.15 us -> 2.54 us
    pallas_call x1 -> x2, Pallas kernels: 30.6 us -> 79.5 us  [the longest x1 42 us: fetch_rows(): pl.pallas_call(lambda *refs: _fetch_kernel(n_grp, n_path, *refs), out_sha...]
    all_to_all x1 -> x0, blocking collectives: 22.1 us -> none  [shards(): lax.all_to_all(requests.reshape(peer_count, capacity), 'path', split_axis...]
    all_to_all x2 -> x0, waiting for transfers between devices: 14.4 us -> none  [the longest x1 14.4 us: shards(): lax.all_to_all(served.reshape(peer_count, capacity, width), 'path', split...]
    slice x1, local copies, waits for them, and re-layouts: 13.2 us -> 2.14 us  [shards(): renewed = gated_update(projected[:, hop_index], carried, w_path_hid)]
    all_to_all x2 -> x0, starting transfers between devices: 10.2 us -> none  [the longest x1 6.29 us: shards(): lax.all_to_all(outgoing.reshape(peer_count, capacity, width), 'path', spl...]
    dot_general x1 -> x0, matrix products: 2.26 us -> none  [shards(): served = jnp.dot(want, own_links, preferred_element_type=f32).astype(bf16)]
    unnamed x23 -> x25, local copies, waits for them, and re-layouts: 2.4 us -> 1.61 us
  transfers between devices with their start and end apart: 2 -> 0, of which waited for: 1 -> 0; matrix products, arithmetic and copies ran while one was open for 1% -> 0% of each run, Pallas kernels for 27% -> 0%
where the time goes in v3:
time: 99.6 us; the launch traced here: 99.3 us
  Pallas kernels  79.5 us (80%)
  matrix products  9.73 us (10%)
  local copies, waits for them, and re-layouts  6.57 us (7%)
  other arithmetic  2.54 us (3%)
  between operations  1.01 us (1%)
    pallas_call x1, Pallas kernels, fetch_rows(): pl.pallas_call(lambda *refs: _fetch_kernel(n_grp, n_path, *refs), out_sha...  42 us
    pallas_call x1, Pallas kernels, exchange_messages(): pl.pallas_call(lambda *refs: _message_kernel(n_grp, n_path, *refs), out_s...  37.5 us
    dot_general x1, matrix products, shards(): projected = jnp.dot(fetched, w_path_in, preferred_element_type=f32)  2.86 us
    dot_general x1, matrix products, shards(): jnp.dot(link_sum.astype(bf16), w_link_in, preferred_element_type=f32)  2.32 us
    slice x1, local copies, waits for them, and re-layouts, shards(): renewed = gated_update(projected[:, hop_index], carried, w_path_hid)  2.14 us
    dot_general x9, matrix products, gated_update(): jnp.dot(carried.astype(jnp.bfloat16), w_hidden, preferred_element_type=jn...  2.06 us

profile of v3, /device:TPU:1, one launch (start us, length us, event | category | flops | bytes accessed | tf_op | source)
XLA Modules:
  0.0 99.3 jit_solution(526598087025378716)
XLA Ops:
  0.6 0.8 copy.34
  1.6 0.5 fusion.11
  2.2 0.5 select_reduce_fusion
  2.7 1.0 %broadcast_in_dim.101.refs_0_ = s32[32,32,128]{2,1,0:T(8,128)} broadcast(s32[32,32]{1,0:T(8,128)S(1)} %sub.57), dimensions={0,1} | broadcast | bytes 528384 | tf_op jit(solution)/shard_map/broadcast_in_dim | solution.py:203
  3.7 42.0 %shard_map.103 = (bf16[32,32,256]{2,1,0:T(8,128)(2,1)}, s32[32,32,128]{2,1,0:T(8,128)}) custom-call(s32[32,32,128]{2,1,0:T(8,128)} %broadcast_in_dim.101.refs_0_, bf16[512,256]{1,0:T(8,128)(2,1)} %bitcast.88), custom_call_target="tpu_custom_call" | custom-call | tf_op jit(solution)/shard_map/pallas_call | solution.py:82
  45.8 2.9 %convolution_bitcast_fusion = f32[128,8,768]{2,1,0:T(8,128)S(1)} fusion(bf16[256,768]{1,0:T(8,128)(2,1)S(1)} %copy-done, bf16[1024,256]{1,0:T(8,128)(2,1)} %bitcast.94, s32[1024]{0:T(1024)S(1)} %fusion.159), kind=kOutput, calls=%fused_computation.11 | convolution fusion | flops 940834816 | bytes 4067328 | tf_op jit(solution)/shard_map/dot_general | solution.py:207
  48.7 2.1 %fusion.173 = (f32[128,1,768]{2,1,0:T(1,128)S(1)}, f32[128,1,768]{2,1,0:T(1,128)S(1)}, f32[128,1,768]{2,1,0:T(1,128)S(1)}, f32[128,1,768]{2,1,0:T(1,128)S(1)}, f...) fusion(f32[128,8,768]{2,1,0:T(8,128)S(1)} %convolution_bitcast_, ...), kind=kLoop, calls=%fused_computation.238 | loop fusion | bytes 6291456 | tf_op jit(solution)/shard_map/slice | solution.py:213
  51.0 0.2 fusion.137
  51.3 0.2 fusion.153
  51.6 0.2 fusion.151
  52.0 0.2 fusion.149
  52.4 0.2 fusion.147
  52.8 0.2 fusion.145
  53.1 0.2 fusion.143
  53.5 0.2 fusion.141
  53.9 1.8 %fusion.7 = bf16[1024,256]{1,0:T(8,128)(2,1)} fusion(s32[1024]{0:T(1024)S(1)} %fusion.159, bf16[128,8,256]{2,0,1:T(8,128)(2,1)S(1)} %get-tuple-element.11), kind=kOutput, calls=%fused_computation.13 | convolution fusion | flops 538181632 | bytes 1052672 | tf_op jit(solution)/shard_map/dot_general | solution.py:218
  55.8 0.2 fusion.135
  56.0 0.7 copy.70
  56.8 37.5 %shard_map.104 = (bf16[32,32,256]{2,1,0:T(8,128)(2,1)}, f32[4,256]{1,0:T(4,128)}) custom-call(bf16[32,32,256]{2,1,0:T(8,128)(2,1)} %bitcast.90, f32[32,4,256]{2,1,0:T(4,128)} %bitcast.91), custom_call_target="tpu_custom_call" | custom-call | tf_op jit(solution)/shard_map/pallas_call | solution.py:154
  94.2 0.6 slice_reduce_fusion
  94.9 2.3 %fusion.9 = f32[512,768]{1,0:T(8,128)S(1)} fusion(bf16[256,768]{1,0:T(8,128)(2,1)S(1)} %copy-done.4, bf16[1024,256]{1,0:T(8,128)(2,1)} %bitcast.89, s32[1024]{0:T(1024)S(1)} %eq.29), kind=kOutput, calls=%fused_computation.15 | convolution fusion | flops 470417408 | bytes 2494464 | tf_op jit(solution)/shard_map/dot_general | solution.py:228
  97.3 0.4 fusion.164
  97.7 1.1 %fusion.29 = bf16[1,512,256]{2,1,0:T(8,128)(2,1)} fusion(f32[512,768]{1,0:T(8,128)S(1)} %fusion.164, f32[512,768]{1,0:T(8,128)S(1)} %fusion.9, bf16[1,512,256]{2,1,0:T(8,128)(2,1)S(1)} %copy-done.2), kind=kLoop, calls=%fused_computation.46 | loop fusion | flops 2097152 | bytes 3670016 | tf_op jit(solution)/shard_map/broadcast_in_dim | solution.py:230
  98.7 0.6 copy.79
  (43 shorter events, 1.6 us)
Async XLA Ops:
  0.6 45.2 %copy-start = (bf16[256,768]{1,0:T(8,128)(2,1)S(1)}, bf16[256,768]{1,0:T(8,128)(2,1)}, u32[]{:S(2)}) copy-start(bf16[256,768]{1,0:T(8,128)(2,1)} %param.11) | copy-start | bytes 1179652
  48.6 2.3 %copy-start.9 = (s32[128,8]{0,1:T(8,128)S(1)}, s32[128,8]{0,1:T(8,128)}, u32[]{:S(2)}) copy-start(s32[128,8]{0,1:T(8,128)} %param.10) | copy-start | bytes 12292
  48.7 2.3 %copy-start.1 = (bf16[256,768]{1,0:T(8,128)(2,1)S(1)}, bf16[256,768]{1,0:T(8,128)(2,1)}, u32[]{:S(2)}) copy-start(bf16[256,768]{1,0:T(8,128)(2,1)} %param.12) | copy-start | bytes 1179652
  48.7 2.3 %copy-start.7 = (bf16[1,128,256]{2,1,0:T(8,128)(2,1)S(1)}, bf16[1,128,256]{2,1,0:T(8,128)(2,1)}, u32[]{:S(2)}) copy-start(bf16[1,128,256]{2,1,0:T(8,128)(2,1)} %param.9) | copy-start | bytes 196612
  53.4 2.3 %copy-start.8 = (bf16[1,128,128]{2,1,0:T(8,128)(2,1)S(1)}, bf16[1,128,128]{2,1,0:T(8,128)(2,1)}, u32[]{:S(2)}) copy-start(bf16[1,128,128]{2,1,0:T(8,128)(2,1)} %param.15) | copy-start | bytes 98308
  53.5 40.7 %copy-start.3 = (s32[32,32,128]{2,1,0:T(8,128)S(1)}, s32[32,32,128]{2,1,0:T(8,128)}, u32[]{:S(2)}) copy-start(s32[32,32,128]{2,1,0:T(8,128)} %get-tuple-element.7) | copy-start | bytes 1572868
  53.8 41.2 %copy-start.4 = (bf16[256,768]{1,0:T(8,128)(2,1)S(1)}, bf16[256,768]{1,0:T(8,128)(2,1)}, u32[]{:S(2)}) copy-start(bf16[256,768]{1,0:T(8,128)(2,1)} %param.13) | copy-start | bytes 1179652
  53.9 43.4 %copy-start.6 = (bf16[128,256]{1,0:T(8,128)(2,1)}, bf16[128,256]{1,0:T(8,128)(2,1)S(1)}, u32[]{:S(2)}) copy-start(bf16[128,256]{1,0:T(8,128)(2,1)S(1)} %get-tuple-element.12) | copy-start | bytes 196612
  53.9 43.4 %copy-start.2 = (bf16[1,512,256]{2,1,0:T(8,128)(2,1)S(1)}, bf16[1,512,256]{2,1,0:T(8,128)(2,1)}, u32[]{:S(2)}) copy-start(bf16[1,512,256]{2,1,0:T(8,128)(2,1)} %param.8) | copy-start | bytes 786436
  53.9 43.4 %copy-start.5 = (bf16[256,768]{1,0:T(8,128)(2,1)S(1)}, bf16[256,768]{1,0:T(8,128)(2,1)}, u32[]{:S(2)}) copy-start(bf16[256,768]{1,0:T(8,128)(2,1)} %param.14) | copy-start | bytes 1179652
  97.3 1.5 %copy-start.10 = (f32[4,256]{1,0:T(4,128)S(1)}, f32[4,256]{1,0:T(4,128)}, u32[]{:S(2)}) copy-start(f32[4,256]{1,0:T(4,128)} %get-tuple-element.58) | copy-start | bytes 12292

commit v4 on v3

--- a/solution.py
+++ b/solution.py
@@ -54,7 +54,7 @@
 
 
 def _fetch_kernel(n_grp, n_path, req_ref, links_ref, got_ref, ids_ref,
-                  reqin, served, gotbuf, rsend, rrecv, asend, arecv):
+                  reqin, want, served, gotbuf, rsend, rrecv, asend, arecv):
     g = lax.axis_index("grp")
     p = lax.axis_index("path")
     _greet(pltpu.get_barrier_semaphore(), g, p, n_grp, n_path, False)
@@ -62,12 +62,14 @@
     lax.fori_loop(1, n_path, start_req, 0)
     reqin[0] = req_ref[0]
     lax.fori_loop(1, n_path, finish_req, 0)
-    n_k, cap, lanes = reqin.shape
+    n_k, cap = served.shape[0], served.shape[1]
     link_dev = links_ref.shape[0]
-    ids = reqin[...].reshape(n_k * cap, lanes)[:, 0:1]
-    want = (ids == lax.broadcasted_iota(jnp.int32, (1, link_dev), 1)).astype(jnp.bfloat16)
-    rows = jnp.dot(want, links_ref[...], preferred_element_type=jnp.float32).astype(jnp.bfloat16)
-    served[...] = rows.reshape(n_k, cap, rows.shape[-1])
+    ids_t = jnp.transpose(reqin[:, 0, :])
+    lanes = lax.broadcasted_iota(jnp.int32, (1, link_dev), 1)
+    for k in range(n_k):
+        want[k * cap : (k + 1) * cap, :] = (ids_t[0:cap, k : k + 1] == lanes).astype(jnp.bfloat16)
+    rows = jnp.dot(want[...], links_ref[...], preferred_element_type=jnp.float32).astype(jnp.bfloat16)
+    served[...] = rows.reshape(served.shape)
     start_ans, finish_ans = _ring_copies(served, gotbuf, asend, arecv, g, p, n_path, -1)
     lax.fori_loop(1, n_path, start_ans, 0)
     gotbuf[0] = served[0]
@@ -76,17 +78,18 @@
     got_ref[...] = gotbuf[...]
 
 
-def fetch_rows(req, own_links, n_grp, n_path):
-    n_k, cap, lanes = req.shape
+def fetch_rows(req, own_links, cap, n_grp, n_path):
+    n_k, rows, lanes = req.shape
     width = own_links.shape[1]
     return pl.pallas_call(
         lambda *refs: _fetch_kernel(n_grp, n_path, *refs),
         out_shape=(jax.ShapeDtypeStruct((n_k, cap, width), jnp.bfloat16),
-                   jax.ShapeDtypeStruct((n_k, cap, lanes), jnp.int32)),
+                   jax.ShapeDtypeStruct((n_k, rows, lanes), jnp.int32)),
         in_specs=[pl.BlockSpec(memory_space=pltpu.VMEM)] * 2,
         out_specs=(pl.BlockSpec(memory_space=pltpu.VMEM),) * 2,
         scratch_shapes=[
-            pltpu.VMEM((n_k, cap, lanes), jnp.int32),
+            pltpu.VMEM((n_k, rows, lanes), jnp.int32),
+            pltpu.VMEM((n_k * cap, own_links.shape[0]), jnp.bfloat16),
             pltpu.VMEM((n_k, cap, width), jnp.bfloat16),
             pltpu.VMEM((n_k, cap, width), jnp.bfloat16),
             pltpu.SemaphoreType.DMA((n_path - 1,)),
@@ -200,8 +203,9 @@
     slot_ids = jnp.arange(slots)
     route = dest[None, :] == slot_ids[:, None]
     requests = jnp.sum(jnp.where(route, local_id[None, :] + 1, 0), axis=1) - 1
-    req = jnp.broadcast_to(requests.reshape(peer_count, capacity, 1), (peer_count, capacity, 128))
-    got, req_ids = fetch_rows(req, own_links, n_grp, peer_count)
+    req = jnp.full((peer_count, 8, 128), -1, jnp.int32)
+    req = lax.dynamic_update_slice(req, requests.reshape(peer_count, 1, capacity), (0, 0, 0))
+    got, req_ids = fetch_rows(req, own_links, capacity, n_grp, peer_count)
     route_t = (dest[:, None] == slot_ids[None, :]).astype(bf16)
     fetched = jnp.dot(route_t, got.reshape(slots, width), preferred_element_type=f32).astype(bf16)
     projected = jnp.dot(fetched, w_path_in, preferred_element_type=f32)
@@ -220,7 +224,7 @@
     term = lax.dot_general(cot, path_final, (((0,), (0,)), ((), ())), preferred_element_type=f32)
     incoming, read_grad = exchange_messages(
         outgoing.reshape(peer_count, capacity, width), term, n_grp, peer_count)
-    received = req_ids[:, :, 0].reshape(-1)
+    received = req_ids[:, 0, :capacity].reshape(-1)
     want = (received[:, None] == jnp.arange(link_dev)[None, :]).astype(bf16)
     link_sum = lax.dot_general(
         want, incoming.reshape(slots, width), (((0,), (0,)), ((), ())), preferred_element_type=f32

time: 99.6 us -> 90.2 us (0.906)
  Pallas kernels: 79.5 us -> 70 us
    pallas_call x1, Pallas kernels: 42 us -> 36.1 us  [fetch_rows(): pl.pallas_call(lambda *refs: _fetch_kernel(n_grp, n_path, *refs), out_sha...]
    pallas_call x1, Pallas kernels: 37.5 us -> 33.9 us  [exchange_messages(): pl.pallas_call(lambda *refs: _message_kernel(n_grp, n_path, *refs), out_s...]
    broadcast_in_dim x1 -> x0, local copies, waits for them, and re-layouts: 1 us -> none  [shards(): jnp.broadcast_to(requests.reshape(peer_count, capacity, 1), (peer_count,...]
where the time goes in v4:
time: 90.2 us; the launch traced here: 89.9 us
  Pallas kernels  70 us (78%)
  matrix products  9.73 us (11%)
  local copies, waits for them, and re-layouts  6.59 us (7%)
  other arithmetic  2.57 us (3%)
  between operations  0.98 us (1%)
    pallas_call x1, Pallas kernels, fetch_rows(): pl.pallas_call(lambda *refs: _fetch_kernel(n_grp, n_path, *refs), out_sha...  36.1 us
    pallas_call x1, Pallas kernels, exchange_messages(): pl.pallas_call(lambda *refs: _message_kernel(n_grp, n_path, *refs), out_s...  33.9 us
    dot_general x1, matrix products, shards(): projected = jnp.dot(fetched, w_path_in, preferred_element_type=f32)  2.86 us
    dot_general x1, matrix products, shards(): jnp.dot(link_sum.astype(bf16), w_link_in, preferred_element_type=f32)  2.31 us
    slice x1, local copies, waits for them, and re-layouts, shards(): renewed = gated_update(projected[:, hop_index], carried, w_path_hid)  2.14 us
    dot_general x9, matrix products, gated_update(): jnp.dot(carried.astype(jnp.bfloat16), w_hidden, preferred_element_type=jn...  2.08 us

profile of v4, /device:TPU:1, one launch (start us, length us, event | category | flops | bytes accessed | tf_op | source)
XLA Modules:
  0.0 89.9 jit_solution(12536817189034827616)
XLA Ops:
  0.6 0.8 copy.34
  1.6 0.5 fusion.11
  2.2 0.5 select_reduce_fusion
  2.8 0.7 dynamic_update_slice.3.refs_0_
  3.4 36.1 %shard_map.103 = (bf16[32,32,256]{2,1,0:T(8,128)(2,1)}, s32[32,8,128]{2,1,0:T(8,128)}) custom-call(s32[32,8,128]{2,1,0:T(8,128)} %dynamic_update_slice.3.refs_0_, bf16[512,256]{1,0:T(8,128)(2,1)} %bitcast.88), custom_call_target="tpu_custom_call" | custom-call | tf_op jit(solution)/shard_map/pallas_call | solution.py:84
  39.6 2.9 %convolution_bitcast_fusion = f32[128,8,768]{2,1,0:T(8,128)S(1)} fusion(bf16[256,768]{1,0:T(8,128)(2,1)S(1)} %copy-done, bf16[1024,256]{1,0:T(8,128)(2,1)} %bitcast.94, s32[1024]{0:T(1024)S(1)} %fusion.159), kind=kOutput, calls=%fused_computation.11 | convolution fusion | flops 940834816 | bytes 4067328 | tf_op jit(solution)/shard_map/dot_general | solution.py:211
  42.5 2.1 %fusion.173 = (f32[128,1,768]{2,1,0:T(1,128)S(1)}, f32[128,1,768]{2,1,0:T(1,128)S(1)}, f32[128,1,768]{2,1,0:T(1,128)S(1)}, f32[128,1,768]{2,1,0:T(1,128)S(1)}, f...) fusion(f32[128,8,768]{2,1,0:T(8,128)S(1)} %convolution_bitcast_, ...), kind=kLoop, calls=%fused_computation.238 | loop fusion | bytes 6291456 | tf_op jit(solution)/shard_map/slice | solution.py:217
  44.8 0.2 fusion.137
  45.1 0.2 fusion.153
  45.5 0.2 fusion.151
  45.9 0.2 fusion.149
  46.2 0.2 fusion.147
  46.6 0.2 fusion.145
  47.0 0.2 fusion.143
  47.4 0.2 fusion.141
  47.8 1.8 %fusion.7 = bf16[1024,256]{1,0:T(8,128)(2,1)} fusion(s32[1024]{0:T(1024)S(1)} %fusion.159, bf16[128,8,256]{2,0,1:T(8,128)(2,1)S(1)} %get-tuple-element.11), kind=kOutput, calls=%fused_computation.13 | convolution fusion | flops 538181632 | bytes 1052672 | tf_op jit(solution)/shard_map/dot_general | solution.py:222
  49.7 0.2 fusion.135
  49.8 0.7 copy.70
  50.6 33.9 %shard_map.104 = (bf16[32,32,256]{2,1,0:T(8,128)(2,1)}, f32[4,256]{1,0:T(4,128)}) custom-call(bf16[32,32,256]{2,1,0:T(8,128)(2,1)} %bitcast.90, f32[32,4,256]{2,1,0:T(4,128)} %bitcast.91), custom_call_target="tpu_custom_call" | custom-call | tf_op jit(solution)/shard_map/pallas_call | solution.py:157
  84.5 0.9 %slice_reduce_fusion = s32[32,32]{1,0:T(8,128)S(1)} fusion(s32[32,8,128]{2,1,0:T(8,128)} %get-tuple-element.7), kind=kLoop, calls=%fused_computation.207 | loop fusion | bytes 8192 | tf_op jit(solution)/shard_map/slice | solution.py:227
  85.5 2.3 %fusion.9 = f32[512,768]{1,0:T(8,128)S(1)} fusion(bf16[256,768]{1,0:T(8,128)(2,1)S(1)} %copy-done.3, bf16[1024,256]{1,0:T(8,128)(2,1)} %bitcast.89, s32[1024]{0:T(1024)S(1)} %eq.29), kind=kOutput, calls=%fused_computation.15 | convolution fusion | flops 470417408 | bytes 2494464 | tf_op jit(solution)/shard_map/dot_general | solution.py:232
  87.9 0.4 fusion.164
  88.2 1.1 %fusion.29 = bf16[1,512,256]{2,1,0:T(8,128)(2,1)} fusion(f32[512,768]{1,0:T(8,128)S(1)} %fusion.164, f32[512,768]{1,0:T(8,128)S(1)} %fusion.9, bf16[1,512,256]{2,1,0:T(8,128)(2,1)S(1)} %copy-done.2), kind=kLoop, calls=%fused_computation.45 | loop fusion | flops 2097152 | bytes 3670016 | tf_op jit(solution)/shard_map/broadcast_in_dim | solution.py:234
  89.3 0.6 copy.79
  (41 shorter events, 1.6 us)
Async XLA Ops:
  0.6 39.0 %copy-start = (bf16[256,768]{1,0:T(8,128)(2,1)S(1)}, bf16[256,768]{1,0:T(8,128)(2,1)}, u32[]{:S(2)}) copy-start(bf16[256,768]{1,0:T(8,128)(2,1)} %param.11) | copy-start | bytes 1179652
  42.5 2.3 %copy-start.8 = (s32[128,8]{0,1:T(8,128)S(1)}, s32[128,8]{0,1:T(8,128)}, u32[]{:S(2)}) copy-start(s32[128,8]{0,1:T(8,128)} %param.10) | copy-start | bytes 12292
  42.5 2.3 %copy-start.1 = (bf16[256,768]{1,0:T(8,128)(2,1)S(1)}, bf16[256,768]{1,0:T(8,128)(2,1)}, u32[]{:S(2)}) copy-start(bf16[256,768]{1,0:T(8,128)(2,1)} %param.12) | copy-start | bytes 1179652
  42.5 2.3 %copy-start.6 = (bf16[1,128,256]{2,1,0:T(8,128)(2,1)S(1)}, bf16[1,128,256]{2,1,0:T(8,128)(2,1)}, u32[]{:S(2)}) copy-start(bf16[1,128,256]{2,1,0:T(8,128)(2,1)} %param.9) | copy-start | bytes 196612
  47.2 2.3 %copy-start.7 = (bf16[1,128,128]{2,1,0:T(8,128)(2,1)S(1)}, bf16[1,128,128]{2,1,0:T(8,128)(2,1)}, u32[]{:S(2)}) copy-start(bf16[1,128,128]{2,1,0:T(8,128)(2,1)} %param.15) | copy-start | bytes 98308
  47.4 38.1 %copy-start.3 = (bf16[256,768]{1,0:T(8,128)(2,1)S(1)}, bf16[256,768]{1,0:T(8,128)(2,1)}, u32[]{:S(2)}) copy-start(bf16[256,768]{1,0:T(8,128)(2,1)} %param.13) | copy-start | bytes 1179652
  47.7 40.1 %copy-start.5 = (bf16[128,256]{1,0:T(8,128)(2,1)}, bf16[128,256]{1,0:T(8,128)(2,1)S(1)}, u32[]{:S(2)}) copy-start(bf16[128,256]{1,0:T(8,128)(2,1)S(1)} %get-tuple-element.12) | copy-start | bytes 196612
  47.7 40.1 %copy-start.2 = (bf16[1,512,256]{2,1,0:T(8,128)(2,1)S(1)}, bf16[1,512,256]{2,1,0:T(8,128)(2,1)}, u32[]{:S(2)}) copy-start(bf16[1,512,256]{2,1,0:T(8,128)(2,1)} %param.8) | copy-start | bytes 786436
  47.8 40.1 %copy-start.4 = (bf16[256,768]{1,0:T(8,128)(2,1)S(1)}, bf16[256,768]{1,0:T(8,128)(2,1)}, u32[]{:S(2)}) copy-start(bf16[256,768]{1,0:T(8,128)(2,1)} %param.14) | copy-start | bytes 1179652
  87.9 1.5 %copy-start.9 = (f32[4,256]{1,0:T(4,128)S(1)}, f32[4,256]{1,0:T(4,128)}, u32[]{:S(2)}) copy-start(f32[4,256]{1,0:T(4,128)} %get-tuple-element.58) | copy-start | bytes 12292

commit v5 on v4

--- a/solution.py
+++ b/solution.py
@@ -101,8 +101,8 @@
     )(req, own_links)
 
 
-def _message_kernel(n_grp, n_path, out_ref, term_ref, inc_ref, grad_ref,
-                    inbuf, recv1, recv2, mid, msend, mrecv, send1, got1, send2, got2):
+def _message_kernel(n_grp, n_path, out_ref, term_ref, sel_ref, w_in_ref, recur_ref, links_ref,
+                    next_ref, grad_ref, inbuf, recv1, recv2, mid, msend, mrecv, send1, got1, send2, got2):
     g = lax.axis_index("grp")
     p = lax.axis_index("path")
     _greet(pltpu.get_barrier_semaphore(), g, p, n_grp, n_path, True)
@@ -146,19 +146,28 @@
 
     lax.fori_loop(1, n_grp, start2, 0)
     lax.fori_loop(1, n_path, finish_msg, 0)
-    inc_ref[...] = inbuf[...]
+    n_k, cap, width = inbuf.shape
+    incoming = inbuf[...].reshape(n_k * cap, width)
+    link_sum = jnp.dot(sel_ref[...], incoming, preferred_element_type=jnp.float32)
+    link_proj = jnp.dot(link_sum.astype(jnp.bfloat16), w_in_ref[...], preferred_element_type=jnp.float32)
+    recur = recur_ref[...]
+    own = links_ref[...].astype(jnp.float32)
+    reset = jax.nn.sigmoid(link_proj[:, :width] + recur[:, :width])
+    update = jax.nn.sigmoid(link_proj[:, width : 2 * width] + recur[:, width : 2 * width])
+    candidate = jnp.tanh(link_proj[:, 2 * width :] + reset * recur[:, 2 * width :])
+    next_ref[...] = ((1.0 - update) * candidate + update * own).astype(next_ref.dtype)
     lax.fori_loop(1, n_grp, finish2, 0)
     grad_ref[...] = mid[...] + jnp.sum(recv2[...], axis=0)
 
 
-def exchange_messages(outgoing, term, n_grp, n_path):
+def exchange_messages(outgoing, term, sel, w_link_in, recur, own_links, n_grp, n_path):
     n_k, cap, width = outgoing.shape
     _, rows, gwidth = term.shape
     return pl.pallas_call(
         lambda *refs: _message_kernel(n_grp, n_path, *refs),
-        out_shape=(jax.ShapeDtypeStruct((n_k, cap, width), jnp.bfloat16),
+        out_shape=(jax.ShapeDtypeStruct(own_links.shape, jnp.bfloat16),
                    jax.ShapeDtypeStruct((rows, gwidth), jnp.float32)),
-        in_specs=[pl.BlockSpec(memory_space=pltpu.VMEM)] * 2,
+        in_specs=[pl.BlockSpec(memory_space=pltpu.VMEM)] * 6,
         out_specs=(pl.BlockSpec(memory_space=pltpu.VMEM),) * 2,
         scratch_shapes=[
             pltpu.VMEM((n_k, cap, width), jnp.bfloat16),
@@ -173,7 +182,7 @@
             pltpu.SemaphoreType.DMA((n_grp - 1,)),
         ],
         compiler_params=pltpu.CompilerParams(collective_id=1, has_side_effects=True),
-    )(outgoing, term)
+    )(outgoing, term, sel, w_link_in, recur, own_links)
 
 
 def shards(
@@ -205,6 +214,7 @@
     requests = jnp.sum(jnp.where(route, local_id[None, :] + 1, 0), axis=1) - 1
     req = jnp.full((peer_count, 8, 128), -1, jnp.int32)
     req = lax.dynamic_update_slice(req, requests.reshape(peer_count, 1, capacity), (0, 0, 0))
+    link_recur = jnp.dot(own_links, w_link_hid, preferred_element_type=f32)
     got, req_ids = fetch_rows(req, own_links, capacity, n_grp, peer_count)
     route_t = (dest[:, None] == slot_ids[None, :]).astype(bf16)
     fetched = jnp.dot(route_t, got.reshape(slots, width), preferred_element_type=f32).astype(bf16)
@@ -222,15 +232,11 @@
     outgoing = jnp.dot(route.astype(bf16), flat_messages, preferred_element_type=f32).astype(bf16)
     cot = cotangent[0].reshape(path_count, peer_count, -1)
     term = lax.dot_general(cot, path_final, (((0,), (0,)), ((), ())), preferred_element_type=f32)
-    incoming, read_grad = exchange_messages(
-        outgoing.reshape(peer_count, capacity, width), term, n_grp, peer_count)
     received = req_ids[:, 0, :capacity].reshape(-1)
-    want = (received[:, None] == jnp.arange(link_dev)[None, :]).astype(bf16)
-    link_sum = lax.dot_general(
-        want, incoming.reshape(slots, width), (((0,), (0,)), ((), ())), preferred_element_type=f32
-    )
-    link_proj = jnp.dot(link_sum.astype(bf16), w_link_in, preferred_element_type=f32)
-    link_next = gated_update(link_proj, own_links.astype(f32), w_link_hid).astype(bf16)
+    sel = (jnp.arange(link_dev)[:, None] == received[None, :]).astype(bf16)
+    link_next, read_grad = exchange_messages(
+        outgoing.reshape(peer_count, capacity, width), term, sel, w_link_in, link_recur, own_links,
+        n_grp, peer_count)
     return (link_next[None], path_final[None], read_grad)
 
 

time: 90.2 us -> 92.5 us (1.025)
  local copies, waits for them, and re-layouts: 6.59 us -> 8.93 us
  matrix products: 9.73 us -> 8.62 us
  Pallas kernels: 70 us -> 71 us
    unnamed x23 -> x20, local copies, waits for them, and re-layouts: 1.61 us -> 3.95 us
    convert_element_type x0 -> x1, other arithmetic: none -> 1.3 us  [shards(): sel = (jnp.arange(link_dev)[:, None] == received[None, :]).astype(bf16)]
    broadcast_in_dim x1 -> x0, other arithmetic: 1.08 us -> none  [shards(): return (link_next[None], path_final[None], read_grad)]
    pallas_call x1, Pallas kernels: 33.9 us -> 34.8 us  [exchange_messages(): pl.pallas_call(lambda *refs: _message_kernel(n_grp, n_path, *refs), out_s...]
    dot_general x9 -> x8, matrix products: 2.08 us -> 1.71 us  [gated_update(): jnp.dot(carried.astype(jnp.bfloat16), w_hidden, preferred_element_type=jn...]
where the time goes in v5:
time: 92.5 us; the launch traced here: 92.2 us
  Pallas kernels  71 us (77%)
  local copies, waits for them, and re-layouts  8.93 us (10%)
  matrix products  8.62 us (9%)
  other arithmetic  2.78 us (3%)
  between operations  0.94 us (1%)
    pallas_call x1, Pallas kernels, fetch_rows(): pl.pallas_call(lambda *refs: _fetch_kernel(n_grp, n_path, *refs), out_sha...  36.1 us
    pallas_call x1, Pallas kernels, exchange_messages(): pl.pallas_call(lambda *refs: _message_kernel(n_grp, n_path, *refs), out_s...  34.8 us
    unnamed x20, local copies, waits for them, and re-layouts  3.95 us
    dot_general x1, matrix products, shards(): projected = jnp.dot(fetched, w_path_in, preferred_element_type=f32)  2.86 us
    slice x1, local copies, waits for them, and re-layouts, shards(): renewed = gated_update(projected[:, hop_index], carried, w_path_hid)  2.14 us

profile of v5, /device:TPU:1, one launch (start us, length us, event | category | flops | bytes accessed | tf_op | source)
XLA Modules:
  0.0 92.2 jit_solution(16199467331725256495)
XLA Ops:
  0.6 0.8 copy.34
  1.6 0.5 fusion.9
  2.2 0.5 select_reduce_fusion
  2.8 0.7 dynamic_update_slice.3.refs_0_
  3.4 36.1 %shard_map.103 = (bf16[32,32,256]{2,1,0:T(8,128)(2,1)}, s32[32,8,128]{2,1,0:T(8,128)}) custom-call(s32[32,8,128]{2,1,0:T(8,128)} %dynamic_update_slice.3.refs_0_, bf16[512,256]{1,0:T(8,128)(2,1)} %bitcast.83), custom_call_target="tpu_custom_call" | custom-call | tf_op jit(solution)/shard_map/pallas_call | solution.py:84
  39.6 2.9 %convolution_bitcast_fusion = f32[128,8,768]{2,1,0:T(8,128)S(1)} fusion(bf16[256,768]{1,0:T(8,128)(2,1)S(1)} %copy-done, bf16[1024,256]{1,0:T(8,128)(2,1)} %bitcast.90, s32[1024]{0:T(1024)S(1)} %fusion.141), kind=kOutput, calls=%fused_computation.11 | convolution fusion | flops 940834816 | bytes 4067328 | tf_op jit(solution)/shard_map/dot_general | solution.py:221
  42.5 2.1 %fusion.155 = (f32[128,1,768]{2,1,0:T(1,128)S(1)}, f32[128,1,768]{2,1,0:T(1,128)S(1)}, f32[128,1,768]{2,1,0:T(1,128)S(1)}, f32[128,1,768]{2,1,0:T(1,128)S(1)}, f...) fusion(f32[128,8,768]{2,1,0:T(8,128)S(1)} %convolution_bitcast_, ...), kind=kLoop, calls=%fused_computation.218 | loop fusion | bytes 6291456 | tf_op jit(solution)/shard_map/slice | solution.py:227
  44.8 0.2 fusion.119
  45.1 0.2 fusion.135
  45.4 0.2 fusion.133
  45.9 0.2 fusion.131
  46.2 0.2 fusion.129
  46.6 0.2 fusion.127
  46.9 0.2 fusion.125
  47.4 0.2 fusion.123
  47.7 1.8 %fusion.7 = bf16[1024,256]{1,0:T(8,128)(2,1)} fusion(s32[1024]{0:T(1024)S(1)} %fusion.141, bf16[128,8,256]{2,0,1:T(8,128)(2,1)S(1)} %get-tuple-element.11), kind=kOutput, calls=%fused_computation.13 | convolution fusion | flops 538181632 | bytes 1052672 | tf_op jit(solution)/shard_map/dot_general | solution.py:232
  49.7 0.2 fusion.117
  49.8 0.7 copy.70
  50.6 0.9 %slice_reduce_fusion = s32[32,32]{1,0:T(8,128)S(1)} fusion(s32[32,8,128]{2,1,0:T(8,128)} %get-tuple-element.8), kind=kLoop, calls=%fused_computation.187 | loop fusion | bytes 8192 | tf_op jit(solution)/shard_map/slice | solution.py:235
  51.6 1.3 %fusion.5.refs_2_ = bf16[512,1024]{1,0:T(8,128)(2,1)} fusion(s32[1024]{0:T(1024)S(1)} %eq.60), kind=kLoop, calls=%fused_computation.10 | loop fusion | flops 1048576 | bytes 1052672 | tf_op jit(solution)/shard_map/convert_element_type | solution.py:236
  52.9 1.5 %fusion.146.refs_4_ = f32[512,768]{1,0:T(8,128)} fusion(bf16[256,768]{1,0:T(8,128)(2,1)S(1)} %copy-done.3, bf16[1,512,256]{2,1,0:T(8,128)(2,1)S(1)} %copy-done.2), kind=kOutput, calls=%fused_computation.216 | convolution fusion | flops 201326592 | bytes 2228224 | tf_op jit(solution)/shard_map/dot_general | solution.py:217
  54.5 34.8 %shard_map.104 = (bf16[512,256]{1,0:T(8,128)(2,1)}, f32[4,256]{1,0:T(4,128)}) custom-call(bf16[32,32,256]{2,1,0:T(8,128)(2,1)} %bitcast.85, f32[32,4,256]{2,1,0:T(4,128)} %bitcast.86, bf16[512,1024]{1,0:T(8,128)(2,1)} %fusion.5.refs_2_, bf16[256,768]{1,0:T(8,128)(2,1)} %refs_3_.1, f32[512,768]{1,0:T(8,128)} %fusion.146.refs_4_, bf16[512,256]{1,0:T(8,128)(2,1)} %bitcast.84), custom_call_target="tpu_custom_call" | custom-call | tf_op jit(solution)/shard_map/pallas_call | solution.py:166
  89.3 1.7 %copy.80 = bf16[1,512,256]{2,1,0:T(8,128)(2,1)} copy(bf16[1,512,256]{2,1,0:T(8,128)(2,1)} %bitcast.87) | data formatting | bytes 524288
  90.9 1.3 %copy.81 = f32[4,256]{1,0:T(4,128)} copy(f32[4,256]{1,0:T(4,128)} %get-tuple-element.58) | data formatting | bytes 8192
  (37 shorter events, 1.6 us)
Async XLA Ops:
  0.6 39.0 %copy-start = (bf16[256,768]{1,0:T(8,128)(2,1)S(1)}, bf16[256,768]{1,0:T(8,128)(2,1)}, u32[]{:S(2)}) copy-start(bf16[256,768]{1,0:T(8,128)(2,1)} %param.11) | copy-start | bytes 1179652
  42.4 2.3 %copy-start.7 = (s32[128,8]{0,1:T(8,128)S(1)}, s32[128,8]{0,1:T(8,128)}, u32[]{:S(2)}) copy-start(s32[128,8]{0,1:T(8,128)} %param.10) | copy-start | bytes 12292
  42.5 2.3 %copy-start.1 = (bf16[256,768]{1,0:T(8,128)(2,1)S(1)}, bf16[256,768]{1,0:T(8,128)(2,1)}, u32[]{:S(2)}) copy-start(bf16[256,768]{1,0:T(8,128)(2,1)} %param.12) | copy-start | bytes 1179652
  42.5 2.3 %copy-start.5 = (bf16[1,128,256]{2,1,0:T(8,128)(2,1)S(1)}, bf16[1,128,256]{2,1,0:T(8,128)(2,1)}, u32[]{:S(2)}) copy-start(bf16[1,128,256]{2,1,0:T(8,128)(2,1)} %param.9) | copy-start | bytes 196612
  47.2 2.3 %copy-start.6 = (bf16[1,128,128]{2,1,0:T(8,128)(2,1)S(1)}, bf16[1,128,128]{2,1,0:T(8,128)(2,1)}, u32[]{:S(2)}) copy-start(bf16[1,128,128]{2,1,0:T(8,128)(2,1)} %param.15) | copy-start | bytes 98308
  47.6 5.3 %copy-start.2 = (bf16[1,512,256]{2,1,0:T(8,128)(2,1)S(1)}, bf16[1,512,256]{2,1,0:T(8,128)(2,1)}, u32[]{:S(2)}) copy-start(bf16[1,512,256]{2,1,0:T(8,128)(2,1)} %param.8) | copy-start | bytes 786436
  47.6 5.3 %copy-start.3 = (bf16[256,768]{1,0:T(8,128)(2,1)S(1)}, bf16[256,768]{1,0:T(8,128)(2,1)}, u32[]{:S(2)}) copy-start(bf16[256,768]{1,0:T(8,128)(2,1)} %param.14) | copy-start | bytes 1179652
  47.7 6.7 %copy-start.4 = (bf16[128,256]{1,0:T(8,128)(2,1)}, bf16[128,256]{1,0:T(8,128)(2,1)S(1)}, u32[]{:S(2)}) copy-start(bf16[128,256]{1,0:T(8,128)(2,1)S(1)} %get-tuple-element.12) | copy-start | bytes 196612

commit v6 on v4

--- a/solution.py
+++ b/solution.py
@@ -107,7 +107,6 @@
     p = lax.axis_index("path")
     _greet(pltpu.get_barrier_semaphore(), g, p, n_grp, n_path, True)
     start_msg, finish_msg = _ring_copies(out_ref, inbuf, msend, mrecv, g, p, n_path, 1)
-    lax.fori_loop(1, n_path, start_msg, 0)
 
     def path_copy(k, q):
         return pltpu.make_async_remote_copy(
@@ -125,6 +124,7 @@
         return c
 
     lax.fori_loop(1, n_path, start1, 0)
+    lax.fori_loop(1, n_path, start_msg, 0)
     inbuf[0] = out_ref[0]
     lax.fori_loop(1, n_path, finish1, 0)
     mid[...] = term_ref[p] + jnp.sum(recv1[...], axis=0)

time: 90.2 us -> 83.7 us (0.928)
  the two profiles are of different devices: /device:TPU:1 before, /device:TPU:6 now
where the time goes in v6:
time: 83.7 us; the launch traced here: 83.2 us
  Pallas kernels  63.4 us (76%)
  matrix products  9.74 us (12%)
  local copies, waits for them, and re-layouts  6.59 us (8%)
  other arithmetic  2.57 us (3%)
  between operations  0.98 us (1%)
    pallas_call x1, Pallas kernels, fetch_rows(): pl.pallas_call(lambda *refs: _fetch_kernel(n_grp, n_path, *refs), out_sha...  34.8 us
    pallas_call x1, Pallas kernels, exchange_messages(): pl.pallas_call(lambda *refs: _message_kernel(n_grp, n_path, *refs), out_s...  28.5 us
    dot_general x1, matrix products, shards(): projected = jnp.dot(fetched, w_path_in, preferred_element_type=f32)  2.86 us
    dot_general x1, matrix products, shards(): jnp.dot(link_sum.astype(bf16), w_link_in, preferred_element_type=f32)  2.31 us
    slice x1, local copies, waits for them, and re-layouts, shards(): renewed = gated_update(projected[:, hop_index], carried, w_path_hid)  2.14 us
    dot_general x9, matrix products, gated_update(): jnp.dot(carried.astype(jnp.bfloat16), w_hidden, preferred_element_type=jn...  2.08 us
    dot_general x1, matrix products, shards(): jnp.dot(route.astype(bf16), flat_messages, preferred_element_type=f32)  1.8 us

profile of v6, /device:TPU:6, one launch (start us, length us, event | category | flops | bytes accessed | tf_op | source)
XLA Modules:
  0.0 83.2 jit_solution(418812622415618962)
XLA Ops:
  0.6 0.8 %copy.34 = s32[128,8]{1,0:T(8,128)S(1)} copy(s32[128,8]{0,1:T(8,128)} %param.10) | data formatting | bytes 8192 | tf_op args[2]
  1.6 0.5 fusion.11
  2.2 0.5 select_reduce_fusion
  2.8 0.7 dynamic_update_slice.3.refs_0_
  3.4 34.8 %shard_map.103 = (bf16[32,32,256]{2,1,0:T(8,128)(2,1)}, s32[32,8,128]{2,1,0:T(8,128)}) custom-call(s32[32,8,128]{2,1,0:T(8,128)} %dynamic_update_slice.3.refs_0_, bf16[512,256]{1,0:T(8,128)(2,1)} %bitcast.88), custom_call_target="tpu_custom_call" | custom-call | tf_op jit(solution)/shard_map/pallas_call | solution.py:84
  38.3 2.9 %convolution_bitcast_fusion = f32[128,8,768]{2,1,0:T(8,128)S(1)} fusion(bf16[256,768]{1,0:T(8,128)(2,1)S(1)} %copy-done, bf16[1024,256]{1,0:T(8,128)(2,1)} %bitcast.94, s32[1024]{0:T(1024)S(1)} %fusion.159), kind=kOutput, calls=%fused_computation.11 | convolution fusion | flops 940834816 | bytes 4067328 | tf_op jit(solution)/shard_map/dot_general | solution.py:211
  41.2 2.1 %fusion.173 = (f32[128,1,768]{2,1,0:T(1,128)S(1)}, f32[128,1,768]{2,1,0:T(1,128)S(1)}, f32[128,1,768]{2,1,0:T(1,128)S(1)}, f32[128,1,768]{2,1,0:T(1,128)S(1)}, f...) fusion(f32[128,8,768]{2,1,0:T(8,128)S(1)} %convolution_bitcast_, ...), kind=kLoop, calls=%fused_computation.238 | loop fusion | bytes 6291456 | tf_op jit(solution)/shard_map/slice | solution.py:217
  43.4 0.2 fusion.137
  43.8 0.2 fusion.153
  44.1 0.2 fusion.151
  44.5 0.2 fusion.149
  44.9 0.2 fusion.147
  45.3 0.2 fusion.145
  45.6 0.2 fusion.143
  46.1 0.2 fusion.141
  46.4 1.8 %fusion.7 = bf16[1024,256]{1,0:T(8,128)(2,1)} fusion(s32[1024]{0:T(1024)S(1)} %fusion.159, bf16[128,8,256]{2,0,1:T(8,128)(2,1)S(1)} %get-tuple-element.11), kind=kOutput, calls=%fused_computation.13 | convolution fusion | flops 538181632 | bytes 1052672 | tf_op jit(solution)/shard_map/dot_general | solution.py:222
  48.3 0.2 fusion.135
  48.5 0.7 copy.70
  49.3 28.5 %shard_map.104 = (bf16[32,32,256]{2,1,0:T(8,128)(2,1)}, f32[4,256]{1,0:T(4,128)}) custom-call(bf16[32,32,256]{2,1,0:T(8,128)(2,1)} %bitcast.90, f32[32,4,256]{2,1,0:T(4,128)} %bitcast.91), custom_call_target="tpu_custom_call" | custom-call | tf_op jit(solution)/shard_map/pallas_call | solution.py:157
  77.8 0.9 %slice_reduce_fusion = s32[32,32]{1,0:T(8,128)S(1)} fusion(s32[32,8,128]{2,1,0:T(8,128)} %get-tuple-element.7), kind=kLoop, calls=%fused_computation.207 | loop fusion | bytes 8192 | tf_op jit(solution)/shard_map/slice | solution.py:227
  78.8 2.3 %fusion.9 = f32[512,768]{1,0:T(8,128)S(1)} fusion(bf16[256,768]{1,0:T(8,128)(2,1)S(1)} %copy-done.3, bf16[1024,256]{1,0:T(8,128)(2,1)} %bitcast.89, s32[1024]{0:T(1024)S(1)} %eq.29), kind=kOutput, calls=%fused_computation.15 | convolution fusion | flops 470417408 | bytes 2494464 | tf_op jit(solution)/shard_map/dot_general | solution.py:232
  81.2 0.4 fusion.164
  81.6 1.1 %fusion.29 = bf16[1,512,256]{2,1,0:T(8,128)(2,1)} fusion(f32[512,768]{1,0:T(8,128)S(1)} %fusion.164, f32[512,768]{1,0:T(8,128)S(1)} %fusion.9, bf16[1,512,256]{2,1,0:T(8,128)(2,1)S(1)} %copy-done.2), kind=kLoop, calls=%fused_computation.45 | loop fusion | flops 2097152 | bytes 3670016 | tf_op jit(solution)/shard_map/broadcast_in_dim | solution.py:234
  82.6 0.6 copy.79
  (41 shorter events, 1.6 us)
Async XLA Ops:
  0.6 37.6 %copy-start = (bf16[256,768]{1,0:T(8,128)(2,1)S(1)}, bf16[256,768]{1,0:T(8,128)(2,1)}, u32[]{:S(2)}) copy-start(bf16[256,768]{1,0:T(8,128)(2,1)} %param.11) | copy-start | bytes 1179652
  41.1 2.3 %copy-start.8 = (s32[128,8]{0,1:T(8,128)S(1)}, s32[128,8]{0,1:T(8,128)}, u32[]{:S(2)}) copy-start(s32[128,8]{0,1:T(8,128)} %param.10) | copy-start | bytes 12292
  41.1 2.3 %copy-start.1 = (bf16[256,768]{1,0:T(8,128)(2,1)S(1)}, bf16[256,768]{1,0:T(8,128)(2,1)}, u32[]{:S(2)}) copy-start(bf16[256,768]{1,0:T(8,128)(2,1)} %param.12) | copy-start | bytes 1179652
  41.1 2.3 %copy-start.6 = (bf16[1,128,256]{2,1,0:T(8,128)(2,1)S(1)}, bf16[1,128,256]{2,1,0:T(8,128)(2,1)}, u32[]{:S(2)}) copy-start(bf16[1,128,256]{2,1,0:T(8,128)(2,1)} %param.9) | copy-start | bytes 196612
  45.9 2.3 %copy-start.7 = (bf16[1,128,128]{2,1,0:T(8,128)(2,1)S(1)}, bf16[1,128,128]{2,1,0:T(8,128)(2,1)}, u32[]{:S(2)}) copy-start(bf16[1,128,128]{2,1,0:T(8,128)(2,1)} %param.15) | copy-start | bytes 98308
  46.0 32.8 %copy-start.3 = (bf16[256,768]{1,0:T(8,128)(2,1)S(1)}, bf16[256,768]{1,0:T(8,128)(2,1)}, u32[]{:S(2)}) copy-start(bf16[256,768]{1,0:T(8,128)(2,1)} %param.13) | copy-start | bytes 1179652
  46.4 34.8 %copy-start.5 = (bf16[128,256]{1,0:T(8,128)(2,1)}, bf16[128,256]{1,0:T(8,128)(2,1)S(1)}, u32[]{:S(2)}) copy-start(bf16[128,256]{1,0:T(8,128)(2,1)S(1)} %get-tuple-element.12) | copy-start | bytes 196612
  46.4 34.8 %copy-start.2 = (bf16[1,512,256]{2,1,0:T(8,128)(2,1)S(1)}, bf16[1,512,256]{2,1,0:T(8,128)(2,1)}, u32[]{:S(2)}) copy-start(bf16[1,512,256]{2,1,0:T(8,128)(2,1)} %param.8) | copy-start | bytes 786436
  46.4 34.8 %copy-start.4 = (bf16[256,768]{1,0:T(8,128)(2,1)S(1)}, bf16[256,768]{1,0:T(8,128)(2,1)}, u32[]{:S(2)}) copy-start(bf16[256,768]{1,0:T(8,128)(2,1)} %param.14) | copy-start | bytes 1179652
  81.2 1.5 %copy-start.9 = (f32[4,256]{1,0:T(4,128)S(1)}, f32[4,256]{1,0:T(4,128)}, u32[]{:S(2)}) copy-start(f32[4,256]{1,0:T(4,128)} %get-tuple-element.58) | copy-start | bytes 12292

commit v7 on v6

--- a/solution.py
+++ b/solution.py
@@ -174,6 +174,42 @@
         ],
         compiler_params=pltpu.CompilerParams(collective_id=1, has_side_effects=True),
     )(outgoing, term)
+
+
+def _hop_kernel(hops, route_t_ref, got_ref, w_in_ref, w_hid_ref, state_ref, live_ref, route_ref, cot_t_ref,
+                final_ref, out_ref, term_ref, proj, msgs):
+    bf16, f32 = jnp.bfloat16, jnp.float32
+    fetched = jnp.dot(route_t_ref[...], got_ref[...], preferred_element_type=f32).astype(bf16)
+    proj[...] = jnp.dot(fetched, w_in_ref[...], preferred_element_type=f32)
+    carried = state_ref[...].astype(f32)
+    n, width = carried.shape
+    for h in range(hops):
+        p_h = proj[h * n : (h + 1) * n, :]
+        renewed = gated_update(p_h, carried, w_hid_ref[...])
+        carried = jnp.where(live_ref[:, h : h + 1] > 0, renewed, carried)
+        msgs[h * n : (h + 1) * n, :] = carried.astype(bf16)
+    final = carried.astype(bf16)
+    final_ref[...] = final
+    out_ref[...] = jnp.dot(route_ref[...], msgs[...], preferred_element_type=f32).astype(bf16)
+    term_ref[...] = jnp.dot(cot_t_ref[...], final, preferred_element_type=f32)
+
+
+def run_hops(route_t, got, w_path_in, w_path_hid, state, live, route, cot_t):
+    entries, slots = route_t.shape
+    n, width = state.shape
+    hops = entries // n
+    return pl.pallas_call(
+        lambda *refs: _hop_kernel(hops, *refs),
+        out_shape=(jax.ShapeDtypeStruct((n, width), jnp.bfloat16),
+                   jax.ShapeDtypeStruct((slots, width), jnp.bfloat16),
+                   jax.ShapeDtypeStruct((cot_t.shape[0], width), jnp.float32)),
+        in_specs=[pl.BlockSpec(memory_space=pltpu.VMEM)] * 8,
+        out_specs=(pl.BlockSpec(memory_space=pltpu.VMEM),) * 3,
+        scratch_shapes=[
+            pltpu.VMEM((entries, w_path_in.shape[1]), jnp.float32),
+            pltpu.VMEM((entries, width), jnp.bfloat16),
+        ],
+    )(route_t, got, w_path_in, w_path_hid, state, live, route, cot_t)
 
 
 def shards(
@@ -200,28 +236,21 @@
     slot_id = jnp.sum(before * marks.astype(f32), axis=1).astype(jnp.int32)
     offset = lax.rem(owner_id - me + peer_count, peer_count)
     dest = jnp.where(is_live, offset * capacity + slot_id, -1)
+    dest = dest.reshape(path_count, hop_count).T.reshape(-1)
+    local_id = local_id.reshape(path_count, hop_count).T.reshape(-1)
     slot_ids = jnp.arange(slots)
     route = dest[None, :] == slot_ids[:, None]
     requests = jnp.sum(jnp.where(route, local_id[None, :] + 1, 0), axis=1) - 1
     req = jnp.full((peer_count, 8, 128), -1, jnp.int32)
     req = lax.dynamic_update_slice(req, requests.reshape(peer_count, 1, capacity), (0, 0, 0))
+    route_t = (dest[:, None] == slot_ids[None, :]).astype(bf16)
+    live_grid = is_live.reshape(path_count, hop_count).astype(jnp.int32)
+    cot_t = cotangent[0].T
     got, req_ids = fetch_rows(req, own_links, capacity, n_grp, peer_count)
-    route_t = (dest[:, None] == slot_ids[None, :]).astype(bf16)
-    fetched = jnp.dot(route_t, got.reshape(slots, width), preferred_element_type=f32).astype(bf16)
-    projected = jnp.dot(fetched, w_path_in, preferred_element_type=f32)
-    projected = projected.reshape(path_count, hop_count, 3 * width)
-    live_grid = is_live.reshape(path_count, hop_count)
-    carried = path_state[0].astype(f32)
-    messages = []
-    for hop_index in range(hop_count):
-        renewed = gated_update(projected[:, hop_index], carried, w_path_hid)
-        carried = jnp.where(live_grid[:, hop_index, None], renewed, carried)
-        messages.append(carried.astype(bf16))
-    path_final = carried.astype(bf16)
-    flat_messages = jnp.stack(messages, axis=1).reshape(-1, width)
-    outgoing = jnp.dot(route.astype(bf16), flat_messages, preferred_element_type=f32).astype(bf16)
-    cot = cotangent[0].reshape(path_count, peer_count, -1)
-    term = lax.dot_general(cot, path_final, (((0,), (0,)), ((), ())), preferred_element_type=f32)
+    path_final, outgoing, term = run_hops(
+        route_t, got.reshape(slots, width), w_path_in, w_path_hid, path_state[0], live_grid,
+        route.astype(bf16), cot_t)
+    term = term.reshape(peer_count, -1, width)
     incoming, read_grad = exchange_messages(
         outgoing.reshape(peer_count, capacity, width), term, n_grp, peer_count)
     received = req_ids[:, 0, :capacity].reshape(-1)

time: 83.7 us -> 86.1 us (1.029)
  Pallas kernels: 63.4 us -> 70.8 us
  matrix products: 9.74 us -> 3.21 us
  other arithmetic: 2.57 us -> 4.98 us
    pallas_call x0 -> x1, Pallas kernels: none -> 7.48 us  [run_hops(): pl.pallas_call(lambda *refs: _hop_kernel(hops, *refs), out_shape=(jax.Sha...]
    dot_general x3 -> x0, matrix products: 4.81 us -> none  [the longest x1 2.86 us: shards(): projected = jnp.dot(fetched, w_path_in, preferred_element_type=f32)]
    convert_element_type x0 -> x3, other arithmetic: none -> 3.26 us  [the longest x1 2.64 us: shards(): route.astype(bf16)]
    slice x1 -> x0, local copies, waits for them, and re-layouts: 2.14 us -> none  [shards(): renewed = gated_update(projected[:, hop_index], carried, w_path_hid)]
    dot_general x9 -> x1, matrix products: 2.08 us -> 0.37 us  [gated_update(): jnp.dot(carried.astype(jnp.bfloat16), w_hidden, preferred_element_type=jn...]
    reshape x0 -> x1, local copies, waits for them, and re-layouts: none -> 1.66 us  [shards(): term = term.reshape(peer_count, -1, width)]
    unnamed x23 -> x13, local copies, waits for them, and re-layouts: 1.61 us -> 2.17 us
where the time goes in v7:
time: 86.1 us; the launch traced here: 85.6 us
  Pallas kernels  70.8 us (82%)
  local copies, waits for them, and re-layouts  5.89 us (7%)
  other arithmetic  4.98 us (6%)
  matrix products  3.21 us (4%)
    pallas_call x1, Pallas kernels, fetch_rows(): pl.pallas_call(lambda *refs: _fetch_kernel(n_grp, n_path, *refs), out_sha...  34.8 us
    pallas_call x1, Pallas kernels, exchange_messages(): pl.pallas_call(lambda *refs: _message_kernel(n_grp, n_path, *refs), out_s...  28.5 us
    pallas_call x1, Pallas kernels, run_hops(): pl.pallas_call(lambda *refs: _hop_kernel(hops, *refs), out_shape=(jax.Sha...  7.48 us
    convert_element_type x1, other arithmetic, shards(): route.astype(bf16)  2.64 us
    dot_general x1, matrix products, shards(): jnp.dot(link_sum.astype(bf16), w_link_in, preferred_element_type=f32)  2.31 us
    unnamed x13, local copies, waits for them, and re-layouts  2.17 us

profile of v7, /device:TPU:6, one launch (start us, length us, event | category | flops | bytes accessed | tf_op | source)
XLA Modules:
  0.0 85.6 jit_solution(12125538912005095606)
XLA Ops:
  0.6 0.0 copy-start
  0.6 0.8 copy.17
  1.5 0.1 reshape.84
  1.6 0.5 fusion.7
  2.1 0.1 convert_element_type.37
  2.2 0.1 fusion.34
  2.4 0.1 copy.24
  2.5 0.5 select_reduce_fusion
  3.0 0.1 sub.29
  3.1 0.7 dynamic_update_slice.3.refs_0_
  3.8 34.8 %shard_map.103 = (bf16[32,32,256]{2,1,0:T(8,128)(2,1)}, s32[32,8,128]{2,1,0:T(8,128)}) custom-call(s32[32,8,128]{2,1,0:T(8,128)} %dynamic_update_slice.3.refs_0_, bf16[512,256]{1,0:T(8,128)(2,1)} %bitcast.23), custom_call_target="tpu_custom_call" | custom-call | tf_op jit(solution)/shard_map/pallas_call | solution.py:84
  38.6 0.0 copy-start.3
  38.6 2.6 %fusion = (bf16[1024,1024]{1,0:T(8,128)(2,1)}, bf16[1024,1024]{1,0:T(8,128)(2,1)}) fusion(s32[1024]{0:T(1024)S(1)} %bitcast.30), kind=kLoop, calls=%fused_computation.3 | loop fusion | flops 4194304 | bytes 4198400 | tf_op jit(solution)/shard_map/convert_element_type | solution.py:252
  41.2 0.6 fusion.39.refs_5_
  41.9 0.7 copy.25
  42.6 7.5 %shard_map.104 = (bf16[128,256]{1,0:T(8,128)(2,1)}, bf16[1024,256]{1,0:T(8,128)(2,1)}, f32[128,256]{1,0:T(8,128)}) custom-call(bf16[1024,1024]{1,0:T(8,128)(2,1)} %get-tuple-element.20.refs_0_, bf16[1024,256]{1,0:T(8,128)(2,1)} %bitcast.26, bf16[256,768]{1,0:T(8,128)(2,1)} %refs_2_.1, bf16[256,768]{1,0:T(8,128)(2,1)} %refs_3_.1, bf16[128,256]{1,0:T(8,128)(2,1)} %bitcast.28, ...), custom_call_target="tpu_custom_call" | custom-call | tf_op jit(solution)/shard_map/pallas_call | solution.py:201
  50.0 1.7 %reshape.87.refs_1_ = f32[32,4,256]{2,1,0:T(4,128)} reshape(f32[128,256]{1,0:T(8,128)} %get-tuple-element.13) | data formatting | bytes 262144 | tf_op jit(solution)/shard_map/reshape | solution.py:253
  51.7 28.5 %shard_map.105 = (bf16[32,32,256]{2,1,0:T(8,128)(2,1)}, f32[4,256]{1,0:T(4,128)}) custom-call(bf16[32,32,256]{2,1,0:T(8,128)(2,1)} %bitcast.25, f32[32,4,256]{2,1,0:T(4,128)} %reshape.87.refs_1_), custom_call_target="tpu_custom_call" | custom-call | tf_op jit(solution)/shard_map/pallas_call | solution.py:157
  80.2 0.9 %slice_reduce_fusion = s32[32,32]{1,0:T(8,128)S(1)} fusion(s32[32,8,128]{2,1,0:T(8,128)} %get-tuple-element.10), kind=kLoop, calls=%fused_computation.57 | loop fusion | bytes 8192 | tf_op jit(solution)/shard_map/slice | solution.py:256
  81.2 0.1 eq.60
  81.3 2.3 %fusion.5 = f32[512,768]{1,0:T(8,128)S(1)} fusion(bf16[256,768]{1,0:T(8,128)(2,1)S(1)} %copy-done, bf16[1024,256]{1,0:T(8,128)(2,1)} %bitcast.24, s32[1024]{0:T(1024)S(1)} %eq.60), kind=kOutput, calls=%fused_computation.10 | convolution fusion | flops 470417408 | bytes 2494464 | tf_op jit(solution)/shard_map/dot_general | solution.py:261
  83.6 0.4 fusion.43
  84.0 1.1 %fusion.23 = bf16[1,512,256]{2,1,0:T(8,128)(2,1)} fusion(f32[512,768]{1,0:T(8,128)S(1)} %fusion.43, f32[512,768]{1,0:T(8,128)S(1)} %fusion.5, bf16[1,512,256]{2,1,0:T(8,128)(2,1)S(1)} %copy-done.1), kind=kLoop, calls=%fused_computation.30 | loop fusion | flops 2097152 | bytes 3670016 | tf_op jit(solution)/shard_map/broadcast_in_dim | solution.py:263
  85.0 0.6 copy.27
  (12 shorter events, 0.1 us)
Async XLA Ops:
  0.6 80.6 %copy-start = (bf16[256,768]{1,0:T(8,128)(2,1)S(1)}, bf16[256,768]{1,0:T(8,128)(2,1)}, u32[]{:S(2)}) copy-start(bf16[256,768]{1,0:T(8,128)(2,1)} %param.13) | copy-start | bytes 1179652
  38.6 3.3 %copy-start.3 = (bf16[1,128,128]{2,1,0:T(8,128)(2,1)S(1)}, bf16[1,128,128]{2,1,0:T(8,128)(2,1)}, u32[]{:S(2)}) copy-start(bf16[1,128,128]{2,1,0:T(8,128)(2,1)} %param.15) | copy-start | bytes 98308
  50.0 33.5 %copy-start.1 = (bf16[1,512,256]{2,1,0:T(8,128)(2,1)S(1)}, bf16[1,512,256]{2,1,0:T(8,128)(2,1)}, u32[]{:S(2)}) copy-start(bf16[1,512,256]{2,1,0:T(8,128)(2,1)} %param.8) | copy-start | bytes 786436
  50.0 33.5 %copy-start.2 = (bf16[256,768]{1,0:T(8,128)(2,1)S(1)}, bf16[256,768]{1,0:T(8,128)(2,1)}, u32[]{:S(2)}) copy-start(bf16[256,768]{1,0:T(8,128)(2,1)} %param.14) | copy-start | bytes 1179652
  84.0 1.1 %copy-start.4 = (f32[4,256]{1,0:T(4,128)S(1)}, f32[4,256]{1,0:T(4,128)}, u32[]{:S(2)}) copy-start(f32[4,256]{1,0:T(4,128)} %get-tuple-element.26) | copy-start | bytes 12292

commit v8 on v7

--- a/solution.py
+++ b/solution.py
@@ -176,10 +176,12 @@
     )(outgoing, term)
 
 
-def _hop_kernel(hops, route_t_ref, got_ref, w_in_ref, w_hid_ref, state_ref, live_ref, route_ref, cot_t_ref,
+def _hop_kernel(hops, dcol_ref, got_ref, w_in_ref, w_hid_ref, state_ref, live_ref, drow_ref, cot_t_ref,
                 final_ref, out_ref, term_ref, proj, msgs):
     bf16, f32 = jnp.bfloat16, jnp.float32
-    fetched = jnp.dot(route_t_ref[...], got_ref[...], preferred_element_type=f32).astype(bf16)
+    entries, slots = dcol_ref.shape[0], got_ref.shape[0]
+    route_t = (dcol_ref[:, 0:1] == lax.broadcasted_iota(jnp.int32, (1, slots), 1)).astype(bf16)
+    fetched = jnp.dot(route_t, got_ref[...], preferred_element_type=f32).astype(bf16)
     proj[...] = jnp.dot(fetched, w_in_ref[...], preferred_element_type=f32)
     carried = state_ref[...].astype(f32)
     n, width = carried.shape
@@ -190,26 +192,31 @@
         msgs[h * n : (h + 1) * n, :] = carried.astype(bf16)
     final = carried.astype(bf16)
     final_ref[...] = final
-    out_ref[...] = jnp.dot(route_ref[...], msgs[...], preferred_element_type=f32).astype(bf16)
-    term_ref[...] = jnp.dot(cot_t_ref[...], final, preferred_element_type=f32)
-
-
-def run_hops(route_t, got, w_path_in, w_path_hid, state, live, route, cot_t):
-    entries, slots = route_t.shape
+    route = (lax.broadcasted_iota(jnp.int32, (slots, 1), 0) == drow_ref[...]).astype(bf16)
+    out_ref[...] = jnp.dot(route, msgs[...], preferred_element_type=f32).astype(bf16)
+    term = jnp.dot(cot_t_ref[...], final, preferred_element_type=f32)
+    share = term_ref.shape[1]
+    for q in range(term_ref.shape[0]):
+        term_ref[q] = term[q * share : (q + 1) * share, :]
+
+
+def run_hops(dcol, got, w_path_in, w_path_hid, state, live, drow, cot_t, n_path):
+    entries = dcol.shape[0]
+    slots = got.shape[0]
     n, width = state.shape
     hops = entries // n
     return pl.pallas_call(
         lambda *refs: _hop_kernel(hops, *refs),
         out_shape=(jax.ShapeDtypeStruct((n, width), jnp.bfloat16),
                    jax.ShapeDtypeStruct((slots, width), jnp.bfloat16),
-                   jax.ShapeDtypeStruct((cot_t.shape[0], width), jnp.float32)),
+                   jax.ShapeDtypeStruct((n_path, cot_t.shape[0] // n_path, width), jnp.float32)),
         in_specs=[pl.BlockSpec(memory_space=pltpu.VMEM)] * 8,
         out_specs=(pl.BlockSpec(memory_space=pltpu.VMEM),) * 3,
         scratch_shapes=[
             pltpu.VMEM((entries, w_path_in.shape[1]), jnp.float32),
             pltpu.VMEM((entries, width), jnp.bfloat16),
         ],
-    )(route_t, got, w_path_in, w_path_hid, state, live, route, cot_t)
+    )(dcol, got, w_path_in, w_path_hid, state, live, drow, cot_t)
 
 
 def shards(
@@ -243,14 +250,13 @@
     requests = jnp.sum(jnp.where(route, local_id[None, :] + 1, 0), axis=1) - 1
     req = jnp.full((peer_count, 8, 128), -1, jnp.int32)
     req = lax.dynamic_update_slice(req, requests.reshape(peer_count, 1, capacity), (0, 0, 0))
-    route_t = (dest[:, None] == slot_ids[None, :]).astype(bf16)
     live_grid = is_live.reshape(path_count, hop_count).astype(jnp.int32)
     cot_t = cotangent[0].T
     got, req_ids = fetch_rows(req, own_links, capacity, n_grp, peer_count)
+    dcol = jnp.broadcast_to(dest[:, None], (entries, 128))
     path_final, outgoing, term = run_hops(
-        route_t, got.reshape(slots, width), w_path_in, w_path_hid, path_state[0], live_grid,
-        route.astype(bf16), cot_t)
-    term = term.reshape(peer_count, -1, width)
+        dcol, got.reshape(slots, width), w_path_in, w_path_hid, path_state[0], live_grid,
+        dest[None, :], cot_t, peer_count)
     incoming, read_grad = exchange_messages(
         outgoing.reshape(peer_count, capacity, width), term, n_grp, peer_count)
     received = req_ids[:, 0, :capacity].reshape(-1)

time: 86.1 us -> 82.6 us (0.959)
  other arithmetic: 4.98 us -> 2.35 us
  Pallas kernels: 70.8 us -> 69.8 us
    convert_element_type x1 -> x0, other arithmetic: 2.64 us -> none  [shards(): route.astype(bf16)]
    reshape x1 -> x0, local copies, waits for them, and re-layouts: 1.66 us -> none  [shards(): term = term.reshape(peer_count, -1, width)]
    pallas_call x1, Pallas kernels: 7.48 us -> 6.3 us  [run_hops(): pl.pallas_call(lambda *refs: _hop_kernel(hops, *refs), out_shape=(jax.Sha...]
    broadcast_in_dim x0 -> x1, local copies, waits for them, and re-layouts: none -> 0.98 us  [shards(): dcol = jnp.broadcast_to(dest[:, None], (entries, 128))]
where the time goes in v8:
time: 82.6 us; the launch traced here: 82.1 us
  Pallas kernels  69.8 us (85%)
  local copies, waits for them, and re-layouts  5.97 us (7%)
  matrix products  3.21 us (4%)
  other arithmetic  2.35 us (3%)
    pallas_call x1, Pallas kernels, fetch_rows(): pl.pallas_call(lambda *refs: _fetch_kernel(n_grp, n_path, *refs), out_sha...  34.8 us
    pallas_call x1, Pallas kernels, exchange_messages(): pl.pallas_call(lambda *refs: _message_kernel(n_grp, n_path, *refs), out_s...  28.7 us
    pallas_call x1, Pallas kernels, run_hops(): pl.pallas_call(lambda *refs: _hop_kernel(hops, *refs), out_shape=(jax.Sha...  6.3 us
    unnamed x13, local copies, waits for them, and re-layouts  2.93 us
    dot_general x1, matrix products, shards(): jnp.dot(link_sum.astype(bf16), w_link_in, preferred_element_type=f32)  2.31 us

profile of v8, /device:TPU:6, one launch (start us, length us, event | category | flops | bytes accessed | tf_op | source)
XLA Modules:
  0.0 82.1 jit_solution(18083024314333046830)
XLA Ops:
  0.6 0.0 copy-start
  0.6 1.5 %copy.37 = bf16[1,128,128]{1,2,0:T(8,128)(2,1)} copy(bf16[1,128,128]{2,1,0:T(8,128)(2,1)} %param.15) | data formatting | bytes 65536 | tf_op args[7]
  2.2 0.8 copy.28
  3.0 0.1 reshape.81
  3.1 0.5 fusion.5
  3.6 0.1 convert_element_type.31
  3.7 0.1 fusion.32
  3.8 0.6 fusion.37.refs_5_
  4.5 0.1 copy.34
  4.6 0.5 select_reduce_fusion
  5.1 0.1 sub.29
  5.2 0.7 dynamic_update_slice.3.refs_0_
  5.9 1.0 %broadcast_in_dim.42.refs_0_ = s32[1024,128]{1,0:T(8,128)} broadcast(s32[1024]{0:T(1024)S(1)} %bitcast.30), dimensions={0} | broadcast | bytes 528384 | tf_op jit(solution)/shard_map/broadcast_in_dim | solution.py:256
  6.8 34.8 %shard_map.103 = (bf16[32,32,256]{2,1,0:T(8,128)(2,1)}, s32[32,8,128]{2,1,0:T(8,128)}) custom-call(s32[32,8,128]{2,1,0:T(8,128)} %dynamic_update_slice.3.refs_0_, bf16[512,256]{1,0:T(8,128)(2,1)} %bitcast.24), custom_call_target="tpu_custom_call" | custom-call | tf_op jit(solution)/shard_map/pallas_call | solution.py:84
  41.7 0.9 %slice_reduce_fusion = s32[32,32]{1,0:T(8,128)S(1)} fusion(s32[32,8,128]{2,1,0:T(8,128)} %get-tuple-element.10), kind=kLoop, calls=%fused_computation.54 | loop fusion | bytes 8192 | tf_op jit(solution)/shard_map/slice | solution.py:262
  42.6 0.1 eq.49
  42.7 0.0 copy-done.3
  42.7 6.3 %shard_map.104 = (bf16[128,256]{1,0:T(8,128)(2,1)}, bf16[1024,256]{1,0:T(8,128)(2,1)}, f32[32,4,256]{2,1,0:T(4,128)}) custom-call(s32[1024,128]{1,0:T(8,128)} %broadcast_in_dim.42.refs_0_, bf16[1024,256]{1,0:T(8,128)(2,1)} %bitcast.27, bf16[256,768]{1,0:T(8,128)(2,1)} %refs_2_.1, bf16[256,768]{1,0:T(8,128)(2,1)} %refs_3_.1, bf16[128,256]{1,0:T(8,128)(2,1)} %bitcast.32, ...), custom_call_target="tpu_custom_call" | custom-call | tf_op jit(solution)/shard_map/pallas_call | solution.py:208
  49.0 28.7 %shard_map.105 = (bf16[32,32,256]{2,1,0:T(8,128)(2,1)}, f32[4,256]{1,0:T(4,128)}) custom-call(bf16[32,32,256]{2,1,0:T(8,128)(2,1)} %bitcast.26, f32[32,4,256]{2,1,0:T(4,128)} %get-tuple-element.13.refs_1_), custom_call_target="tpu_custom_call" | custom-call | tf_op jit(solution)/shard_map/pallas_call | solution.py:157
  77.7 0.0 copy-done
  77.7 2.3 %fusion.3 = f32[512,768]{1,0:T(8,128)S(1)} fusion(bf16[256,768]{1,0:T(8,128)(2,1)S(1)} %copy-done, bf16[1024,256]{1,0:T(8,128)(2,1)} %bitcast.25, s32[1024]{0:T(1024)S(1)} %eq.49), kind=kOutput, calls=%fused_computation.7 | convolution fusion | flops 470417408 | bytes 2494464 | tf_op jit(solution)/shard_map/dot_general | solution.py:267
  80.0 0.4 fusion.41
  80.4 1.1 %fusion.21 = bf16[1,512,256]{2,1,0:T(8,128)(2,1)} fusion(f32[512,768]{1,0:T(8,128)S(1)} %fusion.41, f32[512,768]{1,0:T(8,128)S(1)} %fusion.3, bf16[1,512,256]{2,1,0:T(8,128)(2,1)S(1)} %copy-done.1), kind=kLoop, calls=%fused_computation.27 | loop fusion | flops 2097152 | bytes 3670016 | tf_op jit(solution)/shard_map/broadcast_in_dim | solution.py:269
  81.5 0.6 copy.39
  (11 shorter events, 0.1 us)
Async XLA Ops:
  0.6 77.0 %copy-start = (bf16[256,768]{1,0:T(8,128)(2,1)S(1)}, bf16[256,768]{1,0:T(8,128)(2,1)}, u32[]{:S(2)}) copy-start(bf16[256,768]{1,0:T(8,128)(2,1)} %param.13) | copy-start | bytes 1179652
  4.6 38.1 %copy-start.3 = (s32[8,128]{1,0:T(8,128)}, s32[8,128]{1,0:T(8,128)S(1)}, u32[]{:S(2)}) copy-start(s32[8,128]{1,0:T(8,128)S(1)} %copy.34) | copy-start | bytes 12292
  49.0 31.0 %copy-start.1 = (bf16[1,512,256]{2,1,0:T(8,128)(2,1)S(1)}, bf16[1,512,256]{2,1,0:T(8,128)(2,1)}, u32[]{:S(2)}) copy-start(bf16[1,512,256]{2,1,0:T(8,128)(2,1)} %param.8) | copy-start | bytes 786436
  49.0 31.0 %copy-start.2 = (bf16[256,768]{1,0:T(8,128)(2,1)S(1)}, bf16[256,768]{1,0:T(8,128)(2,1)}, u32[]{:S(2)}) copy-start(bf16[256,768]{1,0:T(8,128)(2,1)} %param.14) | copy-start | bytes 1179652
  80.4 1.1 %copy-start.4 = (f32[4,256]{1,0:T(4,128)S(1)}, f32[4,256]{1,0:T(4,128)}, u32[]{:S(2)}) copy-start(f32[4,256]{1,0:T(4,128)} %get-tuple-element.24) | copy-start | bytes 12292

commit v9 on v8

--- a/solution.py
+++ b/solution.py
@@ -179,8 +179,9 @@
 def _hop_kernel(hops, dcol_ref, got_ref, w_in_ref, w_hid_ref, state_ref, live_ref, drow_ref, cot_t_ref,
                 final_ref, out_ref, term_ref, proj, msgs):
     bf16, f32 = jnp.bfloat16, jnp.float32
-    entries, slots = dcol_ref.shape[0], got_ref.shape[0]
-    route_t = (dcol_ref[:, 0:1] == lax.broadcasted_iota(jnp.int32, (1, slots), 1)).astype(bf16)
+    entries, slots = dcol_ref.shape[1], got_ref.shape[0]
+    dcol = jnp.transpose(dcol_ref[...])[:, 0:1]
+    route_t = (dcol == lax.broadcasted_iota(jnp.int32, (1, slots), 1)).astype(bf16)
     fetched = jnp.dot(route_t, got_ref[...], preferred_element_type=f32).astype(bf16)
     proj[...] = jnp.dot(fetched, w_in_ref[...], preferred_element_type=f32)
     carried = state_ref[...].astype(f32)
@@ -194,14 +195,15 @@
     final_ref[...] = final
     route = (lax.broadcasted_iota(jnp.int32, (slots, 1), 0) == drow_ref[...]).astype(bf16)
     out_ref[...] = jnp.dot(route, msgs[...], preferred_element_type=f32).astype(bf16)
-    term = jnp.dot(cot_t_ref[...], final, preferred_element_type=f32)
+    cot_t = jnp.transpose(cot_t_ref[...].astype(f32)).astype(bf16)
+    term = jnp.dot(cot_t, final, preferred_element_type=f32)
     share = term_ref.shape[1]
     for q in range(term_ref.shape[0]):
         term_ref[q] = term[q * share : (q + 1) * share, :]
 
 
 def run_hops(dcol, got, w_path_in, w_path_hid, state, live, drow, cot_t, n_path):
-    entries = dcol.shape[0]
+    entries = dcol.shape[1]
     slots = got.shape[0]
     n, width = state.shape
     hops = entries // n
@@ -209,7 +211,7 @@
         lambda *refs: _hop_kernel(hops, *refs),
         out_shape=(jax.ShapeDtypeStruct((n, width), jnp.bfloat16),
                    jax.ShapeDtypeStruct((slots, width), jnp.bfloat16),
-                   jax.ShapeDtypeStruct((n_path, cot_t.shape[0] // n_path, width), jnp.float32)),
+                   jax.ShapeDtypeStruct((n_path, cot_t.shape[1] // n_path, width), jnp.float32)),
         in_specs=[pl.BlockSpec(memory_space=pltpu.VMEM)] * 8,
         out_specs=(pl.BlockSpec(memory_space=pltpu.VMEM),) * 3,
         scratch_shapes=[
@@ -251,12 +253,11 @@
     req = jnp.full((peer_count, 8, 128), -1, jnp.int32)
     req = lax.dynamic_update_slice(req, requests.reshape(peer_count, 1, capacity), (0, 0, 0))
     live_grid = is_live.reshape(path_count, hop_count).astype(jnp.int32)
-    cot_t = cotangent[0].T
     got, req_ids = fetch_rows(req, own_links, capacity, n_grp, peer_count)
-    dcol = jnp.broadcast_to(dest[:, None], (entries, 128))
+    drow = jnp.broadcast_to(dest[None, :], (8, entries))
     path_final, outgoing, term = run_hops(
-        dcol, got.reshape(slots, width), w_path_in, w_path_hid, path_state[0], live_grid,
-        dest[None, :], cot_t, peer_count)
+        drow, got.reshape(slots, width), w_path_in, w_path_hid, path_state[0], live_grid,
+        drow[0:1], cotangent[0], peer_count)
     incoming, read_grad = exchange_messages(
         outgoing.reshape(peer_count, capacity, width), term, n_grp, peer_count)
     received = req_ids[:, 0, :capacity].reshape(-1)

time: 82.6 us -> 81 us (0.981)
  local copies, waits for them, and re-layouts: 5.97 us -> 4.12 us
    unnamed x13 -> x12, local copies, waits for them, and re-layouts: 2.93 us -> 1.45 us
where the time goes in v9:
time: 81 us; the launch traced here: 80.5 us
  Pallas kernels  70 us (86%)
  local copies, waits for them, and re-layouts  4.12 us (5%)
  matrix products  3.21 us (4%)
  other arithmetic  2.36 us (3%)
    pallas_call x1, Pallas kernels, fetch_rows(): pl.pallas_call(lambda *refs: _fetch_kernel(n_grp, n_path, *refs), out_sha...  34.8 us
    pallas_call x1, Pallas kernels, exchange_messages(): pl.pallas_call(lambda *refs: _message_kernel(n_grp, n_path, *refs), out_s...  28.7 us
    pallas_call x1, Pallas kernels, run_hops(): pl.pallas_call(lambda *refs: _hop_kernel(hops, *refs), out_shape=(jax.Sha...  6.51 us
    dot_general x1, matrix products, shards(): jnp.dot(link_sum.astype(bf16), w_link_in, preferred_element_type=f32)  2.31 us

profile of v9, /device:TPU:6, one launch (start us, length us, event | category | flops | bytes accessed | tf_op | source)
XLA Modules:
  0.0 80.5 jit_solution(4344352186076155106)
XLA Ops:
  0.6 0.0 copy-start
  0.6 0.8 %copy.26 = s32[128,8]{1,0:T(8,128)S(1)} copy(s32[128,8]{0,1:T(8,128)} %param.10) | data formatting | bytes 8192 | tf_op args[2]
  1.5 0.1 reshape.82
  1.6 0.5 fusion.5
  2.1 0.1 convert_element_type.31
  2.2 0.1 fusion.32
  2.3 0.6 fusion.37.refs_5_
  3.0 0.1 copy.32
  3.1 0.5 select_reduce_fusion
  3.6 0.1 sub.29
  3.7 0.6 broadcast_in_dim.42.refs_0_
  4.3 0.7 dynamic_update_slice.3.refs_0_
  5.0 34.8 %shard_map.103 = (bf16[32,32,256]{2,1,0:T(8,128)(2,1)}, s32[32,8,128]{2,1,0:T(8,128)}) custom-call(s32[32,8,128]{2,1,0:T(8,128)} %dynamic_update_slice.3.refs_0_, bf16[512,256]{1,0:T(8,128)(2,1)} %bitcast.22), custom_call_target="tpu_custom_call" | custom-call | tf_op jit(solution)/shard_map/pallas_call | solution.py:84
  39.8 0.9 %slice_reduce_fusion = s32[32,32]{1,0:T(8,128)S(1)} fusion(s32[32,8,128]{2,1,0:T(8,128)} %get-tuple-element.10), kind=kLoop, calls=%fused_computation.54 | loop fusion | bytes 8192 | tf_op jit(solution)/shard_map/slice | solution.py:263
  40.8 0.1 eq.49
  40.9 0.0 copy-done.3
  40.9 6.5 %shard_map.104 = (bf16[128,256]{1,0:T(8,128)(2,1)}, bf16[1024,256]{1,0:T(8,128)(2,1)}, f32[32,4,256]{2,1,0:T(4,128)}) custom-call(s32[8,1024]{1,0:T(8,128)} %broadcast_in_dim.42.refs_0_, bf16[1024,256]{1,0:T(8,128)(2,1)} %bitcast.23, bf16[256,768]{1,0:T(8,128)(2,1)} %refs_2_.1, bf16[256,768]{1,0:T(8,128)(2,1)} %refs_3_.1, bf16[128,256]{1,0:T(8,128)(2,1)} %bitcast.29, ...), custom_call_target="tpu_custom_call" | custom-call | tf_op jit(solution)/shard_map/pallas_call | solution.py:210
  47.4 28.7 %shard_map.105 = (bf16[32,32,256]{2,1,0:T(8,128)(2,1)}, f32[4,256]{1,0:T(4,128)}) custom-call(bf16[32,32,256]{2,1,0:T(8,128)(2,1)} %bitcast.25, f32[32,4,256]{2,1,0:T(4,128)} %get-tuple-element.13.refs_1_), custom_call_target="tpu_custom_call" | custom-call | tf_op jit(solution)/shard_map/pallas_call | solution.py:157
  76.1 0.0 copy-done
  76.1 2.3 %fusion.3 = f32[512,768]{1,0:T(8,128)S(1)} fusion(bf16[256,768]{1,0:T(8,128)(2,1)S(1)} %copy-done, bf16[1024,256]{1,0:T(8,128)(2,1)} %bitcast.24, s32[1024]{0:T(1024)S(1)} %eq.49), kind=kOutput, calls=%fused_computation.7 | convolution fusion | flops 470417408 | bytes 2494464 | tf_op jit(solution)/shard_map/dot_general | solution.py:268
  78.4 0.4 fusion.41
  78.8 1.1 %fusion.21 = bf16[1,512,256]{2,1,0:T(8,128)(2,1)} fusion(f32[512,768]{1,0:T(8,128)S(1)} %fusion.41, f32[512,768]{1,0:T(8,128)S(1)} %fusion.3, bf16[1,512,256]{2,1,0:T(8,128)(2,1)S(1)} %copy-done.1), kind=kLoop, calls=%fused_computation.27 | loop fusion | flops 2097152 | bytes 3670016 | tf_op jit(solution)/shard_map/broadcast_in_dim | solution.py:270
  79.9 0.0 copy-done.4
  79.9 0.6 copy.36
  (10 shorter events, 0.1 us)
Async XLA Ops:
  0.6 75.5 %copy-start = (bf16[256,768]{1,0:T(8,128)(2,1)S(1)}, bf16[256,768]{1,0:T(8,128)(2,1)}, u32[]{:S(2)}) copy-start(bf16[256,768]{1,0:T(8,128)(2,1)} %param.13) | copy-start | bytes 1179652
  3.1 37.8 %copy-start.3 = (s32[8,128]{1,0:T(8,128)}, s32[8,128]{1,0:T(8,128)S(1)}, u32[]{:S(2)}) copy-start(s32[8,128]{1,0:T(8,128)S(1)} %copy.32) | copy-start | bytes 12292
  47.4 31.0 %copy-start.1 = (bf16[1,512,256]{2,1,0:T(8,128)(2,1)S(1)}, bf16[1,512,256]{2,1,0:T(8,128)(2,1)}, u32[]{:S(2)}) copy-start(bf16[1,512,256]{2,1,0:T(8,128)(2,1)} %param.8) | copy-start | bytes 786436
  47.4 31.0 %copy-start.2 = (bf16[256,768]{1,0:T(8,128)(2,1)S(1)}, bf16[256,768]{1,0:T(8,128)(2,1)}, u32[]{:S(2)}) copy-start(bf16[256,768]{1,0:T(8,128)(2,1)} %param.14) | copy-start | bytes 1179652
  78.8 1.1 %copy-start.4 = (f32[4,256]{1,0:T(4,128)S(1)}, f32[4,256]{1,0:T(4,128)}, u32[]{:S(2)}) copy-start(f32[4,256]{1,0:T(4,128)} %get-tuple-element.24) | copy-start | bytes 12292

commit v10 on v9

--- a/solution.py
+++ b/solution.py
@@ -54,10 +54,11 @@
 
 
 def _fetch_kernel(n_grp, n_path, req_ref, links_ref, got_ref, ids_ref,
-                  reqin, want, served, gotbuf, rsend, rrecv, asend, arecv):
+                  reqin, want, served, gotbuf, rsend, rrecv, asend, arecv, greet=True):
     g = lax.axis_index("grp")
     p = lax.axis_index("path")
-    _greet(pltpu.get_barrier_semaphore(), g, p, n_grp, n_path, False)
+    if greet:
+        _greet(pltpu.get_barrier_semaphore(), g, p, n_grp, n_path, False)
     start_req, finish_req = _ring_copies(req_ref, reqin, rsend, rrecv, g, p, n_path, 1)
     lax.fori_loop(1, n_path, start_req, 0)
     reqin[0] = req_ref[0]
@@ -102,10 +103,11 @@
 
 
 def _message_kernel(n_grp, n_path, out_ref, term_ref, inc_ref, grad_ref,
-                    inbuf, recv1, recv2, mid, msend, mrecv, send1, got1, send2, got2):
+                    inbuf, recv1, recv2, mid, msend, mrecv, send1, got1, send2, got2, greet=True):
     g = lax.axis_index("grp")
     p = lax.axis_index("path")
-    _greet(pltpu.get_barrier_semaphore(), g, p, n_grp, n_path, True)
+    if greet:
+        _greet(pltpu.get_barrier_semaphore(), g, p, n_grp, n_path, True)
     start_msg, finish_msg = _ring_copies(out_ref, inbuf, msend, mrecv, g, p, n_path, 1)
 
     def path_copy(k, q):
@@ -179,10 +181,12 @@
 def _hop_kernel(hops, dcol_ref, got_ref, w_in_ref, w_hid_ref, state_ref, live_ref, drow_ref, cot_t_ref,
                 final_ref, out_ref, term_ref, proj, msgs):
     bf16, f32 = jnp.bfloat16, jnp.float32
-    entries, slots = dcol_ref.shape[1], got_ref.shape[0]
+    width = got_ref.shape[-1]
+    got = got_ref[...].reshape(-1, width)
+    entries, slots = dcol_ref.shape[1], got.shape[0]
     dcol = jnp.transpose(dcol_ref[...])[:, 0:1]
     route_t = (dcol == lax.broadcasted_iota(jnp.int32, (1, slots), 1)).astype(bf16)
-    fetched = jnp.dot(route_t, got_ref[...], preferred_element_type=f32).astype(bf16)
+    fetched = jnp.dot(route_t, got, preferred_element_type=f32).astype(bf16)
     proj[...] = jnp.dot(fetched, w_in_ref[...], preferred_element_type=f32)
     carried = state_ref[...].astype(f32)
     n, width = carried.shape
@@ -194,7 +198,7 @@
     final = carried.astype(bf16)
     final_ref[...] = final
     route = (lax.broadcasted_iota(jnp.int32, (slots, 1), 0) == drow_ref[...]).astype(bf16)
-    out_ref[...] = jnp.dot(route, msgs[...], preferred_element_type=f32).astype(bf16)
+    out_ref[...] = jnp.dot(route, msgs[...], preferred_element_type=f32).astype(bf16).reshape(out_ref.shape)
     cot_t = jnp.transpose(cot_t_ref[...].astype(f32)).astype(bf16)
     term = jnp.dot(cot_t, final, preferred_element_type=f32)
     share = term_ref.shape[1]
@@ -219,6 +223,61 @@
             pltpu.VMEM((entries, width), jnp.bfloat16),
         ],
     )(dcol, got, w_path_in, w_path_hid, state, live, drow, cot_t)
+
+
+def _all_kernel(n_grp, n_path, req_ref, links_ref, dcol_ref, w_in_ref, w_hid_ref, state_ref, live_ref,
+                drow_ref, cot_ref, ids_ref, final_ref, inc_ref, grad_ref,
+                reqin, want, served, gotbuf, gotv, rsend, rrecv, asend, arecv,
+                proj, msgs, outbuf, termbuf,
+                inbuf, recv1, recv2, mid, msend, mrecv, send1, got1, send2, got2):
+    g = lax.axis_index("grp")
+    p = lax.axis_index("path")
+    _greet(pltpu.get_barrier_semaphore(), g, p, n_grp, n_path, True)
+    _fetch_kernel(n_grp, n_path, req_ref, links_ref, gotv, ids_ref,
+                  reqin, want, served, gotbuf, rsend, rrecv, asend, arecv, greet=False)
+    hops = dcol_ref.shape[1] // state_ref.shape[0]
+    _hop_kernel(hops, dcol_ref, gotv, w_in_ref, w_hid_ref, state_ref, live_ref, drow_ref, cot_ref,
+                final_ref, outbuf, termbuf, proj, msgs)
+    _message_kernel(n_grp, n_path, outbuf, termbuf, inc_ref, grad_ref,
+                    inbuf, recv1, recv2, mid, msend, mrecv, send1, got1, send2, got2, greet=False)
+
+
+def run_all(req, own_links, drow8, w_path_in, w_path_hid, state, live, drow1, cot, cap, n_grp, n_path):
+    n_k, rows, lanes = req.shape
+    link_dev, width = own_links.shape
+    entries = drow8.shape[1]
+    n = state.shape[0]
+    share = cot.shape[1] // n_path
+    vmem = pltpu.VMEM
+    dma = pltpu.SemaphoreType.DMA
+    return pl.pallas_call(
+        lambda *refs: _all_kernel(n_grp, n_path, *refs),
+        out_shape=(jax.ShapeDtypeStruct((n_k, rows, lanes), jnp.int32),
+                   jax.ShapeDtypeStruct((n, width), jnp.bfloat16),
+                   jax.ShapeDtypeStruct((n_k, cap, width), jnp.bfloat16),
+                   jax.ShapeDtypeStruct((share, width), jnp.float32)),
+        in_specs=[pl.BlockSpec(memory_space=vmem)] * 9,
+        out_specs=(pl.BlockSpec(memory_space=vmem),) * 4,
+        scratch_shapes=[
+            vmem((n_k, rows, lanes), jnp.int32),
+            vmem((n_k * cap, link_dev), jnp.bfloat16),
+            vmem((n_k, cap, width), jnp.bfloat16),
+            vmem((n_k, cap, width), jnp.bfloat16),
+            vmem((n_k, cap, width), jnp.bfloat16),
+            dma((n_path - 1,)), dma((n_path - 1,)), dma((n_path - 1,)), dma((n_path - 1,)),
+            vmem((entries, w_path_in.shape[1]), jnp.float32),
+            vmem((entries, width), jnp.bfloat16),
+            vmem((n_k, cap, width), jnp.bfloat16),
+            vmem((n_path, share, width), jnp.float32),
+            vmem((n_k, cap, width), jnp.bfloat16),
+            vmem((n_path - 1, share, width), jnp.float32),
+            vmem((n_grp - 1, share, width), jnp.float32),
+            vmem((share, width), jnp.float32),
+            dma((n_path - 1,)), dma((n_path - 1,)), dma((n_path - 1,)), dma((n_path - 1,)),
+            dma((n_grp - 1,)), dma((n_grp - 1,)),
+        ],
+        compiler_params=pltpu.CompilerParams(collective_id=0, has_side_effects=True),
+    )(req, own_links, drow8, w_path_in, w_path_hid, state, live, drow1, cot)
 
 
 def shards(
@@ -253,13 +312,10 @@
     req = jnp.full((peer_count, 8, 128), -1, jnp.int32)
     req = lax.dynamic_update_slice(req, requests.reshape(peer_count, 1, capacity), (0, 0, 0))
     live_grid = is_live.reshape(path_count, hop_count).astype(jnp.int32)
-    got, req_ids = fetch_rows(req, own_links, capacity, n_grp, peer_count)
     drow = jnp.broadcast_to(dest[None, :], (8, entries))
-    path_final, outgoing, term = run_hops(
-        drow, got.reshape(slots, width), w_path_in, w_path_hid, path_state[0], live_grid,
-        drow[0:1], cotangent[0], peer_count)
-    incoming, read_grad = exchange_messages(
-        outgoing.reshape(peer_count, capacity, width), term, n_grp, peer_count)
+    req_ids, path_final, incoming, read_grad = run_all(
+        req, own_links, drow, w_path_in, w_path_hid, path_state[0], live_grid, drow[0:1],
+        cotangent[0], capacity, n_grp, peer_count)
     received = req_ids[:, 0, :capacity].reshape(-1)
     want = (received[:, None] == jnp.arange(link_dev)[None, :]).astype(bf16)
     link_sum = lax.dot_general(

time: 81 us -> 73.2 us (0.904)
  Pallas kernels: 70 us -> 61.9 us
    pallas_call x3 -> x1, Pallas kernels: 70 us -> 61.9 us  [run_all(): pl.pallas_call(lambda *refs: _all_kernel(n_grp, n_path, *refs), out_shape...]
    unnamed x12 -> x15, local copies, waits for them, and re-layouts: 1.45 us -> 2.09 us
where the time goes in v10:
time: 73.2 us; the launch traced here: 73 us
  Pallas kernels  61.9 us (85%)
  local copies, waits for them, and re-layouts  4.81 us (7%)
  matrix products  3.21 us (4%)
  other arithmetic  2.36 us (3%)
  between operations  0.76 us (1%)
    pallas_call x1, Pallas kernels, run_all(): pl.pallas_call(lambda *refs: _all_kernel(n_grp, n_path, *refs), out_shape...  61.9 us
    dot_general x1, matrix products, shards(): jnp.dot(link_sum.astype(bf16), w_link_in, preferred_element_type=f32)  2.31 us
    unnamed x15, local copies, waits for them, and re-layouts  2.09 us

profile of v10, /device:TPU:6, one launch (start us, length us, event | category | flops | bytes accessed | tf_op | source)
XLA Modules:
  0.0 73.0 jit_solution(17387613279570242986)
XLA Ops:
  0.6 0.0 copy-start
  0.6 0.8 %copy.26 = s32[128,8]{1,0:T(8,128)S(1)} copy(s32[128,8]{0,1:T(8,128)} %param.10) | data formatting | bytes 8192 | tf_op args[2]
  1.5 0.1 reshape.76
  1.6 0.5 fusion.5
  2.1 0.1 convert_element_type.31
  2.2 0.1 fusion.34
  2.3 0.6 fusion.37.refs_6_
  3.0 0.1 copy.33
  3.1 0.5 select_reduce_fusion
  3.6 0.1 sub.29
  3.7 0.6 broadcast_in_dim.42.refs_2_
  4.3 0.7 dynamic_update_slice.3.refs_0_
  5.0 0.0 copy-done.3
  5.0 61.9 %shard_map.103 = (s32[32,8,128]{2,1,0:T(8,128)}, bf16[128,256]{1,0:T(8,128)(2,1)}, bf16[32,32,256]{2,1,0:T(8,128)(2,1)}, f32[4,256]{1,0:T(4,128)}) custom-call(s32[32,8,128]{2,1,0:T(8,128)} %dynamic_update_slice.3.refs_0_, bf16[512,256]{1,0:T(8,128)(2,1)} %bitcast.20, s32[8,1024]{1,0:T(8,128)} %broadcast_in_dim.42.refs_2_, bf16[256,768]{1,0:T(8,128)(2,1)} %refs_3_.1, ...), custom_call_target="tpu_custom_call" | custom-call | tf_op jit(solution)/shard_map/pallas_call | solution.py:253
  66.9 0.0 copy-start.1
  66.9 0.0 copy-start.2
  66.9 1.0 %slice_reduce_fusion = s32[32,32]{1,0:T(8,128)S(1)} fusion(s32[32,8,128]{2,1,0:T(8,128)} %get-tuple-element.7), kind=kLoop, calls=%fused_computation.54 | loop fusion | bytes 8192 | tf_op jit(solution)/shard_map/slice | solution.py:319
  67.9 0.1 eq.49
  68.0 2.3 %fusion.3 = f32[512,768]{1,0:T(8,128)S(1)} fusion(bf16[256,768]{1,0:T(8,128)(2,1)S(1)} %copy-done, bf16[1024,256]{1,0:T(8,128)(2,1)} %bitcast.21, s32[1024]{0:T(1024)S(1)} %eq.49), kind=kOutput, calls=%fused_computation.7 | convolution fusion | flops 470417408 | bytes 2494464 | tf_op jit(solution)/shard_map/dot_general | solution.py:324
  70.3 0.4 fusion.41
  70.7 1.1 %fusion.21 = bf16[1,512,256]{2,1,0:T(8,128)(2,1)} fusion(f32[512,768]{1,0:T(8,128)S(1)} %fusion.41, f32[512,768]{1,0:T(8,128)S(1)} %fusion.3, bf16[1,512,256]{2,1,0:T(8,128)(2,1)S(1)} %copy-done.1), kind=kLoop, calls=%fused_computation.27 | loop fusion | flops 2097152 | bytes 3670016 | tf_op jit(solution)/shard_map/broadcast_in_dim | solution.py:326
  71.8 0.0 copy-done.4
  71.8 0.6 copy.37
  72.4 0.6 copy.38
  (11 shorter events, 0.1 us)
Async XLA Ops:
  0.6 67.4 %copy-start = (bf16[256,768]{1,0:T(8,128)(2,1)S(1)}, bf16[256,768]{1,0:T(8,128)(2,1)}, u32[]{:S(2)}) copy-start(bf16[256,768]{1,0:T(8,128)(2,1)} %param.13) | copy-start | bytes 1179652
  3.0 2.0 %copy-start.3 = (s32[8,128]{1,0:T(8,128)}, s32[8,128]{1,0:T(8,128)S(1)}, u32[]{:S(2)}) copy-start(s32[8,128]{1,0:T(8,128)S(1)} %copy.32) | copy-start | bytes 12292
  66.9 3.4 %copy-start.1 = (bf16[1,512,256]{2,1,0:T(8,128)(2,1)S(1)}, bf16[1,512,256]{2,1,0:T(8,128)(2,1)}, u32[]{:S(2)}) copy-start(bf16[1,512,256]{2,1,0:T(8,128)(2,1)} %param.8) | copy-start | bytes 786436
  66.9 3.4 %copy-start.2 = (bf16[256,768]{1,0:T(8,128)(2,1)S(1)}, bf16[256,768]{1,0:T(8,128)(2,1)}, u32[]{:S(2)}) copy-start(bf16[256,768]{1,0:T(8,128)(2,1)} %param.14) | copy-start | bytes 1179652
  70.7 1.1 %copy-start.4 = (bf16[128,256]{1,0:T(8,128)(2,1)S(1)}, bf16[128,256]{1,0:T(8,128)(2,1)}, u32[]{:S(2)}) copy-start(bf16[128,256]{1,0:T(8,128)(2,1)} %get-tuple-element.9) | copy-start | bytes 196612
  70.7 1.7 %copy-start.5 = (f32[4,256]{1,0:T(4,128)S(1)}, f32[4,256]{1,0:T(4,128)}, u32[]{:S(2)}) copy-start(f32[4,256]{1,0:T(4,128)} %get-tuple-element.18) | copy-start | bytes 12292

commit v11 on v10

--- a/solution.py
+++ b/solution.py
@@ -54,7 +54,7 @@
 
 
 def _fetch_kernel(n_grp, n_path, req_ref, links_ref, got_ref, ids_ref,
-                  reqin, want, served, gotbuf, rsend, rrecv, asend, arecv, greet=True):
+                  reqin, want, served, gotbuf, rsend, rrecv, asend, arecv, greet=True, during=None):
     g = lax.axis_index("grp")
     p = lax.axis_index("path")
     if greet:
@@ -74,7 +74,10 @@
     start_ans, finish_ans = _ring_copies(served, gotbuf, asend, arecv, g, p, n_path, -1)
     lax.fori_loop(1, n_path, start_ans, 0)
     gotbuf[0] = served[0]
-    ids_ref[...] = reqin[...]
+    if ids_ref is not None:
+        ids_ref[...] = reqin[...]
+    if during is not None:
+        during()
     lax.fori_loop(1, n_path, finish_ans, 0)
     got_ref[...] = gotbuf[...]
 
@@ -103,7 +106,8 @@
 
 
 def _message_kernel(n_grp, n_path, out_ref, term_ref, inc_ref, grad_ref,
-                    inbuf, recv1, recv2, mid, msend, mrecv, send1, got1, send2, got2, greet=True):
+                    inbuf, recv1, recv2, mid, msend, mrecv, send1, got1, send2, got2, greet=True,
+                    after_msgs=None):
     g = lax.axis_index("grp")
     p = lax.axis_index("path")
     if greet:
@@ -148,7 +152,10 @@
 
     lax.fori_loop(1, n_grp, start2, 0)
     lax.fori_loop(1, n_path, finish_msg, 0)
-    inc_ref[...] = inbuf[...]
+    if inc_ref is not None:
+        inc_ref[...] = inbuf[...]
+    if after_msgs is not None:
+        after_msgs()
     lax.fori_loop(1, n_grp, finish2, 0)
     grad_ref[...] = mid[...] + jnp.sum(recv2[...], axis=0)
 
@@ -226,23 +233,42 @@
 
 
 def _all_kernel(n_grp, n_path, req_ref, links_ref, dcol_ref, w_in_ref, w_hid_ref, state_ref, live_ref,
-                drow_ref, cot_ref, ids_ref, final_ref, inc_ref, grad_ref,
+                drow_ref, cot_ref, w_lin_ref, w_lhid_ref, final_ref, next_ref, grad_ref,
                 reqin, want, served, gotbuf, gotv, rsend, rrecv, asend, arecv,
-                proj, msgs, outbuf, termbuf,
+                proj, msgs, outbuf, termbuf, recur_buf,
                 inbuf, recv1, recv2, mid, msend, mrecv, send1, got1, send2, got2):
+    f32 = jnp.float32
     g = lax.axis_index("grp")
     p = lax.axis_index("path")
     _greet(pltpu.get_barrier_semaphore(), g, p, n_grp, n_path, True)
-    _fetch_kernel(n_grp, n_path, req_ref, links_ref, gotv, ids_ref,
-                  reqin, want, served, gotbuf, rsend, rrecv, asend, arecv, greet=False)
+
+    def link_recur():
+        recur_buf[...] = jnp.dot(links_ref[...], w_lhid_ref[...], preferred_element_type=f32)
+
+    def link_update():
+        width = links_ref.shape[1]
+        incoming = inbuf[...].reshape(-1, width)
+        link_sum = lax.dot_general(want[...], incoming, (((0,), (0,)), ((), ())), preferred_element_type=f32)
+        link_proj = jnp.dot(link_sum.astype(jnp.bfloat16), w_lin_ref[...], preferred_element_type=f32)
+        recur = recur_buf[...]
+        own = links_ref[...].astype(f32)
+        reset = jax.nn.sigmoid(link_proj[:, :width] + recur[:, :width])
+        update = jax.nn.sigmoid(link_proj[:, width : 2 * width] + recur[:, width : 2 * width])
+        candidate = jnp.tanh(link_proj[:, 2 * width :] + reset * recur[:, 2 * width :])
+        next_ref[...] = ((1.0 - update) * candidate + update * own).astype(next_ref.dtype)
+
+    _fetch_kernel(n_grp, n_path, req_ref, links_ref, gotv, None,
+                  reqin, want, served, gotbuf, rsend, rrecv, asend, arecv, greet=False, during=link_recur)
     hops = dcol_ref.shape[1] // state_ref.shape[0]
     _hop_kernel(hops, dcol_ref, gotv, w_in_ref, w_hid_ref, state_ref, live_ref, drow_ref, cot_ref,
                 final_ref, outbuf, termbuf, proj, msgs)
-    _message_kernel(n_grp, n_path, outbuf, termbuf, inc_ref, grad_ref,
-                    inbuf, recv1, recv2, mid, msend, mrecv, send1, got1, send2, got2, greet=False)
-
-
-def run_all(req, own_links, drow8, w_path_in, w_path_hid, state, live, drow1, cot, cap, n_grp, n_path):
+    _message_kernel(n_grp, n_path, outbuf, termbuf, None, grad_ref,
+                    inbuf, recv1, recv2, mid, msend, mrecv, send1, got1, send2, got2, greet=False,
+                    after_msgs=link_update)
+
+
+def run_all(req, own_links, drow8, w_path_in, w_path_hid, state, live, drow1, cot, w_link_in, w_link_hid,
+            cap, n_grp, n_path):
     n_k, rows, lanes = req.shape
     link_dev, width = own_links.shape
     entries = drow8.shape[1]
@@ -252,12 +278,11 @@
     dma = pltpu.SemaphoreType.DMA
     return pl.pallas_call(
         lambda *refs: _all_kernel(n_grp, n_path, *refs),
-        out_shape=(jax.ShapeDtypeStruct((n_k, rows, lanes), jnp.int32),
-                   jax.ShapeDtypeStruct((n, width), jnp.bfloat16),
-                   jax.ShapeDtypeStruct((n_k, cap, width), jnp.bfloat16),
+        out_shape=(jax.ShapeDtypeStruct((n, width), jnp.bfloat16),
+                   jax.ShapeDtypeStruct((link_dev, width), jnp.bfloat16),
                    jax.ShapeDtypeStruct((share, width), jnp.float32)),
-        in_specs=[pl.BlockSpec(memory_space=vmem)] * 9,
-        out_specs=(pl.BlockSpec(memory_space=vmem),) * 4,
+        in_specs=[pl.BlockSpec(memory_space=vmem)] * 11,
+        out_specs=(pl.BlockSpec(memory_space=vmem),) * 3,
         scratch_shapes=[
             vmem((n_k, rows, lanes), jnp.int32),
             vmem((n_k * cap, link_dev), jnp.bfloat16),
@@ -269,6 +294,7 @@
             vmem((entries, width), jnp.bfloat16),
             vmem((n_k, cap, width), jnp.bfloat16),
             vmem((n_path, share, width), jnp.float32),
+            vmem((link_dev, w_link_hid.shape[1]), jnp.float32),
             vmem((n_k, cap, width), jnp.bfloat16),
             vmem((n_path - 1, share, width), jnp.float32),
             vmem((n_grp - 1, share, width), jnp.float32),
@@ -277,7 +303,7 @@
             dma((n_grp - 1,)), dma((n_grp - 1,)),
         ],
         compiler_params=pltpu.CompilerParams(collective_id=0, has_side_effects=True),
-    )(req, own_links, drow8, w_path_in, w_path_hid, state, live, drow1, cot)
+    )(req, own_links, drow8, w_path_in, w_path_hid, state, live, drow1, cot, w_link_in, w_link_hid)
 
 
 def shards(
@@ -313,16 +339,9 @@
     req = lax.dynamic_update_slice(req, requests.reshape(peer_count, 1, capacity), (0, 0, 0))
     live_grid = is_live.reshape(path_count, hop_count).astype(jnp.int32)
     drow = jnp.broadcast_to(dest[None, :], (8, entries))
-    req_ids, path_final, incoming, read_grad = run_all(
+    path_final, link_next, read_grad = run_all(
         req, own_links, drow, w_path_in, w_path_hid, path_state[0], live_grid, drow[0:1],
-        cotangent[0], capacity, n_grp, peer_count)
-    received = req_ids[:, 0, :capacity].reshape(-1)
-    want = (received[:, None] == jnp.arange(link_dev)[None, :]).astype(bf16)
-    link_sum = lax.dot_general(
-        want, incoming.reshape(slots, width), (((0,), (0,)), ((), ())), preferred_element_type=f32
-    )
-    link_proj = jnp.dot(link_sum.astype(bf16), w_link_in, preferred_element_type=f32)
-    link_next = gated_update(link_proj, own_links.astype(f32), w_link_hid).astype(bf16)
+        cotangent[0], w_link_in, w_link_hid, capacity, n_grp, peer_count)
     return (link_next[None], path_final[None], read_grad)
 
 

time: 73.2 us -> 71.1 us (0.971)
  matrix products: 3.21 us -> 0.53 us
  Pallas kernels: 61.9 us -> 63 us
  other arithmetic: 2.36 us -> 1.28 us
    dot_general x2 -> x0, matrix products: 2.68 us -> none  [the longest x1 2.31 us: shards(): jnp.dot(link_sum.astype(bf16), w_link_in, preferred_element_type=f32)]
    unnamed x15 -> x10, local copies, waits for them, and re-layouts: 2.09 us -> 3.72 us
    pallas_call x1, Pallas kernels: 61.9 us -> 63 us  [run_all(): pl.pallas_call(lambda *refs: _all_kernel(n_grp, n_path, *refs), out_shape...]
    broadcast_in_dim x1 -> x0, other arithmetic: 1.08 us -> none  [shards(): return (link_next[None], path_final[None], read_grad)]
    slice x1 -> x0, local copies, waits for them, and re-layouts: 1.01 us -> none  [shards(): received = req_ids[:, 0, :capacity].reshape(-1)]
where the time goes in v11:
time: 71.1 us; the launch traced here: 70.9 us
  Pallas kernels  63 us (89%)
  local copies, waits for them, and re-layouts  5.37 us (8%)
  other arithmetic  1.28 us (2%)
    pallas_call x1, Pallas kernels, run_all(): pl.pallas_call(lambda *refs: _all_kernel(n_grp, n_path, *refs), out_shape...  63 us
    unnamed x10, local copies, waits for them, and re-layouts  3.72 us

profile of v11, /device:TPU:6, one launch (start us, length us, event | category | flops | bytes accessed | tf_op | source)
XLA Modules:
  0.0 70.9 jit_solution(1106420114342257001)
XLA Ops:
  0.6 0.8 %copy.26 = s32[128,8]{1,0:T(8,128)S(1)} copy(s32[128,8]{0,1:T(8,128)} %param.10) | data formatting | bytes 8192 | tf_op args[2]
  1.4 0.1 reshape.72
  1.5 0.5 fusion.2
  2.1 0.1 convert_element_type.20
  2.2 0.1 fusion.15
  2.3 0.6 fusion.18.refs_6_
  3.0 0.0 copy-start
  3.0 0.1 copy.33
  3.0 0.5 select_reduce_fusion
  3.6 0.1 sub.26
  3.7 0.6 broadcast_in_dim.41.refs_2_
  4.3 0.7 dynamic_update_slice.3.refs_0_
  4.9 0.0 copy-done
  4.9 63.0 %shard_map.103 = (bf16[128,256]{1,0:T(8,128)(2,1)}, bf16[512,256]{1,0:T(8,128)(2,1)}, f32[4,256]{1,0:T(4,128)}) custom-call(s32[32,8,128]{2,1,0:T(8,128)} %dynamic_update_slice.3.refs_0_, bf16[512,256]{1,0:T(8,128)(2,1)} %bitcast.12, s32[8,1024]{1,0:T(8,128)} %broadcast_in_dim.41.refs_2_, bf16[256,768]{1,0:T(8,128)(2,1)} %refs_3_.1, ...), custom_call_target="tpu_custom_call" | custom-call | tf_op jit(solution)/shard_map/pallas_call | solution.py:279
  67.9 0.0 copy-start.1
  67.9 0.0 copy-start.2
  67.9 1.7 %copy.38 = bf16[1,512,256]{2,1,0:T(8,128)(2,1)} copy(bf16[1,512,256]{2,1,0:T(8,128)(2,1)} %bitcast.13) | data formatting | bytes 524288
  69.6 0.0 copy-done.1
  69.6 0.6 copy.39
  70.3 0.0 copy-done.2
  70.3 0.6 copy.40
  (4 shorter events, 0.1 us)
Async XLA Ops:
  3.0 2.0 %copy-start = (s32[8,128]{1,0:T(8,128)}, s32[8,128]{1,0:T(8,128)S(1)}, u32[]{:S(2)}) copy-start(s32[8,128]{1,0:T(8,128)S(1)} %copy.32) | copy-start | bytes 12292
  67.9 1.7 %copy-start.1 = (bf16[128,256]{1,0:T(8,128)(2,1)S(1)}, bf16[128,256]{1,0:T(8,128)(2,1)}, u32[]{:S(2)}) copy-start(bf16[128,256]{1,0:T(8,128)(2,1)} %get-tuple-element.7) | copy-start | bytes 196612
  67.9 2.3 %copy-start.2 = (f32[4,256]{1,0:T(4,128)S(1)}, f32[4,256]{1,0:T(4,128)}, u32[]{:S(2)}) copy-start(f32[4,256]{1,0:T(4,128)} %get-tuple-element.16) | copy-start | bytes 12292

commit v12 on v11

--- a/solution.py
+++ b/solution.py
@@ -185,27 +185,30 @@
     )(outgoing, term)
 
 
-def _hop_kernel(hops, dcol_ref, got_ref, w_in_ref, w_hid_ref, state_ref, live_ref, drow_ref, cot_t_ref,
+def _route_mats(drow, slots):
+    dcol = jnp.transpose(jnp.broadcast_to(drow, (8, drow.shape[1])))[:, 0:1]
+    route_t = (dcol == lax.broadcasted_iota(jnp.int32, (1, slots), 1)).astype(jnp.bfloat16)
+    route = (lax.broadcasted_iota(jnp.int32, (slots, 1), 0) == drow).astype(jnp.bfloat16)
+    return route_t, route
+
+
+def _hop_kernel(hops, route_t_ref, got_ref, w_in_ref, w_hid_ref, state_ref, live_ref, route_ref, cot_t_ref,
                 final_ref, out_ref, term_ref, proj, msgs):
     bf16, f32 = jnp.bfloat16, jnp.float32
     width = got_ref.shape[-1]
     got = got_ref[...].reshape(-1, width)
-    entries, slots = dcol_ref.shape[1], got.shape[0]
-    dcol = jnp.transpose(dcol_ref[...])[:, 0:1]
-    route_t = (dcol == lax.broadcasted_iota(jnp.int32, (1, slots), 1)).astype(bf16)
-    fetched = jnp.dot(route_t, got, preferred_element_type=f32).astype(bf16)
+    fetched = jnp.dot(route_t_ref[...], got, preferred_element_type=f32).astype(bf16)
     proj[...] = jnp.dot(fetched, w_in_ref[...], preferred_element_type=f32)
     carried = state_ref[...].astype(f32)
     n, width = carried.shape
     for h in range(hops):
         p_h = proj[h * n : (h + 1) * n, :]
         renewed = gated_update(p_h, carried, w_hid_ref[...])
-        carried = jnp.where(live_ref[:, h : h + 1] > 0, renewed, carried)
+        carried = jnp.where(live_ref[:, h : h + 1] >= 0, renewed, carried)
         msgs[h * n : (h + 1) * n, :] = carried.astype(bf16)
     final = carried.astype(bf16)
     final_ref[...] = final
-    route = (lax.broadcasted_iota(jnp.int32, (slots, 1), 0) == drow_ref[...]).astype(bf16)
-    out_ref[...] = jnp.dot(route, msgs[...], preferred_element_type=f32).astype(bf16).reshape(out_ref.shape)
+    out_ref[...] = jnp.dot(route_ref[...], msgs[...], preferred_element_type=f32).astype(bf16).reshape(out_ref.shape)
     cot_t = jnp.transpose(cot_t_ref[...].astype(f32)).astype(bf16)
     term = jnp.dot(cot_t, final, preferred_element_type=f32)
     share = term_ref.shape[1]
@@ -232,10 +235,10 @@
     )(dcol, got, w_path_in, w_path_hid, state, live, drow, cot_t)
 
 
-def _all_kernel(n_grp, n_path, req_ref, links_ref, dcol_ref, w_in_ref, w_hid_ref, state_ref, live_ref,
+def _all_kernel(n_grp, n_path, req_ref, links_ref, w_in_ref, w_hid_ref, state_ref, live_ref,
                 drow_ref, cot_ref, w_lin_ref, w_lhid_ref, final_ref, next_ref, grad_ref,
                 reqin, want, served, gotbuf, gotv, rsend, rrecv, asend, arecv,
-                proj, msgs, outbuf, termbuf, recur_buf,
+                proj, msgs, outbuf, termbuf, recur_buf, route_t_buf, route_buf,
                 inbuf, recv1, recv2, mid, msend, mrecv, send1, got1, send2, got2):
     f32 = jnp.float32
     g = lax.axis_index("grp")
@@ -244,6 +247,9 @@
 
     def link_recur():
         recur_buf[...] = jnp.dot(links_ref[...], w_lhid_ref[...], preferred_element_type=f32)
+        route_t, route = _route_mats(drow_ref[...], route_buf.shape[0])
+        route_t_buf[...] = route_t
+        route_buf[...] = route
 
     def link_update():
         width = links_ref.shape[1]
@@ -259,19 +265,19 @@
 
     _fetch_kernel(n_grp, n_path, req_ref, links_ref, gotv, None,
                   reqin, want, served, gotbuf, rsend, rrecv, asend, arecv, greet=False, during=link_recur)
-    hops = dcol_ref.shape[1] // state_ref.shape[0]
-    _hop_kernel(hops, dcol_ref, gotv, w_in_ref, w_hid_ref, state_ref, live_ref, drow_ref, cot_ref,
+    hops = drow_ref.shape[1] // state_ref.shape[0]
+    _hop_kernel(hops, route_t_buf, gotv, w_in_ref, w_hid_ref, state_ref, live_ref, route_buf, cot_ref,
                 final_ref, outbuf, termbuf, proj, msgs)
     _message_kernel(n_grp, n_path, outbuf, termbuf, None, grad_ref,
                     inbuf, recv1, recv2, mid, msend, mrecv, send1, got1, send2, got2, greet=False,
                     after_msgs=link_update)
 
 
-def run_all(req, own_links, drow8, w_path_in, w_path_hid, state, live, drow1, cot, w_link_in, w_link_hid,
+def run_all(req, own_links, w_path_in, w_path_hid, state, live, drow1, cot, w_link_in, w_link_hid,
             cap, n_grp, n_path):
     n_k, rows, lanes = req.shape
     link_dev, width = own_links.shape
-    entries = drow8.shape[1]
+    entries = drow1.shape[1]
     n = state.shape[0]
     share = cot.shape[1] // n_path
     vmem = pltpu.VMEM
@@ -281,7 +287,7 @@
         out_shape=(jax.ShapeDtypeStruct((n, width), jnp.bfloat16),
                    jax.ShapeDtypeStruct((link_dev, width), jnp.bfloat16),
                    jax.ShapeDtypeStruct((share, width), jnp.float32)),
-        in_specs=[pl.BlockSpec(memory_space=vmem)] * 11,
+        in_specs=[pl.BlockSpec(memory_space=vmem)] * 10,
         out_specs=(pl.BlockSpec(memory_space=vmem),) * 3,
         scratch_shapes=[
             vmem((n_k, rows, lanes), jnp.int32),
@@ -295,6 +301,8 @@
             vmem((n_k, cap, width), jnp.bfloat16),
             vmem((n_path, share, width), jnp.float32),
             vmem((link_dev, w_link_hid.shape[1]), jnp.float32),
+            vmem((entries, n_k * cap), jnp.bfloat16),
+            vmem((n_k * cap, entries), jnp.bfloat16),
             vmem((n_k, cap, width), jnp.bfloat16),
             vmem((n_path - 1, share, width), jnp.float32),
             vmem((n_grp - 1, share, width), jnp.float32),
@@ -303,7 +311,7 @@
             dma((n_grp - 1,)), dma((n_grp - 1,)),
         ],
         compiler_params=pltpu.CompilerParams(collective_id=0, has_side_effects=True),
-    )(req, own_links, drow8, w_path_in, w_path_hid, state, live, drow1, cot, w_link_in, w_link_hid)
+    )(req, own_links, w_path_in, w_path_hid, state, live, drow1, cot, w_link_in, w_link_hid)
 
 
 def shards(
@@ -337,10 +345,8 @@
     requests = jnp.sum(jnp.where(route, local_id[None, :] + 1, 0), axis=1) - 1
     req = jnp.full((peer_count, 8, 128), -1, jnp.int32)
     req = lax.dynamic_update_slice(req, requests.reshape(peer_count, 1, capacity), (0, 0, 0))
-    live_grid = is_live.reshape(path_count, hop_count).astype(jnp.int32)
-    drow = jnp.broadcast_to(dest[None, :], (8, entries))
     path_final, link_next, read_grad = run_all(
-        req, own_links, drow, w_path_in, w_path_hid, path_state[0], live_grid, drow[0:1],
+        req, own_links, w_path_in, w_path_hid, path_state[0], path_links, dest[None, :],
         cotangent[0], w_link_in, w_link_hid, capacity, n_grp, peer_count)
     return (link_next[None], path_final[None], read_grad)
 

time: 71.1 us -> 69.5 us (0.977)
    unnamed x10 -> x12, local copies, waits for them, and re-layouts: 3.72 us -> 3.73 us
where the time goes in v12:
time: 69.5 us; the launch traced here: 69.3 us
  Pallas kernels  62.6 us (90%)
  local copies, waits for them, and re-layouts  4.77 us (7%)
  between operations  0.72 us (1%)
    pallas_call x1, Pallas kernels, run_all(): pl.pallas_call(lambda *refs: _all_kernel(n_grp, n_path, *refs), out_shape...  62.6 us
    unnamed x12, local copies, waits for them, and re-layouts  3.73 us

profile of v12, /device:TPU:6, one launch (start us, length us, event | category | flops | bytes accessed | tf_op | source)
XLA Modules:
  0.0 69.3 jit_solution(5462820911043140066)
XLA Ops:
  0.6 0.8 %copy.30.refs_5_ = s32[128,8]{1,0:T(8,128)S(1)} copy(s32[128,8]{0,1:T(8,128)} %param.10) | data formatting | bytes 8192 | tf_op args[2]
  1.4 0.0 copy-start
  1.4 0.1 reshape.69
  1.5 0.5 fusion.2
  2.1 0.1 convert_element_type.17
  2.2 0.0 copy-done
  2.2 0.1 fusion.15
  2.3 0.0 copy-start.2
  2.3 0.1 copy.37
  2.4 0.5 select_reduce_fusion
  2.9 0.1 sub.26
  3.0 0.7 dynamic_update_slice.3.refs_0_
  3.7 0.0 copy-done.2
  3.7 62.6 %shard_map.103 = (bf16[128,256]{1,0:T(8,128)(2,1)}, bf16[512,256]{1,0:T(8,128)(2,1)}, f32[4,256]{1,0:T(4,128)}) custom-call(s32[32,8,128]{2,1,0:T(8,128)} %dynamic_update_slice.3.refs_0_, bf16[512,256]{1,0:T(8,128)(2,1)} %bitcast.13, bf16[256,768]{1,0:T(8,128)(2,1)} %refs_2_.1, bf16[256,768]{1,0:T(8,128)(2,1)} %refs_3_.1, bf16[128,256]{1,0:T(8,128)(2,1)} %bitcast.14, ...), custom_call_target="tpu_custom_call" | custom-call | tf_op jit(solution)/shard_map/pallas_call | solution.py:285
  66.3 0.0 copy-start.1
  66.3 0.0 copy-start.3
  66.4 1.7 %copy.43 = bf16[1,512,256]{2,1,0:T(8,128)(2,1)} copy(bf16[1,512,256]{2,1,0:T(8,128)(2,1)} %bitcast.12) | data formatting | bytes 524288
  68.1 0.0 copy-done.1
  68.1 0.6 copy.44
  68.7 0.0 copy-done.3
  68.7 0.6 copy.45
  (4 shorter events, 0.1 us)
Async XLA Ops:
  1.4 0.8 %copy-start = (s32[128,8]{1,0:T(8,128)}, s32[128,8]{1,0:T(8,128)S(1)}, u32[]{:S(2)}) copy-start(s32[128,8]{1,0:T(8,128)S(1)} %copy.30.refs_5_) | copy-start | bytes 12292
  2.3 1.4 %copy-start.2 = (s32[8,128]{1,0:T(8,128)}, s32[8,128]{1,0:T(8,128)S(1)}, u32[]{:S(2)}) copy-start(s32[8,128]{1,0:T(8,128)S(1)} %copy.36) | copy-start | bytes 12292
  66.3 1.7 %copy-start.1 = (bf16[128,256]{1,0:T(8,128)(2,1)S(1)}, bf16[128,256]{1,0:T(8,128)(2,1)}, u32[]{:S(2)}) copy-start(bf16[128,256]{1,0:T(8,128)(2,1)} %get-tuple-element.7) | copy-start | bytes 196612
  66.3 2.3 %copy-start.3 = (f32[4,256]{1,0:T(4,128)S(1)}, f32[4,256]{1,0:T(4,128)}, u32[]{:S(2)}) copy-start(f32[4,256]{1,0:T(4,128)} %get-tuple-element.16) | copy-start | bytes 12292

commit v13 on v12

--- a/solution.py
+++ b/solution.py
@@ -186,10 +186,10 @@
 
 
 def _route_mats(drow, slots):
-    dcol = jnp.transpose(jnp.broadcast_to(drow, (8, drow.shape[1])))[:, 0:1]
-    route_t = (dcol == lax.broadcasted_iota(jnp.int32, (1, slots), 1)).astype(jnp.bfloat16)
+    dcols = jnp.transpose(jnp.broadcast_to(drow, (8, drow.shape[1])))
+    route_t = (dcols[:, 0:1] == lax.broadcasted_iota(jnp.int32, (1, slots), 1)).astype(jnp.bfloat16)
     route = (lax.broadcasted_iota(jnp.int32, (slots, 1), 0) == drow).astype(jnp.bfloat16)
-    return route_t, route
+    return route_t, route, dcols
 
 
 def _hop_kernel(hops, route_t_ref, got_ref, w_in_ref, w_hid_ref, state_ref, live_ref, route_ref, cot_t_ref,
@@ -204,7 +204,7 @@
     for h in range(hops):
         p_h = proj[h * n : (h + 1) * n, :]
         renewed = gated_update(p_h, carried, w_hid_ref[...])
-        carried = jnp.where(live_ref[:, h : h + 1] >= 0, renewed, carried)
+        carried = jnp.where(live_ref[h * n : (h + 1) * n, 0:1] >= 0, renewed, carried)
         msgs[h * n : (h + 1) * n, :] = carried.astype(bf16)
     final = carried.astype(bf16)
     final_ref[...] = final
@@ -235,10 +235,10 @@
     )(dcol, got, w_path_in, w_path_hid, state, live, drow, cot_t)
 
 
-def _all_kernel(n_grp, n_path, req_ref, links_ref, w_in_ref, w_hid_ref, state_ref, live_ref,
+def _all_kernel(n_grp, n_path, req_ref, links_ref, w_in_ref, w_hid_ref, state_ref,
                 drow_ref, cot_ref, w_lin_ref, w_lhid_ref, final_ref, next_ref, grad_ref,
                 reqin, want, served, gotbuf, gotv, rsend, rrecv, asend, arecv,
-                proj, msgs, outbuf, termbuf, recur_buf, route_t_buf, route_buf,
+                proj, msgs, outbuf, termbuf, recur_buf, route_t_buf, route_buf, live_buf, next_buf, next_sem,
                 inbuf, recv1, recv2, mid, msend, mrecv, send1, got1, send2, got2):
     f32 = jnp.float32
     g = lax.axis_index("grp")
@@ -247,9 +247,10 @@
 
     def link_recur():
         recur_buf[...] = jnp.dot(links_ref[...], w_lhid_ref[...], preferred_element_type=f32)
-        route_t, route = _route_mats(drow_ref[...], route_buf.shape[0])
+        route_t, route, dcols = _route_mats(drow_ref[...], route_buf.shape[0])
         route_t_buf[...] = route_t
         route_buf[...] = route
+        live_buf[...] = dcols
 
     def link_update():
         width = links_ref.shape[1]
@@ -261,19 +262,21 @@
         reset = jax.nn.sigmoid(link_proj[:, :width] + recur[:, :width])
         update = jax.nn.sigmoid(link_proj[:, width : 2 * width] + recur[:, width : 2 * width])
         candidate = jnp.tanh(link_proj[:, 2 * width :] + reset * recur[:, 2 * width :])
-        next_ref[...] = ((1.0 - update) * candidate + update * own).astype(next_ref.dtype)
+        next_buf[...] = ((1.0 - update) * candidate + update * own).astype(next_buf.dtype)
+        pltpu.make_async_copy(next_buf, next_ref, next_sem).start()
 
     _fetch_kernel(n_grp, n_path, req_ref, links_ref, gotv, None,
                   reqin, want, served, gotbuf, rsend, rrecv, asend, arecv, greet=False, during=link_recur)
     hops = drow_ref.shape[1] // state_ref.shape[0]
-    _hop_kernel(hops, route_t_buf, gotv, w_in_ref, w_hid_ref, state_ref, live_ref, route_buf, cot_ref,
+    _hop_kernel(hops, route_t_buf, gotv, w_in_ref, w_hid_ref, state_ref, live_buf, route_buf, cot_ref,
                 final_ref, outbuf, termbuf, proj, msgs)
     _message_kernel(n_grp, n_path, outbuf, termbuf, None, grad_ref,
                     inbuf, recv1, recv2, mid, msend, mrecv, send1, got1, send2, got2, greet=False,
                     after_msgs=link_update)
-
-
-def run_all(req, own_links, w_path_in, w_path_hid, state, live, drow1, cot, w_link_in, w_link_hid,
+    pltpu.make_async_copy(next_buf, next_ref, next_sem).wait()
+
+
+def run_all(req, own_links, w_path_in, w_path_hid, state, drow1, cot, w_link_in, w_link_hid,
             cap, n_grp, n_path):
     n_k, rows, lanes = req.shape
     link_dev, width = own_links.shape
@@ -287,8 +290,9 @@
         out_shape=(jax.ShapeDtypeStruct((n, width), jnp.bfloat16),
                    jax.ShapeDtypeStruct((link_dev, width), jnp.bfloat16),
                    jax.ShapeDtypeStruct((share, width), jnp.float32)),
-        in_specs=[pl.BlockSpec(memory_space=vmem)] * 10,
-        out_specs=(pl.BlockSpec(memory_space=vmem),) * 3,
+        in_specs=[pl.BlockSpec(memory_space=vmem)] * 9,
+        out_specs=(pl.BlockSpec(memory_space=vmem), pl.BlockSpec(memory_space=pl.ANY),
+                   pl.BlockSpec(memory_space=vmem)),
         scratch_shapes=[
             vmem((n_k, rows, lanes), jnp.int32),
             vmem((n_k * cap, link_dev), jnp.bfloat16),
@@ -303,6 +307,9 @@
             vmem((link_dev, w_link_hid.shape[1]), jnp.float32),
             vmem((entries, n_k * cap), jnp.bfloat16),
             vmem((n_k * cap, entries), jnp.bfloat16),
+            vmem((entries, 8), jnp.int32),
+            vmem((link_dev, width), jnp.bfloat16),
+            dma(()),
             vmem((n_k, cap, width), jnp.bfloat16),
             vmem((n_path - 1, share, width), jnp.float32),
             vmem((n_grp - 1, share, width), jnp.float32),
@@ -311,7 +318,7 @@
             dma((n_grp - 1,)), dma((n_grp - 1,)),
         ],
         compiler_params=pltpu.CompilerParams(collective_id=0, has_side_effects=True),
-    )(req, own_links, w_path_in, w_path_hid, state, live, drow1, cot, w_link_in, w_link_hid)
+    )(req, own_links, w_path_in, w_path_hid, state, drow1, cot, w_link_in, w_link_hid)
 
 
 def shards(
@@ -346,7 +353,7 @@
     req = jnp.full((peer_count, 8, 128), -1, jnp.int32)
     req = lax.dynamic_update_slice(req, requests.reshape(peer_count, 1, capacity), (0, 0, 0))
     path_final, link_next, read_grad = run_all(
-        req, own_links, w_path_in, w_path_hid, path_state[0], path_links, dest[None, :],
+        req, own_links, w_path_in, w_path_hid, path_state[0], dest[None, :],
         cotangent[0], w_link_in, w_link_hid, capacity, n_grp, peer_count)
     return (link_next[None], path_final[None], read_grad)
 

time: 69.5 us -> 69.9 us (level)
    unnamed x12 -> x10, local copies, waits for them, and re-layouts: 3.73 us -> 3.72 us
where the time goes in v13:
time: 69.9 us; the launch traced here: 69.7 us
  Pallas kernels  63.1 us (90%)
  local copies, waits for them, and re-layouts  4.76 us (7%)
  between operations  0.71 us (1%)
    pallas_call x1, Pallas kernels, run_all(): pl.pallas_call(lambda *refs: _all_kernel(n_grp, n_path, *refs), out_shape...  63.1 us
    unnamed x10, local copies, waits for them, and re-layouts  3.72 us

profile of v13, /device:TPU:6, one launch (start us, length us, event | category | flops | bytes accessed | tf_op | source)
XLA Modules:
  0.0 69.7 jit_solution(6663503762440168396)
XLA Ops:
  0.6 0.8 %copy.27 = s32[128,8]{1,0:T(8,128)S(1)} copy(s32[128,8]{0,1:T(8,128)} %param.10) | data formatting | bytes 8192 | tf_op args[2]
  1.4 0.1 reshape.69
  1.5 0.5 fusion.2
  2.1 0.1 convert_element_type.17
  2.2 0.1 fusion.15
  2.3 0.0 copy-start.1
  2.3 0.1 copy.34
  2.4 0.5 select_reduce_fusion
  2.9 0.1 sub.26
  3.0 0.7 dynamic_update_slice.3.refs_0_
  3.7 0.0 copy-done.1
  3.7 63.1 %shard_map.103 = (bf16[128,256]{1,0:T(8,128)(2,1)}, bf16[512,256]{1,0:T(8,128)(2,1)}, f32[4,256]{1,0:T(4,128)}) custom-call(s32[32,8,128]{2,1,0:T(8,128)} %dynamic_update_slice.3.refs_0_, bf16[512,256]{1,0:T(8,128)(2,1)} %bitcast.13, bf16[256,768]{1,0:T(8,128)(2,1)} %refs_2_.1, bf16[256,768]{1,0:T(8,128)(2,1)} %refs_3_.1, bf16[128,256]{1,0:T(8,128)(2,1)} %bitcast.14, ...), custom_call_target="tpu_custom_call" | custom-call | tf_op jit(solution)/shard_map/pallas_call | solution.py:288
  66.8 0.0 copy-start
  66.8 0.0 copy-start.2
  66.8 1.7 %copy.39 = bf16[1,512,256]{2,1,0:T(8,128)(2,1)} copy(bf16[1,512,256]{2,1,0:T(8,128)(2,1)} %bitcast.12) | data formatting | bytes 524288
  68.5 0.0 copy-done
  68.5 0.6 copy.40
  69.1 0.0 copy-done.2
  69.1 0.6 copy.41
  (4 shorter events, 0.1 us)
Async XLA Ops:
  2.3 1.4 %copy-start.1 = (s32[8,128]{1,0:T(8,128)}, s32[8,128]{1,0:T(8,128)S(1)}, u32[]{:S(2)}) copy-start(s32[8,128]{1,0:T(8,128)S(1)} %copy.33) | copy-start | bytes 12292
  66.8 1.7 %copy-start = (bf16[128,256]{1,0:T(8,128)(2,1)S(1)}, bf16[128,256]{1,0:T(8,128)(2,1)}, u32[]{:S(2)}) copy-start(bf16[128,256]{1,0:T(8,128)(2,1)} %get-tuple-element.7) | copy-start | bytes 196612
  66.8 2.3 %copy-start.2 = (f32[4,256]{1,0:T(4,128)S(1)}, f32[4,256]{1,0:T(4,128)}, u32[]{:S(2)}) copy-start(f32[4,256]{1,0:T(4,128)} %get-tuple-element.16) | copy-start | bytes 12292

commit v14 on v12

--- a/solution.py
+++ b/solution.py
@@ -62,24 +62,27 @@
     start_req, finish_req = _ring_copies(req_ref, reqin, rsend, rrecv, g, p, n_path, 1)
     lax.fori_loop(1, n_path, start_req, 0)
     reqin[0] = req_ref[0]
-    lax.fori_loop(1, n_path, finish_req, 0)
     n_k, cap = served.shape[0], served.shape[1]
     link_dev = links_ref.shape[0]
-    ids_t = jnp.transpose(reqin[:, 0, :])
     lanes = lax.broadcasted_iota(jnp.int32, (1, link_dev), 1)
-    for k in range(n_k):
-        want[k * cap : (k + 1) * cap, :] = (ids_t[0:cap, k : k + 1] == lanes).astype(jnp.bfloat16)
-    rows = jnp.dot(want[...], links_ref[...], preferred_element_type=jnp.float32).astype(jnp.bfloat16)
-    served[...] = rows.reshape(served.shape)
     start_ans, finish_ans = _ring_copies(served, gotbuf, asend, arecv, g, p, n_path, -1)
-    lax.fori_loop(1, n_path, start_ans, 0)
+    half = n_k // 2
+    for lo, hi in ((0, half), (half, n_k)):
+        lax.fori_loop(max(lo, 1), hi, finish_req, 0)
+        ids_t = jnp.transpose(reqin[lo:hi, 0, :])
+        for k in range(lo, hi):
+            want[k * cap : (k + 1) * cap, :] = (ids_t[0:cap, k - lo : k - lo + 1] == lanes).astype(jnp.bfloat16)
+        rows = jnp.dot(want[lo * cap : hi * cap, :], links_ref[...], preferred_element_type=jnp.float32)
+        served[lo:hi] = rows.astype(jnp.bfloat16).reshape(hi - lo, cap, rows.shape[-1])
+        lax.fori_loop(max(lo, 1), hi, start_ans, 0)
     gotbuf[0] = served[0]
     if ids_ref is not None:
         ids_ref[...] = reqin[...]
     if during is not None:
         during()
     lax.fori_loop(1, n_path, finish_ans, 0)
-    got_ref[...] = gotbuf[...]
+    if got_ref is not None:
+        got_ref[...] = gotbuf[...]
 
 
 def fetch_rows(req, own_links, cap, n_grp, n_path):
@@ -263,10 +266,10 @@
         candidate = jnp.tanh(link_proj[:, 2 * width :] + reset * recur[:, 2 * width :])
         next_ref[...] = ((1.0 - update) * candidate + update * own).astype(next_ref.dtype)
 
-    _fetch_kernel(n_grp, n_path, req_ref, links_ref, gotv, None,
+    _fetch_kernel(n_grp, n_path, req_ref, links_ref, None, None,
                   reqin, want, served, gotbuf, rsend, rrecv, asend, arecv, greet=False, during=link_recur)
     hops = drow_ref.shape[1] // state_ref.shape[0]
-    _hop_kernel(hops, route_t_buf, gotv, w_in_ref, w_hid_ref, state_ref, live_ref, route_buf, cot_ref,
+    _hop_kernel(hops, route_t_buf, gotbuf, w_in_ref, w_hid_ref, state_ref, live_ref, route_buf, cot_ref,
                 final_ref, outbuf, termbuf, proj, msgs)
     _message_kernel(n_grp, n_path, outbuf, termbuf, None, grad_ref,
                     inbuf, recv1, recv2, mid, msend, mrecv, send1, got1, send2, got2, greet=False,

time: 69.5 us -> 69 us (level)
  no operation moved by 1% of the time
where the time goes in v14:
time: 69 us; the launch traced here: 68.8 us
  Pallas kernels  62.2 us (90%)
  local copies, waits for them, and re-layouts  4.77 us (7%)
  between operations  0.72 us (1%)
    pallas_call x1, Pallas kernels, run_all(): pl.pallas_call(lambda *refs: _all_kernel(n_grp, n_path, *refs), out_shape...  62.2 us
    unnamed x12, local copies, waits for them, and re-layouts  3.73 us

profile of v14, /device:TPU:6, one launch (start us, length us, event | category | flops | bytes accessed | tf_op | source)
XLA Modules:
  0.0 68.8 jit_solution(3623806357626618590)
XLA Ops:
  0.6 0.8 %copy.30.refs_5_ = s32[128,8]{1,0:T(8,128)S(1)} copy(s32[128,8]{0,1:T(8,128)} %param.10) | data formatting | bytes 8192 | tf_op args[2]
  1.4 0.0 copy-start
  1.4 0.1 reshape.69
  1.5 0.5 fusion.2
  2.1 0.1 convert_element_type.17
  2.2 0.0 copy-done
  2.2 0.1 fusion.15
  2.3 0.0 copy-start.2
  2.3 0.1 copy.37
  2.4 0.5 select_reduce_fusion
  2.9 0.1 sub.26
  3.0 0.7 dynamic_update_slice.3.refs_0_
  3.7 0.0 copy-done.2
  3.7 62.2 %shard_map.103 = (bf16[128,256]{1,0:T(8,128)(2,1)}, bf16[512,256]{1,0:T(8,128)(2,1)}, f32[4,256]{1,0:T(4,128)}) custom-call(s32[32,8,128]{2,1,0:T(8,128)} %dynamic_update_slice.3.refs_0_, bf16[512,256]{1,0:T(8,128)(2,1)} %bitcast.13, bf16[256,768]{1,0:T(8,128)(2,1)} %refs_2_.1, bf16[256,768]{1,0:T(8,128)(2,1)} %refs_3_.1, bf16[128,256]{1,0:T(8,128)(2,1)} %bitcast.14, ...), custom_call_target="tpu_custom_call" | custom-call | tf_op jit(solution)/shard_map/pallas_call | solution.py:288
  65.9 0.0 copy-start.1
  65.9 0.0 copy-start.3
  65.9 1.7 %copy.43 = bf16[1,512,256]{2,1,0:T(8,128)(2,1)} copy(bf16[1,512,256]{2,1,0:T(8,128)(2,1)} %bitcast.12) | data formatting | bytes 524288
  67.6 0.0 copy-done.1
  67.6 0.6 copy.44
  68.2 0.0 copy-done.3
  68.2 0.6 copy.45
  (4 shorter events, 0.1 us)
Async XLA Ops:
  1.4 0.8 %copy-start = (s32[128,8]{1,0:T(8,128)}, s32[128,8]{1,0:T(8,128)S(1)}, u32[]{:S(2)}) copy-start(s32[128,8]{1,0:T(8,128)S(1)} %copy.30.refs_5_) | copy-start | bytes 12292
  2.3 1.4 %copy-start.2 = (s32[8,128]{1,0:T(8,128)}, s32[8,128]{1,0:T(8,128)S(1)}, u32[]{:S(2)}) copy-start(s32[8,128]{1,0:T(8,128)S(1)} %copy.36) | copy-start | bytes 12292
  65.9 1.7 %copy-start.1 = (bf16[128,256]{1,0:T(8,128)(2,1)S(1)}, bf16[128,256]{1,0:T(8,128)(2,1)}, u32[]{:S(2)}) copy-start(bf16[128,256]{1,0:T(8,128)(2,1)} %get-tuple-element.7) | copy-start | bytes 196612
  65.9 2.3 %copy-start.3 = (f32[4,256]{1,0:T(4,128)S(1)}, f32[4,256]{1,0:T(4,128)}, u32[]{:S(2)}) copy-start(f32[4,256]{1,0:T(4,128)} %get-tuple-element.16) | copy-start | bytes 12292

commit v15 on v14

--- a/solution.py
+++ b/solution.py
@@ -66,8 +66,8 @@
     link_dev = links_ref.shape[0]
     lanes = lax.broadcasted_iota(jnp.int32, (1, link_dev), 1)
     start_ans, finish_ans = _ring_copies(served, gotbuf, asend, arecv, g, p, n_path, -1)
-    half = n_k // 2
-    for lo, hi in ((0, half), (half, n_k)):
+    part = n_k // 4
+    for lo, hi in ((0, part), (part, 2 * part), (2 * part, 3 * part), (3 * part, n_k)):
         lax.fori_loop(max(lo, 1), hi, finish_req, 0)
         ids_t = jnp.transpose(reqin[lo:hi, 0, :])
         for k in range(lo, hi):

time: 69 us -> 67.9 us (0.984)
  Pallas kernels: 62.2 us -> 61.1 us
    pallas_call x1, Pallas kernels: 62.2 us -> 61.1 us  [run_all(): pl.pallas_call(lambda *refs: _all_kernel(n_grp, n_path, *refs), out_shape...]
where the time goes in v15:
time: 67.9 us; the launch traced here: 67.7 us
  Pallas kernels  61.1 us (90%)
  local copies, waits for them, and re-layouts  4.77 us (7%)
  between operations  0.72 us (1%)
    pallas_call x1, Pallas kernels, run_all(): pl.pallas_call(lambda *refs: _all_kernel(n_grp, n_path, *refs), out_shape...  61.1 us
    unnamed x12, local copies, waits for them, and re-layouts  3.73 us

profile of v15, /device:TPU:6, one launch (start us, length us, event | category | flops | bytes accessed | tf_op | source)
XLA Modules:
  0.0 67.7 jit_solution(7442612062805754757)
XLA Ops:
  0.6 0.8 %copy.30.refs_5_ = s32[128,8]{1,0:T(8,128)S(1)} copy(s32[128,8]{0,1:T(8,128)} %param.10) | data formatting | bytes 8192 | tf_op args[2]
  1.4 0.0 copy-start
  1.4 0.1 reshape.69
  1.5 0.5 fusion.2
  2.1 0.1 convert_element_type.17
  2.2 0.0 copy-done
  2.2 0.1 fusion.15
  2.3 0.0 copy-start.2
  2.3 0.1 copy.37
  2.4 0.5 select_reduce_fusion
  2.9 0.1 sub.26
  3.0 0.7 dynamic_update_slice.3.refs_0_
  3.7 0.0 copy-done.2
  3.7 61.1 %shard_map.103 = (bf16[128,256]{1,0:T(8,128)(2,1)}, bf16[512,256]{1,0:T(8,128)(2,1)}, f32[4,256]{1,0:T(4,128)}) custom-call(s32[32,8,128]{2,1,0:T(8,128)} %dynamic_update_slice.3.refs_0_, bf16[512,256]{1,0:T(8,128)(2,1)} %bitcast.13, bf16[256,768]{1,0:T(8,128)(2,1)} %refs_2_.1, bf16[256,768]{1,0:T(8,128)(2,1)} %refs_3_.1, bf16[128,256]{1,0:T(8,128)(2,1)} %bitcast.14, ...), custom_call_target="tpu_custom_call" | custom-call | tf_op jit(solution)/shard_map/pallas_call | solution.py:288
  64.8 0.0 copy-start.1
  64.8 0.0 copy-start.3
  64.8 1.7 %copy.43 = bf16[1,512,256]{2,1,0:T(8,128)(2,1)} copy(bf16[1,512,256]{2,1,0:T(8,128)(2,1)} %bitcast.12) | data formatting | bytes 524288
  66.5 0.0 copy-done.1
  66.5 0.6 copy.44
  67.1 0.0 copy-done.3
  67.1 0.6 copy.45
  (4 shorter events, 0.1 us)
Async XLA Ops:
  1.4 0.8 %copy-start = (s32[128,8]{1,0:T(8,128)}, s32[128,8]{1,0:T(8,128)S(1)}, u32[]{:S(2)}) copy-start(s32[128,8]{1,0:T(8,128)S(1)} %copy.30.refs_5_) | copy-start | bytes 12292
  2.3 1.4 %copy-start.2 = (s32[8,128]{1,0:T(8,128)}, s32[8,128]{1,0:T(8,128)S(1)}, u32[]{:S(2)}) copy-start(s32[8,128]{1,0:T(8,128)S(1)} %copy.36) | copy-start | bytes 12292
  64.8 1.7 %copy-start.1 = (bf16[128,256]{1,0:T(8,128)(2,1)S(1)}, bf16[128,256]{1,0:T(8,128)(2,1)}, u32[]{:S(2)}) copy-start(bf16[128,256]{1,0:T(8,128)(2,1)} %get-tuple-element.7) | copy-start | bytes 196612
  64.8 2.3 %copy-start.3 = (f32[4,256]{1,0:T(4,128)S(1)}, f32[4,256]{1,0:T(4,128)}, u32[]{:S(2)}) copy-start(f32[4,256]{1,0:T(4,128)} %get-tuple-element.16) | copy-start | bytes 12292

commit v16 on v15

--- a/solution.py
+++ b/solution.py
@@ -110,7 +110,7 @@
 
 def _message_kernel(n_grp, n_path, out_ref, term_ref, inc_ref, grad_ref,
                     inbuf, recv1, recv2, mid, msend, mrecv, send1, got1, send2, got2, greet=True,
-                    after_msgs=None):
+                    after_msgs=None, send_msgs=None):
     g = lax.axis_index("grp")
     p = lax.axis_index("path")
     if greet:
@@ -133,7 +133,10 @@
         return c
 
     lax.fori_loop(1, n_path, start1, 0)
-    lax.fori_loop(1, n_path, start_msg, 0)
+    if send_msgs is None:
+        lax.fori_loop(1, n_path, start_msg, 0)
+    else:
+        send_msgs(start_msg)
     inbuf[0] = out_ref[0]
     lax.fori_loop(1, n_path, finish1, 0)
     mid[...] = term_ref[p] + jnp.sum(recv1[...], axis=0)
@@ -211,7 +214,8 @@
         msgs[h * n : (h + 1) * n, :] = carried.astype(bf16)
     final = carried.astype(bf16)
     final_ref[...] = final
-    out_ref[...] = jnp.dot(route_ref[...], msgs[...], preferred_element_type=f32).astype(bf16).reshape(out_ref.shape)
+    if out_ref is not None:
+        out_ref[...] = jnp.dot(route_ref[...], msgs[...], preferred_element_type=f32).astype(bf16).reshape(out_ref.shape)
     cot_t = jnp.transpose(cot_t_ref[...].astype(f32)).astype(bf16)
     term = jnp.dot(cot_t, final, preferred_element_type=f32)
     share = term_ref.shape[1]
@@ -270,10 +274,18 @@
                   reqin, want, served, gotbuf, rsend, rrecv, asend, arecv, greet=False, during=link_recur)
     hops = drow_ref.shape[1] // state_ref.shape[0]
     _hop_kernel(hops, route_t_buf, gotbuf, w_in_ref, w_hid_ref, state_ref, live_ref, route_buf, cot_ref,
-                final_ref, outbuf, termbuf, proj, msgs)
+                final_ref, None, termbuf, proj, msgs)
+
+    def send_msgs(start_msg):
+        n_k, cap, width = outbuf.shape
+        half = n_k // 2
+        for lo, hi in ((0, half), (half, n_k)):
+            part = jnp.dot(route_buf[lo * cap : hi * cap, :], msgs[...], preferred_element_type=f32)
+            outbuf[lo:hi] = part.astype(jnp.bfloat16).reshape(hi - lo, cap, width)
+            lax.fori_loop(max(lo, 1), hi, start_msg, 0)
     _message_kernel(n_grp, n_path, outbuf, termbuf, None, grad_ref,
                     inbuf, recv1, recv2, mid, msend, mrecv, send1, got1, send2, got2, greet=False,
-                    after_msgs=link_update)
+                    after_msgs=link_update, send_msgs=send_msgs)
 
 
 def run_all(req, own_links, w_path_in, w_path_hid, state, live, drow1, cot, w_link_in, w_link_hid,

time: 67.9 us -> 68.4 us (level); the launches traced: 67.7 us -> 67.3 us
  no operation moved by 1% of the time
where the time goes in v16:
time: 68.4 us; the launch traced here: 67.3 us
  Pallas kernels  60.7 us (89%)
  local copies, waits for them, and re-layouts  4.77 us (7%)
  between operations  0.72 us (1%)
    pallas_call x1, Pallas kernels, run_all(): pl.pallas_call(lambda *refs: _all_kernel(n_grp, n_path, *refs), out_shape...  60.7 us
    unnamed x12, local copies, waits for them, and re-layouts  3.73 us

profile of v16, /device:TPU:6, one launch (start us, length us, event | category | flops | bytes accessed | tf_op | source)
XLA Modules:
  0.0 67.3 jit_solution(3286299744776425225)
XLA Ops:
  0.6 0.8 %copy.30.refs_5_ = s32[128,8]{1,0:T(8,128)S(1)} copy(s32[128,8]{0,1:T(8,128)} %param.10) | data formatting | bytes 8192 | tf_op args[2]
  1.4 0.0 copy-start
  1.4 0.1 reshape.69
  1.5 0.5 fusion.2
  2.1 0.1 convert_element_type.17
  2.2 0.0 copy-done
  2.2 0.1 fusion.15
  2.3 0.0 copy-start.2
  2.3 0.1 copy.37
  2.4 0.5 select_reduce_fusion
  2.9 0.1 sub.26
  3.0 0.7 dynamic_update_slice.3.refs_0_
  3.7 0.0 copy-done.2
  3.7 60.7 %shard_map.103 = (bf16[128,256]{1,0:T(8,128)(2,1)}, bf16[512,256]{1,0:T(8,128)(2,1)}, f32[4,256]{1,0:T(4,128)}) custom-call(s32[32,8,128]{2,1,0:T(8,128)} %dynamic_update_slice.3.refs_0_, bf16[512,256]{1,0:T(8,128)(2,1)} %bitcast.13, bf16[256,768]{1,0:T(8,128)(2,1)} %refs_2_.1, bf16[256,768]{1,0:T(8,128)(2,1)} %refs_3_.1, bf16[128,256]{1,0:T(8,128)(2,1)} %bitcast.14, ...), custom_call_target="tpu_custom_call" | custom-call | tf_op jit(solution)/shard_map/pallas_call | solution.py:300
  64.4 0.0 copy-start.1
  64.4 0.0 copy-start.3
  64.4 1.7 %copy.43 = bf16[1,512,256]{2,1,0:T(8,128)(2,1)} copy(bf16[1,512,256]{2,1,0:T(8,128)(2,1)} %bitcast.12) | data formatting | bytes 524288
  66.1 0.0 copy-done.1
  66.1 0.6 copy.44
  66.8 0.0 copy-done.3
  66.8 0.6 copy.45
  (4 shorter events, 0.1 us)
Async XLA Ops:
  1.4 0.8 %copy-start = (s32[128,8]{1,0:T(8,128)}, s32[128,8]{1,0:T(8,128)S(1)}, u32[]{:S(2)}) copy-start(s32[128,8]{1,0:T(8,128)S(1)} %copy.30.refs_5_) | copy-start | bytes 12292
  2.3 1.4 %copy-start.2 = (s32[8,128]{1,0:T(8,128)}, s32[8,128]{1,0:T(8,128)S(1)}, u32[]{:S(2)}) copy-start(s32[8,128]{1,0:T(8,128)S(1)} %copy.36) | copy-start | bytes 12292
  64.4 1.7 %copy-start.1 = (bf16[128,256]{1,0:T(8,128)(2,1)S(1)}, bf16[128,256]{1,0:T(8,128)(2,1)}, u32[]{:S(2)}) copy-start(bf16[128,256]{1,0:T(8,128)(2,1)} %get-tuple-element.7) | copy-start | bytes 196612
  64.4 2.3 %copy-start.3 = (f32[4,256]{1,0:T(4,128)S(1)}, f32[4,256]{1,0:T(4,128)}, u32[]{:S(2)}) copy-start(f32[4,256]{1,0:T(4,128)} %get-tuple-element.16) | copy-start | bytes 12292

commit v17 on v15

--- a/solution.py
+++ b/solution.py
@@ -330,7 +330,7 @@
     entries = path_count * hop_count
     capacity = entries // peer_count
     slots = peer_count * capacity
-    flat_ids = path_links.reshape(-1)
+    flat_ids = path_links.T.reshape(-1)
     is_live = flat_ids >= 0
     owner_id = jnp.where(is_live, flat_ids // link_dev, peer_count)
     local_id = jnp.where(is_live, flat_ids % link_dev, 0)
@@ -341,8 +341,6 @@
     slot_id = jnp.sum(before * marks.astype(f32), axis=1).astype(jnp.int32)
     offset = lax.rem(owner_id - me + peer_count, peer_count)
     dest = jnp.where(is_live, offset * capacity + slot_id, -1)
-    dest = dest.reshape(path_count, hop_count).T.reshape(-1)
-    local_id = local_id.reshape(path_count, hop_count).T.reshape(-1)
     slot_ids = jnp.arange(slots)
     route = dest[None, :] == slot_ids[:, None]
     requests = jnp.sum(jnp.where(route, local_id[None, :] + 1, 0), axis=1) - 1

time: 67.9 us -> 68.9 us (1.015)
  other arithmetic: 0.64 us -> 1.86 us
    unnamed x12 -> x10, local copies, waits for them, and re-layouts: 3.73 us -> 3.79 us
where the time goes in v17:
time: 68.9 us; the launch traced here: 68.6 us
  Pallas kernels  61 us (89%)
  local copies, waits for them, and re-layouts  4.54 us (7%)
  other arithmetic  1.86 us (3%)
  between operations  0.69 us (1%)
    pallas_call x1, Pallas kernels, run_all(): pl.pallas_call(lambda *refs: _all_kernel(n_grp, n_path, *refs), out_shape...  61 us
    unnamed x10, local copies, waits for them, and re-layouts  3.79 us

profile of v17, /device:TPU:6, one launch (start us, length us, event | category | flops | bytes accessed | tf_op | source)
XLA Modules:
  0.0 68.6 jit_solution(13336171253639309166)
XLA Ops:
  0.6 0.7 %fusion.5 = s32[1024]{0:T(1024)S(1)} fusion(s32[128,8]{0,1:T(8,128)} %param.10), kind=kLoop, calls=%fused_computation.24 | loop fusion | flops 17408 | bytes 8192 | tf_op jit(solution)/shard_map/jit(_where)/select_n | solution.py:335
  1.3 0.0 copy-start
  1.3 0.5 fusion.2
  1.9 0.1 copy-done
  2.0 0.6 compare_select_fusion.5.refs_6_
  2.7 0.5 select_reduce_fusion
  3.2 0.1 sub.36
  3.3 0.7 %copy.12.refs_5_ = s32[128,8]{1,0:T(8,128)} copy(s32[128,8]{0,1:T(8,128)S(1)} %copy-done) | data formatting | bytes 8192 | tf_op args[2]
  4.0 0.7 dynamic_update_slice.3.refs_0_
  4.7 61.0 %shard_map.103 = (bf16[128,256]{1,0:T(8,128)(2,1)}, bf16[512,256]{1,0:T(8,128)(2,1)}, f32[4,256]{1,0:T(4,128)}) custom-call(s32[32,8,128]{2,1,0:T(8,128)} %dynamic_update_slice.3.refs_0_, bf16[512,256]{1,0:T(8,128)(2,1)} %bitcast.46, bf16[256,768]{1,0:T(8,128)(2,1)} %refs_2_.1, bf16[256,768]{1,0:T(8,128)(2,1)} %refs_3_.1, bf16[128,256]{1,0:T(8,128)(2,1)} %bitcast.47, ...), custom_call_target="tpu_custom_call" | custom-call | tf_op jit(solution)/shard_map/pallas_call | solution.py:288
  65.7 0.0 copy-start.1
  65.7 0.0 copy-start.2
  65.7 1.7 %copy.16 = bf16[1,512,256]{2,1,0:T(8,128)(2,1)} copy(bf16[1,512,256]{2,1,0:T(8,128)(2,1)} %bitcast.45) | data formatting | bytes 524288
  67.4 0.0 copy-done.1
  67.4 0.6 copy.17
  68.0 0.0 copy-done.2
  68.0 0.6 copy.18
  (3 shorter events, 0.0 us)
Async XLA Ops:
  1.3 0.7 %copy-start = (s32[128,8]{0,1:T(8,128)S(1)}, s32[128,8]{0,1:T(8,128)}, u32[]{:S(2)}) copy-start(s32[128,8]{0,1:T(8,128)} %param.10) | copy-start | bytes 12292
  65.7 1.7 %copy-start.1 = (bf16[128,256]{1,0:T(8,128)(2,1)S(1)}, bf16[128,256]{1,0:T(8,128)(2,1)}, u32[]{:S(2)}) copy-start(bf16[128,256]{1,0:T(8,128)(2,1)} %get-tuple-element.7) | copy-start | bytes 196612
  65.7 2.3 %copy-start.2 = (f32[4,256]{1,0:T(4,128)S(1)}, f32[4,256]{1,0:T(4,128)}, u32[]{:S(2)}) copy-start(f32[4,256]{1,0:T(4,128)} %get-tuple-element.16) | copy-start | bytes 12292
